TPU v7x, 32 devices: a whole 2x2x4 slice. The times are simulated.
32 devices in a mesh: event: 4 (over x, core), row: 2 (over y), col: 4 (over z).
Axes of the slice: x: 2, y: 2, z: 4, core: 2. Of those that a mesh axis runs over, the one named last changes fastest.
Arguments:
- depth_states: float32 [8, 3, 128, 4096], P('event', None, 'row', 'col'), may hold values from 0.8 to 1.2
- wet_mask: int32 [8, 128, 4096], P('event', 'row', 'col'), may hold values 0 or 1
- bed: float32 [128, 4096], P('row', 'col'), may hold values from -0.5 to 0.5
- log_manning: float32 [128, 4096], P('row', 'col'), may hold values from -0.4 to 0.4
- direction: float32 [128, 4096], P('row', 'col'), may hold values from -12 to 12
- gauge_cells: int32 [8, 2, 4, 1024], P('event', 'row', 'col'), may hold values from 0 to 65535
Outputs:
- hess_product: float32 [128, 4096], P('row', 'col')
- curvature: float32 [], replicated
All inputs are finite; a program needn't handle non-finite values. No bound on the sum of `wet_mask` on one device may be relied on, other than what follows from the above.
Results may differ from a plain program's by a relative error of at most 0.0003.
Values sent between devices are 32-bit elements; how exact they have to be, the bound alone decides.
No kernel may reach another device: no remote copies, remote signals or barrier semaphores. Data moves between devices by JAX's collectives and lax.ppermute only.
A program may use at most 128 MiB of HBM per device.

v0:
```python
import functools

import jax
import jax.numpy as jnp
from jax import lax
from jax.experimental import pallas as pl
from jax.experimental.pallas import tpu as pltpu
from jax.sharding import PartitionSpec as P

time_step = 0.035
slope_floor = 0.01
gauge_weight = 100.0
REACH = 6
LANES = 128
SUB = 8


def pairs(count, first):
    out = []
    for i in range(first, count - 1, 2):
        out += [(i, i + 1), (i + 1, i)]
    return out


def exchange(x, axis, first):
    perm = pairs(lax.axis_size(axis), first)
    return lax.ppermute(x, axis, perm) if perm else None


def lanes_of(shape):
    return lax.broadcasted_iota(jnp.int32, shape, 1)


def gauge_kernel(par, g_ref, da, wa, ba, ra, va, db, wb, bb, rb, vb, cnt, pay_a, pay_b):
    events, rows, cols = cnt.shape
    gauges = g_ref.shape[-1]
    tall = rows * cols // 256
    which = lax.broadcasted_iota(jnp.int32, (tall, gauges), 0)
    low = lax.broadcasted_iota(jnp.int32, (256, gauges), 0)
    one = lambda hit: jnp.where(hit, 1.0, 0.0).astype(jnp.bfloat16)
    steps = da.shape[1]
    edge_a = pl.multiple_of((par[0] * (rows // SUB - 1)) * SUB, SUB)
    edge_b = pl.multiple_of((rows - SUB) - edge_a, SUB)
    for e in range(events):
        g = g_ref[e]
        row, col = g // cols, g % cols
        high = (col // 256) * rows + row
        tally = lax.dot_general(
            one(which == high),
            one(low == col % 256),
            (((1,), (1,)), ((), ())),
            preferred_element_type=jnp.float32,
        )
        for b in range(cols // 256):
            cnt[e, :, b * 256 : (b + 1) * 256] = tally[b * rows : (b + 1) * rows]
    for pay, d, w, b, r, v, edge in (
        (pay_a, da, wa, ba, ra, va, edge_a),
        (pay_b, db, wb, bb, rb, vb, edge_b),
    ):
        for e in range(events):
            for t in range(steps):
                pay[e * steps + t] = d[e, t]
            pay[events * steps + e] = w[e].astype(jnp.float32)
            pay[events * (steps + 1) + 3 + e] = cnt[e, pl.ds(edge, SUB), :]
        base = events * (steps + 1)
        pay[base], pay[base + 1], pay[base + 2] = b[...], r[...], v[...]


def gauges_and_rows(par, cells, depth, wet, bed, rough, direction):
    events, steps, rows, cols = depth.shape
    top = rows // SUB - 1
    fields = events * (steps + 2) + 3

    def edges(flip):
        at = lambda p: (1 - p[0] if flip else p[0]) * top
        return [
            pl.BlockSpec((events, steps, SUB, cols), lambda i, p: (0, 0, at(p), 0)),
            pl.BlockSpec((events, SUB, cols), lambda i, p: (0, at(p), 0)),
        ] + [pl.BlockSpec((SUB, cols), lambda i, p: (at(p), 0))] * 3

    whole = lambda shape: pl.BlockSpec(shape, lambda i, p: (0,) * len(shape))
    return pl.pallas_call(
        gauge_kernel,
        grid_spec=pltpu.PrefetchScalarGridSpec(
            num_scalar_prefetch=1,
            grid=(1,),
            in_specs=[whole(cells.shape)] + edges(False) + edges(True),
            out_specs=[whole((events, rows, cols))] + [whole((fields, SUB, cols))] * 2,
        ),
        out_shape=[jax.ShapeDtypeStruct((events, rows, cols), jnp.float32)]
        + [jax.ShapeDtypeStruct((fields, SUB, cols), jnp.float32)] * 2,
        name="gauges_and_rows",
    )(par, cells, *(depth, wet, bed, rough, direction) * 2)


def column_kernel(par, *refs):
    sides = (refs[0:6], refs[6:12])
    rims = refs[12:16]
    pay_a, pay_b = refs[16:18]
    events, steps, rows, _ = sides[0][0].shape
    even_row = par[0] == 1
    even_col = par[1] == 1
    packs = []
    for side in range(2):
        d, w, b, r, v, c = sides[side]
        rim_a, rim_b = rims[2 * side], rims[2 * side + 1]
        lane = lanes_of((rows + 2 * SUB, LANES))
        pack = jnp.zeros((rows + 2 * SUB, LANES), jnp.float32)
        own = [d[e, t] for e in range(events) for t in range(steps)]
        own += [w[e].astype(jnp.float32) for e in range(events)]
        own += [b[...], r[...], v[...]]
        own += [c[e] for e in range(events)]
        for f, x in enumerate(own):
            top = jnp.where(even_row, rim_b[f], rim_a[f])
            bottom = jnp.where(even_row, rim_a[f], rim_b[f])
            x = jnp.concatenate([top, x, bottom], axis=0)
            place = f * REACH
            shift = (place + REACH if side == 1 else place) % LANES
            if shift:
                x = pltpu.roll(x, shift, 1)
            pack = jnp.where((lane >= place) & (lane < place + REACH), x, pack)
        packs.append(pack)
    pay_a[...] = jnp.where(even_col, packs[1], packs[0])
    pay_b[...] = jnp.where(even_col, packs[0], packs[1])


def edge_columns(par, depth, wet, bed, rough, direction, counts, rim_a, rim_b):
    events, steps, rows, cols = depth.shape
    fields = rim_a.shape[0]
    last = cols // LANES - 1

    def side(j):
        return [
            pl.BlockSpec((events, steps, rows, LANES), lambda i, p: (0, 0, 0, j)),
            pl.BlockSpec((events, rows, LANES), lambda i, p: (0, 0, j)),
            pl.BlockSpec((rows, LANES), lambda i, p: (0, j)),
            pl.BlockSpec((rows, LANES), lambda i, p: (0, j)),
            pl.BlockSpec((rows, LANES), lambda i, p: (0, j)),
            pl.BlockSpec((events, rows, LANES), lambda i, p: (0, 0, j)),
        ]

    rim = lambda j: [pl.BlockSpec((fields, SUB, LANES), lambda i, p: (0, 0, j))] * 2
    tall = (rows + 2 * SUB, LANES)
    own = (depth, wet, bed, rough, direction, counts)
    return pl.pallas_call(
        column_kernel,
        grid_spec=pltpu.PrefetchScalarGridSpec(
            num_scalar_prefetch=1,
            grid=(1,),
            in_specs=side(0) + side(last) + rim(0) + rim(last),
            out_specs=[pl.BlockSpec(tall, lambda i, p: (0, 0))] * 2,
        ),
        out_shape=[jax.ShapeDtypeStruct(tall, jnp.float32)] * 2,
        name="edge_columns",
    )(par, *own, *own, rim_a, rim_b, rim_a, rim_b)


def model_kernel(
    par, depth, wet, bed, rough, direction, counts, rim_a, rim_b, side_a, side_b,
    grad_ref, curve_ref,
    hx, wx, bx, mx, qx, cx, inv_x, inv_y, sum_x, sum_y,
    a_x, b_x, c_x, a_y, b_y, c_y, state, work, flow, g_x, g_y,
):
    events, steps, rows, cols = depth.shape
    tall = rows + 2 * SUB
    tiles = cols // LANES
    count = tiles + 1
    even_row = par[0] == 1
    even_col = par[1] == 1
    lane = lanes_of((tall, LANES))
    right_rim = jnp.where(even_col, side_a[...], side_b[...])
    left_rim = jnp.where(even_col, side_b[...], side_a[...])

    def assemble(f, own, put):
        top = jnp.where(even_row, rim_b[f], rim_a[f])
        bottom = jnp.where(even_row, rim_a[f], rim_b[f])
        put(slice(0, SUB), slice(0, cols), top)
        put(slice(SUB, SUB + rows), slice(0, cols), own)
        put(slice(SUB + rows, tall), slice(0, cols), bottom)
        place = f * REACH
        r = pltpu.roll(right_rim, (LANES - place) % LANES, 1) if place else right_rim
        l = pltpu.roll(left_rim, (LANES - REACH - place) % LANES, 1)
        extra = jnp.where(lane < REACH, r, jnp.where(lane >= LANES - REACH, l, 0.0))
        put(slice(0, tall), slice(cols, cols + LANES), extra)

    def into(ref, *lead):
        def put(rs, cs, x):
            ref[(*lead, rs, cs)] = x

        return put

    for e in range(events):
        for t in range(steps):
            assemble(e * steps + t, depth[e, t], into(hx, e, t))
        assemble(events * steps + e, wet[e].astype(jnp.float32), into(wx, e))
        assemble(events * (steps + 1) + 3 + e, counts[e], into(cx, e))
    base = events * (steps + 1)
    assemble(base, bed[...], into(bx))
    assemble(base + 1, rough[...], into(mx))
    assemble(base + 2, direction[...], into(qx))

    def at(j):
        return pl.ds(pl.multiple_of(j * LANES, LANES), LANES)

    def after(j):
        return jnp.where(j == count - 1, 0, j + 1)

    def before(j):
        return jnp.where(j == 0, count - 1, j - 1)

    below = lambda x: pltpu.roll(x, tall - 1, 0)
    above = lambda x: pltpu.roll(x, 1, 0)

    def right(x, nxt):
        return jnp.where(lane == LANES - 1, pltpu.roll(nxt, LANES - 1, 1), pltpu.roll(x, LANES - 1, 1))

    def left(x, prv):
        return jnp.where(lane == 0, pltpu.roll(prv, 1, 1), pltpu.roll(x, 1, 1))

    @pl.loop(0, count)
    def _(j):
        m = jnp.exp(mx[:, at(j)])
        mx[:, at(j)] = m
        qx[:, at(j)] = m * qx[:, at(j)]

    scale = time_step * 2.0 ** (-2.0 / 3.0)

    @pl.loop(0, count)
    def _(j):
        n = after(j)
        m, q = mx[:, at(j)], qx[:, at(j)]
        inv_x[:, at(j)] = 1.0 / (m + right(m, mx[:, at(n)]))
        inv_y[:, at(j)] = 1.0 / (m + below(m))
        sum_x[:, at(j)] = q + right(q, qx[:, at(n)])
        sum_y[:, at(j)] = q + below(q)
        g_x[:, at(j)] = jnp.zeros((tall, LANES), jnp.float32)
        g_y[:, at(j)] = jnp.zeros((tall, LANES), jnp.float32)

    def face(h, h_k, s, cond, inv):
        hs = h + h_k
        x = s * s + slope_floor
        lx = jnp.log(x)
        p = cond * jnp.exp((2.0 / 3.0) * jnp.log(hs) - 0.25 * lx)
        t = p * hs
        return (
            (5.0 / 3.0) * (p * s),
            t * (0.5 + (0.5 * slope_floor) * jnp.exp(-lx)),
            -(t * s) * inv,
        )

    curve_ref[...] = jnp.zeros(curve_ref.shape, jnp.float32)

    @pl.loop(0, events)
    def _(e):
        for t in range(steps):

            @pl.loop(0, count)
            def _(j):
                n = after(j)
                h, b = hx[e, t, :, at(j)], bx[:, at(j)]
                w = wx[e, :, at(j)]
                h_n = hx[e, t, :, at(n)]
                surface = h + b
                inv = inv_x[:, at(j)]
                A, B, C = face(
                    h,
                    right(h, h_n),
                    right(surface, h_n + bx[:, at(n)]) - surface,
                    (scale * inv) * (w * right(w, wx[e, :, at(n)])),
                    inv,
                )
                inv = inv_y[:, at(j)]
                A2, B2, C2 = face(
                    h,
                    below(h),
                    below(surface) - surface,
                    (scale * inv) * (w * below(w)),
                    inv,
                )
                c_x[t, :, at(j)] = C
                c_y[t, :, at(j)] = C2
                fx = C * sum_x[:, at(j)]
                fy = C2 * sum_y[:, at(j)]
                if t:
                    a_x[t - 1, :, at(j)] = A
                    b_x[t - 1, :, at(j)] = B
                    a_y[t - 1, :, at(j)] = A2
                    b_y[t - 1, :, at(j)] = B2
                    d = state[:, at(j)]
                    k = right(d, state[:, at(n)])
                    fx += A * (d + k) + B * (k - d)
                    k = below(d)
                    fy += A2 * (d + k) + B2 * (k - d)
                    work[:, at(j)] = d + fx + (fy - above(fy))
                else:
                    work[:, at(j)] = fx + (fy - above(fy))
                flow[:, at(j)] = fx

            @pl.loop(0, count)
            def _(j):
                r = work[:, at(j)] - left(flow[:, at(j)], flow[:, at(before(j))])
                if t == steps - 1:
                    c = cx[e, :, at(j)] * gauge_weight
                    s = c * r

                    @pl.when(j < tiles)
                    def _():
                        own = (s * r)[SUB : SUB + rows]
                        total = own[0:SUB]
                        for i in range(1, rows // SUB):
                            total += own[i * SUB : (i + 1) * SUB]
                        curve_ref[...] += total

                    r = s
                state[:, at(j)] = r

        for t in range(steps - 1, -1, -1):

            @pl.loop(0, count)
            def _(j):
                n = after(j)
                l = state[:, at(j)]
                px = l - right(l, state[:, at(n)])
                py = l - below(l)
                g_x[:, at(j)] += c_x[t, :, at(j)] * px
                g_y[:, at(j)] += c_y[t, :, at(j)] * py
                if t:
                    u, v = a_x[t - 1, :, at(j)] * px, b_x[t - 1, :, at(j)] * px
                    u2, v2 = a_y[t - 1, :, at(j)] * py, b_y[t - 1, :, at(j)] * py
                    work[:, at(j)] = l + (u - v) + (u2 - v2) + above(u2 + v2)
                    flow[:, at(j)] = u + v

            if t:

                @pl.loop(0, count)
                def _(j):
                    state[:, at(j)] = work[:, at(j)] + left(
                        flow[:, at(j)], flow[:, at(before(j))]
                    )

    @pl.loop(0, tiles)
    def _(j):
        x, y = g_x[:, at(j)], g_y[:, at(j)]
        g = mx[:, at(j)] * ((x + left(x, g_x[:, at(before(j))])) + (y + above(y)))
        grad_ref[:, at(j)] = g[SUB : SUB + rows]


def model(par, depth, wet, bed, rough, direction, counts, rim_a, rim_b, side_a, side_b):
    events, steps, rows, cols = depth.shape
    tall, wide = rows + 2 * SUB, cols + LANES
    f32 = functools.partial(pltpu.VMEM, dtype=jnp.float32)
    vm = lambda *lead: pltpu.VMEM((*lead, tall, wide), jnp.float32)
    vmem = pl.BlockSpec(memory_space=pltpu.VMEM)
    return pl.pallas_call(
        model_kernel,
        in_specs=[pl.BlockSpec(memory_space=pltpu.SMEM)] + [vmem] * 10,
        out_specs=[vmem] * 2,
        out_shape=[
            jax.ShapeDtypeStruct((rows, cols), jnp.float32),
            jax.ShapeDtypeStruct((SUB, LANES), jnp.float32),
        ],
        scratch_shapes=[vm(events, steps), vm(events), vm(), vm(), vm(), vm(events)]
        + [vm()] * 4
        + [vm(steps - 1), vm(steps - 1), vm(steps)] * 2
        + [vm()] * 5,
        compiler_params=pltpu.CompilerParams(vmem_limit_bytes=56 * 1024 * 1024),
        name="model",
    )(par, depth, wet, bed, rough, direction, counts, rim_a, rim_b, side_a, side_b)


def total_over(x, axis):
    count = lax.axis_size(axis)
    hop = 1
    while hop < count:
        x = x + lax.ppermute(x, axis, [(i, i ^ hop) for i in range(count)])
        hop *= 2
    return x


def local(depth, wet, bed, rough, direction, gauge_cells):
    events, steps, rows, cols = depth.shape
    cells = gauge_cells.reshape(events, 1, -1)
    par = jnp.stack([1 - lax.axis_index("row") % 2, 1 - lax.axis_index("col") % 2]).astype(jnp.int32)
    counts, pay_a, pay_b = gauges_and_rows(par, cells, depth, wet, bed, rough, direction)
    rim_a = exchange(pay_a, "row", 0)
    rim_b = exchange(pay_b, "row", 1)
    if rim_b is None:
        rim_b = jnp.zeros_like(rim_a)
    send_a, send_b = edge_columns(par, depth, wet, bed, rough, direction, counts, rim_a, rim_b)
    side_a = exchange(send_a, "col", 0)
    side_b = exchange(send_b, "col", 1)
    grad, curve = model(par, depth, wet, bed, rough, direction, counts, rim_a, rim_b, side_a, side_b)
    hess_product = total_over(grad, "event")
    c = total_over(total_over(total_over(curve, "event"), "row"), "col")
    return (hess_product, jnp.sum(c))


def solution(mesh):
    placed = (
        P("event", None, "row", "col"),
        P("event", "row", "col"),
        P("row", "col"),
        P("row", "col"),
        P("row", "col"),
        P("event", "row", "col", None),
    )
    return jax.shard_map(
        local, mesh=mesh, in_specs=placed, out_specs=(P("row", "col"), P()), check_vma=False
    )
```

profile of v0, /device:TPU:0, one launch (start us, length us, event | category | flops | bytes accessed | tf_op | source)
XLA Modules:
  0.0 81.9 jit_solution(6584013807877079269)
XLA Ops:
  0.6 0.7 pad_add_fusion.par
  1.3 3.4 %gauges_and_rows.1 = (f32[2,64,1024]{2,1,0:T(8,128)}, f32[13,8,1024]{2,1,0:T(8,128)}, f32[13,8,1024]{2,1,0:T(8,128)}) custom-call(s32[2]{0:T(128)} %pad_add_fusion.par, s32[2,1,1024]{2,1,0:T(1,128)} %bitcast.3, f32[2,3,64,1024]{3,2,1,0:T(8,128)} %depth.1, s32[2,64,1024]{2,1,0:T(8,128)} %wet.1, f32[64,1024]{1,0:T(8,128)} %bed.1, f32[64,1024]{1,0:T(8,128)} %rough.1, ...), custom_call_target="tpu_custom_call" | custom-call | tf_op jit(solution)/shard_map/gauges_and_rows/pallas_call | solution.py:82
  4.7 3.0 %collective-permute-start = (f32[13,8,1024]{2,1,0:T(8,128)}, f32[13,8,1024]{2,1,0:T(8,128)S(1)}, u32[]{:S(2)}, u32[]{:S(2)}) collective-permute-start(f32[13,8,1024]{2,1,0:T(8,128)} %get-tuple-element.9), channel_id=1, source_target_pairs={{0,4},{4,0},{1,5},{5,1},{2,6},{6,2},{3,7},{7,3},{8,12},{12,8},{9,1... | collective-permute-start | bytes 1277960 | tf_op jit(solution)/shard_map/ppermute | solution.py:27
  7.7 10.0 %collective-permute-done.refs_12_.refs_14_.rim_a = f32[13,8,1024]{2,1,0:T(8,128)S(1)} collective-permute-done((f32[13,8,1024]{2,1,0:T(8,128)}, f32[13,8,1024]{2,1,0:T(8,128)S(1)}, u32[]{:S(2)}, u32[]{:S(2)}) %collective-permute-start) | collective-permute-done | bytes 426016 | tf_op jit(solution)/shard_map/ppermute | solution.py:27
  17.7 0.0 copy-start
  17.7 0.9 %broadcast_in_dim.3.refs_13_.refs_15_.rim_b = f32[13,8,1024]{2,1,0:T(8,128)} broadcast(f32[]{:T(128)} %constant.29.clone.1), dimensions={} | broadcast | bytes 425988 | tf_op jit(solution)/shard_map/broadcast_in_dim | solution.py:388
  18.6 0.0 copy-done
  18.6 2.9 %edge_columns.1 = (f32[80,128]{1,0:T(8,128)}, f32[80,128]{1,0:T(8,128)}) custom-call(s32[2]{0:T(128)} %pad_add_fusion.par, f32[2,3,64,1024]{3,2,1,0:T(8,128)} %depth.1, s32[2,64,1024]{2,1,0:T(8,128)} %wet.1, f32[64,1024]{1,0:T(8,128)} %bed.1, f32[64,1024]{1,0:T(8,128)} %rough.1, f32[64,1024]{1,0:T(8,128)} %direction.1, ...), custom_call_target="tpu_custom_call" | custom-call | tf_op jit(solution)/shard_map/edge_columns/pallas_call | solution.py:145
  21.5 1.8 %collective-permute-start.1 = (f32[80,128]{1,0:T(8,128)}, f32[80,128]{1,0:T(8,128)S(1)}, u32[]{:S(2)}, u32[]{:S(2)}) collective-permute-start(f32[80,128]{1,0:T(8,128)} %get-tuple-element.10), channel_id=1, source_target_pairs={{0,1},{1,0},{2,3},{3,2},{4,5},{5,4},{6,7},{7,6},{8,9},{9,8},{10,11... | collective-permute-start | bytes 122888 | tf_op jit(solution)/shard_map/ppermute | solution.py:27
  23.3 0.7 collective-permute-start.2
  24.0 1.8 %collective-permute-done.1.side_a = f32[80,128]{1,0:T(8,128)S(1)} collective-permute-done((f32[80,128]{1,0:T(8,128)}, f32[80,128]{1,0:T(8,128)S(1)}, u32[]{:S(2)}, u32[]{:S(2)}) %collective-permute-start.1) | collective-permute-done | bytes 40992 | tf_op jit(solution)/shard_map/ppermute | solution.py:27
  25.8 0.0 copy-start.1
  25.8 0.0 collective-permute-done.2.side_b
  25.8 0.6 copy-done.1
  26.4 0.0 copy-start.2
  26.4 0.6 copy-done.2
  27.0 27.8 %model.1 = (f32[64,1024]{1,0:T(8,128)}, f32[8,128]{1,0:T(8,128)}) custom-call(s32[2]{0:T(128)} %pad_add_fusion.par, f32[2,3,64,1024]{3,2,1,0:T(8,128)} %depth.1, s32[2,64,1024]{2,1,0:T(8,128)} %wet.1, f32[64,1024]{1,0:T(8,128)} %bed.1, f32[64,1024]{1,0:T(8,128)} %rough.1, f32[64,1024]{1,0:T(8,128)} %direction.1, ...), custom_call_target="tpu_custom_call" | custom-call | tf_op jit(solution)/shard_map/model/pallas_call | solution.py:354
  54.8 0.0 collective-permute-start.3
  54.8 1.7 %collective-permute-done.3 = f32[64,1024]{1,0:T(8,128)S(1)} collective-permute-done((f32[64,1024]{1,0:T(8,128)}, f32[64,1024]{1,0:T(8,128)S(1)}, u32[]{:S(2)}, u32[]{:S(2)}) %collective-permute-start.3) | collective-permute-done | bytes 262176 | tf_op jit(solution)/shard_map/ppermute | solution.py:375
  56.6 1.0 %add.30 = f32[64,1024]{1,0:T(8,128)S(1)} add(f32[64,1024]{1,0:T(8,128)} %get-tuple-element.12, f32[64,1024]{1,0:T(8,128)S(1)} %collective-permute-done.3) | non-fusion elementwise | flops 65536 | bytes 786432 | tf_op jit(solution)/shard_map/add | solution.py:375
  57.5 1.8 %collective-permute-start.4 = (f32[64,1024]{1,0:T(8,128)S(1)}, f32[64,1024]{1,0:T(8,128)S(1)}, u32[]{:S(2)}, u32[]{:S(2)}) collective-permute-start(f32[64,1024]{1,0:T(8,128)S(1)} %add.30), channel_id=1, source_target_pairs={{0,16},{8,24},{16,0},{24,8},{1,17},{9,25},{17,1},{25,9},{2,18},{10... | collective-permute-start | bytes 786440 | tf_op jit(solution)/shard_map/ppermute | solution.py:375
  59.3 0.0 collective-permute-start.5
  59.3 1.4 %collective-permute-done.5 = f32[8,128]{1,0:T(8,128)S(1)} collective-permute-done((f32[8,128]{1,0:T(8,128)}, f32[8,128]{1,0:T(8,128)S(1)}, u32[]{:S(2)}, u32[]{:S(2)}) %collective-permute-start.5) | collective-permute-done | bytes 4128 | tf_op jit(solution)/shard_map/ppermute | solution.py:375
  60.7 0.7 add.32
  61.4 0.3 collective-permute-start.6
  61.7 4.3 %collective-permute-done.6 = f32[8,128]{1,0:T(8,128)S(1)} collective-permute-done((f32[8,128]{1,0:T(8,128)S(1)}, f32[8,128]{1,0:T(8,128)S(1)}, u32[]{:S(2)}, u32[]{:S(2)}) %collective-permute-start.6) | collective-permute-done | bytes 4128 | tf_op jit(solution)/shard_map/ppermute | solution.py:375
  66.0 1.7 %collective-permute-start.7 = (f32[8,128]{1,0:T(8,128)S(1)}, f32[8,128]{1,0:T(8,128)S(1)}, u32[]{:S(2)}, u32[]{:S(2)}) collective-permute-start(f32[8,128]{1,0:T(8,128)S(1)} %add.33), channel_id=1, source_target_pairs={{0,4},{4,0},{1,5},{5,1},{2,6},{6,2},{3,7},{7,3},{8,12},{12,8},{9,1... | collective-permute-start | bytes 12296 | tf_op jit(solution)/shard_map/ppermute | solution.py:375
  67.8 1.9 %collective-permute-done.7 = f32[8,128]{1,0:T(8,128)S(1)} collective-permute-done((f32[8,128]{1,0:T(8,128)S(1)}, f32[8,128]{1,0:T(8,128)S(1)}, u32[]{:S(2)}, u32[]{:S(2)}) %collective-permute-start.7) | collective-permute-done | bytes 4128 | tf_op jit(solution)/shard_map/ppermute | solution.py:375
  69.7 4.2 %collective-permute-start.8 = (f32[8,128]{1,0:T(8,128)S(1)}, f32[8,128]{1,0:T(8,128)S(1)}, u32[]{:S(2)}, u32[]{:S(2)}) collective-permute-start(f32[8,128]{1,0:T(8,128)S(1)} %add.34), channel_id=1, source_target_pairs={{0,1},{1,0},{2,3},{3,2},{4,5},{5,4},{6,7},{7,6},{8,9},{9,8},{10,11... | collective-permute-start | bytes 12296 | tf_op jit(solution)/shard_map/ppermute | solution.py:375
  73.9 1.6 %collective-permute-done.8 = f32[8,128]{1,0:T(8,128)S(1)} collective-permute-done((f32[8,128]{1,0:T(8,128)S(1)}, f32[8,128]{1,0:T(8,128)S(1)}, u32[]{:S(2)}, u32[]{:S(2)}) %collective-permute-start.8) | collective-permute-done | bytes 4128 | tf_op jit(solution)/shard_map/ppermute | solution.py:375
  75.5 3.5 %collective-permute-start.9 = (f32[8,128]{1,0:T(8,128)S(1)}, f32[8,128]{1,0:T(8,128)S(1)}, u32[]{:S(2)}, u32[]{:S(2)}) collective-permute-start(f32[8,128]{1,0:T(8,128)S(1)} %add.35), channel_id=1, source_target_pairs={{0,2},{1,3},{2,0},{3,1},{4,6},{5,7},{6,4},{7,5},{8,10},{9,11},{10,... | collective-permute-start | bytes 12296 | tf_op jit(solution)/shard_map/ppermute | solution.py:375
  78.9 1.6 %collective-permute-done.9 = f32[8,128]{1,0:T(8,128)S(1)} collective-permute-done((f32[8,128]{1,0:T(8,128)S(1)}, f32[8,128]{1,0:T(8,128)S(1)}, u32[]{:S(2)}, u32[]{:S(2)}) %collective-permute-start.9) | collective-permute-done | bytes 4128 | tf_op jit(solution)/shard_map/ppermute | solution.py:375
  80.5 0.6 add_reduce_fusion
  81.1 0.0 collective-permute-done.4
  81.1 0.7 add.31
  (3 shorter events, 0.0 us)
Async XLA Ops:
  4.7 13.0 %collective-permute-start = (f32[13,8,1024]{2,1,0:T(8,128)}, f32[13,8,1024]{2,1,0:T(8,128)S(1)}, u32[]{:S(2)}, u32[]{:S(2)}) collective-permute-start(f32[13,8,1024]{2,1,0:T(8,128)} %get-tuple-element.9), channel_id=1, source_target_pairs={{0,4},{4,0},{1,5},{5,1},{2,6},{6,2},{3,7},{7,3},{8,12},{12,8},{9,1... | collective-permute-start | bytes 1277960 | tf_op jit(solution)/shard_map/ppermute | solution.py:27
  17.7 0.9 %copy-start = (f32[13,8,1024]{2,1,0:T(8,128)}, f32[13,8,1024]{2,1,0:T(8,128)S(1)}, u32[]{:S(2)}) copy-start(f32[13,8,1024]{2,1,0:T(8,128)S(1)} %collective-permute-done.refs_12_.refs_14_.rim_a) | copy-start | bytes 1277956
  21.5 4.2 %collective-permute-start.1 = (f32[80,128]{1,0:T(8,128)}, f32[80,128]{1,0:T(8,128)S(1)}, u32[]{:S(2)}, u32[]{:S(2)}) collective-permute-start(f32[80,128]{1,0:T(8,128)} %get-tuple-element.10), channel_id=1, source_target_pairs={{0,1},{1,0},{2,3},{3,2},{4,5},{5,4},{6,7},{7,6},{8,9},{9,8},{10,11... | collective-permute-start | bytes 122888 | tf_op jit(solution)/shard_map/ppermute | solution.py:27
  23.3 2.4 %collective-permute-start.2 = (f32[80,128]{1,0:T(8,128)}, f32[80,128]{1,0:T(8,128)S(1)}, u32[]{:S(2)}, u32[]{:S(2)}) collective-permute-start(f32[80,128]{1,0:T(8,128)} %get-tuple-element.11), channel_id=1, source_target_pairs={{1,2},{2,1},{5,6},{6,5},{9,10},{10,9},{13,14},{14,13},{17,18},{18,... | collective-permute-start | bytes 122888 | tf_op jit(solution)/shard_map/ppermute | solution.py:27
  25.8 0.6 copy-start.1
  26.4 0.6 copy-start.2
  54.8 1.7 %collective-permute-start.3 = (f32[64,1024]{1,0:T(8,128)}, f32[64,1024]{1,0:T(8,128)S(1)}, u32[]{:S(2)}, u32[]{:S(2)}) collective-permute-start(f32[64,1024]{1,0:T(8,128)} %get-tuple-element.12), channel_id=1, source_target_pairs={{0,8},{8,0},{16,24},{24,16},{1,9},{9,1},{17,25},{25,17},{2,10},{10... | collective-permute-start | bytes 786440 | tf_op jit(solution)/shard_map/ppermute | solution.py:375
  57.5 23.6 %collective-permute-start.4 = (f32[64,1024]{1,0:T(8,128)S(1)}, f32[64,1024]{1,0:T(8,128)S(1)}, u32[]{:S(2)}, u32[]{:S(2)}) collective-permute-start(f32[64,1024]{1,0:T(8,128)S(1)} %add.30), channel_id=1, source_target_pairs={{0,16},{8,24},{16,0},{24,8},{1,17},{9,25},{17,1},{25,9},{2,18},{10... | collective-permute-start | bytes 786440 | tf_op jit(solution)/shard_map/ppermute | solution.py:375
  59.3 1.4 %collective-permute-start.5 = (f32[8,128]{1,0:T(8,128)}, f32[8,128]{1,0:T(8,128)S(1)}, u32[]{:S(2)}, u32[]{:S(2)}) collective-permute-start(f32[8,128]{1,0:T(8,128)} %get-tuple-element.13), channel_id=1, source_target_pairs={{0,8},{8,0},{16,24},{24,16},{1,9},{9,1},{17,25},{25,17},{2,10},{10... | collective-permute-start | bytes 12296 | tf_op jit(solution)/shard_map/ppermute | solution.py:375
  61.4 4.7 %collective-permute-start.6 = (f32[8,128]{1,0:T(8,128)S(1)}, f32[8,128]{1,0:T(8,128)S(1)}, u32[]{:S(2)}, u32[]{:S(2)}) collective-permute-start(f32[8,128]{1,0:T(8,128)S(1)} %add.32), channel_id=1, source_target_pairs={{0,16},{8,24},{16,0},{24,8},{1,17},{9,25},{17,1},{25,9},{2,18},{10... | collective-permute-start | bytes 12296 | tf_op jit(solution)/shard_map/ppermute | solution.py:375
  66.0 3.6 %collective-permute-start.7 = (f32[8,128]{1,0:T(8,128)S(1)}, f32[8,128]{1,0:T(8,128)S(1)}, u32[]{:S(2)}, u32[]{:S(2)}) collective-permute-start(f32[8,128]{1,0:T(8,128)S(1)} %add.33), channel_id=1, source_target_pairs={{0,4},{4,0},{1,5},{5,1},{2,6},{6,2},{3,7},{7,3},{8,12},{12,8},{9,1... | collective-permute-start | bytes 12296 | tf_op jit(solution)/shard_map/ppermute | solution.py:375
  69.7 5.8 %collective-permute-start.8 = (f32[8,128]{1,0:T(8,128)S(1)}, f32[8,128]{1,0:T(8,128)S(1)}, u32[]{:S(2)}, u32[]{:S(2)}) collective-permute-start(f32[8,128]{1,0:T(8,128)S(1)} %add.34), channel_id=1, source_target_pairs={{0,1},{1,0},{2,3},{3,2},{4,5},{5,4},{6,7},{7,6},{8,9},{9,8},{10,11... | collective-permute-start | bytes 12296 | tf_op jit(solution)/shard_map/ppermute | solution.py:375
  75.5 5.1 %collective-permute-start.9 = (f32[8,128]{1,0:T(8,128)S(1)}, f32[8,128]{1,0:T(8,128)S(1)}, u32[]{:S(2)}, u32[]{:S(2)}) collective-permute-start(f32[8,128]{1,0:T(8,128)S(1)} %add.35), channel_id=1, source_target_pairs={{0,2},{1,3},{2,0},{3,1},{4,6},{5,7},{6,4},{7,5},{8,10},{9,11},{10,... | collective-permute-start | bytes 12296 | tf_op jit(solution)/shard_map/ppermute | solution.py:375
where the time goes:
time: 82.1 us; the launch traced here: 81.9 us
  Pallas kernels  34.2 us (42%)
  waiting for transfers between devices  24.3 us (30%)
  starting transfers between devices  16.9 us (21%)
  other arithmetic  3.67 us (4%)
  local copies, waits for them, and re-layouts  2.13 us (3%)
    pallas_call x1, Pallas kernels, model(): pl.pallas_call(model_kernel, in_specs=[pl.BlockSpec(memory_space=pltpu.SM...  27.8 us
    ppermute x7, waiting for transfers between devices, total_over(): x = x + lax.ppermute(x, axis, [(i, i ^ hop) for i in range(count)])  12.5 us
    ppermute x3, waiting for transfers between devices, exchange(): return lax.ppermute(x, axis, perm) if perm else None  11.8 us
    ppermute x7, starting transfers between devices, total_over(): x = x + lax.ppermute(x, axis, [(i, i ^ hop) for i in range(count)])  11.5 us
    ppermute x3, starting transfers between devices, exchange(): return lax.ppermute(x, axis, perm) if perm else None  5.42 us
    pallas_call x1, Pallas kernels, gauges_and_rows(): pl.pallas_call(gauge_kernel, grid_spec=pltpu.PrefetchScalarGridSpec(num_s...  3.44 us
    pallas_call x1, Pallas kernels, edge_columns(): pl.pallas_call(column_kernel, grid_spec=pltpu.PrefetchScalarGridSpec(num_...  2.9 us
    add x6, other arithmetic, total_over(): x = x + lax.ppermute(x, axis, [(i, i ^ hop) for i in range(count)])  2.41 us
  transfers between devices with their start and end apart: 10, of which 8 were waited for; matrix products, arithmetic and copies ran while one was open for 2% of the time, Pallas kernels for 0%

commit v1 on v0

--- a/solution.py
+++ b/solution.py
@@ -12,6 +12,7 @@
 gauge_weight = 100.0
 REACH = 6
 LANES = 128
+LN2 = 0.6931471805599453
 SUB = 8
 
 
@@ -89,6 +90,7 @@
         ),
         out_shape=[jax.ShapeDtypeStruct((events, rows, cols), jnp.float32)]
         + [jax.ShapeDtypeStruct((fields, SUB, cols), jnp.float32)] * 2,
+        compiler_params=pltpu.CompilerParams(vmem_limit_bytes=56 * 1024 * 1024),
         name="gauges_and_rows",
     )(par, cells, *(depth, wet, bed, rough, direction) * 2)
 
@@ -151,6 +153,7 @@
             out_specs=[pl.BlockSpec(tall, lambda i, p: (0, 0))] * 2,
         ),
         out_shape=[jax.ShapeDtypeStruct(tall, jnp.float32)] * 2,
+        compiler_params=pltpu.CompilerParams(vmem_limit_bytes=12 * 1024 * 1024),
         name="edge_columns",
     )(par, *own, *own, rim_a, rim_b, rim_a, rim_b)
 
@@ -158,199 +161,240 @@
 def model_kernel(
     par, depth, wet, bed, rough, direction, counts, rim_a, rim_b, side_a, side_b,
     grad_ref, curve_ref,
-    hx, wx, bx, mx, qx, cx, inv_x, inv_y, sum_x, sum_y,
-    a_x, b_x, c_x, a_y, b_y, c_y, state, work, flow, g_x, g_y,
+    nat, hx, sb_x, sb_y, m_c, q_x, q_y, inv_x, inv_y, cond_x, cond_y, cnt,
+    a_x, b_x, c_x, a_y, b_y, c_y, tan_a, tan_b, flow, g_x, g_y, tmp,
 ):
     events, steps, rows, cols = depth.shape
     tall = rows + 2 * SUB
+    deep = tall // SUB
     tiles = cols // LANES
     count = tiles + 1
     even_row = par[0] == 1
     even_col = par[1] == 1
-    lane = lanes_of((tall, LANES))
+    lane_t = lanes_of((tall, LANES))
+    lane = lanes_of((SUB, LANES))
+    sub = lax.broadcasted_iota(jnp.int32, (SUB, LANES), 0)
+    last_lane, first_lane = lane == LANES - 1, lane == 0
     right_rim = jnp.where(even_col, side_a[...], side_b[...])
     left_rim = jnp.where(even_col, side_b[...], side_a[...])
-
-    def assemble(f, own, put):
+    J = [slice(j * LANES, (j + 1) * LANES) for j in range(count)]
+    zero = jnp.zeros((SUB, LANES), jnp.float32)
+
+    def assemble(f, own, k):
         top = jnp.where(even_row, rim_b[f], rim_a[f])
         bottom = jnp.where(even_row, rim_a[f], rim_b[f])
-        put(slice(0, SUB), slice(0, cols), top)
-        put(slice(SUB, SUB + rows), slice(0, cols), own)
-        put(slice(SUB + rows, tall), slice(0, cols), bottom)
+        for j in range(tiles):
+            nat[k, j, 0:SUB, :] = top[:, J[j]]
+            nat[k, j, SUB : SUB + rows, :] = own[:, J[j]]
+            nat[k, j, SUB + rows : tall, :] = bottom[:, J[j]]
         place = f * REACH
         r = pltpu.roll(right_rim, (LANES - place) % LANES, 1) if place else right_rim
         l = pltpu.roll(left_rim, (LANES - REACH - place) % LANES, 1)
-        extra = jnp.where(lane < REACH, r, jnp.where(lane >= LANES - REACH, l, 0.0))
-        put(slice(0, tall), slice(cols, cols + LANES), extra)
-
-    def into(ref, *lead):
-        def put(rs, cs, x):
-            ref[(*lead, rs, cs)] = x
-
-        return put
-
+        extra = jnp.where(lane_t < REACH, r, jnp.where(lane_t >= LANES - REACH, l, 0.0))
+        nat[k, tiles] = extra
+
+    def spread(k, i):
+        return [nat[k, j, pl.ds(i, SUB, stride=deep), :] for j in range(count)]
+
+    up = lambda x: pltpu.roll(x, SUB - 1, 0)
+    down = lambda x: pltpu.roll(x, 1, 0)
+    to_left = lambda x: pltpu.roll(x, LANES - 1, 1)
+    to_right = lambda x: pltpu.roll(x, 1, 1)
+
+    def right(xs):
+        r = [to_left(x) for x in xs]
+        return [jnp.where(last_lane, r[(j + 1) % count], r[j]) for j in range(count)]
+
+    def left(xs):
+        r = [to_right(x) for x in xs]
+        return [jnp.where(first_lane, r[j - 1], r[j]) for j in range(count)]
+
+    def get(ref, *at):
+        return [ref[(*at, slice(None), J[j])] for j in range(count)]
+
+    def put(xs, ref, *at):
+        for j in range(count):
+            ref[(*at, slice(None), J[j])] = xs[j]
+
+    def wrap(ref, *at):
+        put([up(x) for x in get(ref, *at, 0)], ref, *at, deep)
+
+    base = events * (steps + 1)
+    for k, (f, x) in enumerate(((base, bed), (base + 1, rough), (base + 2, direction))):
+        assemble(f, x[...], k)
+    for e in range(events):
+        assemble(events * steps + e, wet[e].astype(jnp.float32), 3 + e)
+        assemble(base + 3 + e, counts[e], 3 + events + e)
+        for t in range(steps):
+            assemble(e * steps + t, depth[e, t], 3 + 2 * events + e * steps + t)
+
+    @pl.loop(0, deep, unroll=5)
+    def _(i):
+        m = [jnp.exp(x) for x in spread(1, i)]
+        put(spread(0, i), tmp, 0, i)
+        put(m, tmp, 1, i)
+        put(m, m_c, i)
+        put([x * y for x, y in zip(m, spread(2, i))], tmp, 2, i)
+        for e in range(events):
+            put(spread(3 + e, i), tmp, 3 + e, i)
+            put(spread(3 + events + e, i), cnt, e, i)
+            for t in range(steps):
+                put(spread(3 + 2 * events + e * steps + t, i), hx, e, t, i)
+
+    for k in range(3 + events):
+        wrap(tmp, k)
     for e in range(events):
         for t in range(steps):
-            assemble(e * steps + t, depth[e, t], into(hx, e, t))
-        assemble(events * steps + e, wet[e].astype(jnp.float32), into(wx, e))
-        assemble(events * (steps + 1) + 3 + e, counts[e], into(cx, e))
-    base = events * (steps + 1)
-    assemble(base, bed[...], into(bx))
-    assemble(base + 1, rough[...], into(mx))
-    assemble(base + 2, direction[...], into(qx))
-
-    def at(j):
-        return pl.ds(pl.multiple_of(j * LANES, LANES), LANES)
-
-    def after(j):
-        return jnp.where(j == count - 1, 0, j + 1)
-
-    def before(j):
-        return jnp.where(j == 0, count - 1, j - 1)
-
-    below = lambda x: pltpu.roll(x, tall - 1, 0)
-    above = lambda x: pltpu.roll(x, 1, 0)
-
-    def right(x, nxt):
-        return jnp.where(lane == LANES - 1, pltpu.roll(nxt, LANES - 1, 1), pltpu.roll(x, LANES - 1, 1))
-
-    def left(x, prv):
-        return jnp.where(lane == 0, pltpu.roll(prv, 1, 1), pltpu.roll(x, 1, 1))
-
-    @pl.loop(0, count)
-    def _(j):
-        m = jnp.exp(mx[:, at(j)])
-        mx[:, at(j)] = m
-        qx[:, at(j)] = m * qx[:, at(j)]
+            wrap(hx, e, t)
 
     scale = time_step * 2.0 ** (-2.0 / 3.0)
 
-    @pl.loop(0, count)
-    def _(j):
-        n = after(j)
-        m, q = mx[:, at(j)], qx[:, at(j)]
-        inv_x[:, at(j)] = 1.0 / (m + right(m, mx[:, at(n)]))
-        inv_y[:, at(j)] = 1.0 / (m + below(m))
-        sum_x[:, at(j)] = q + right(q, qx[:, at(n)])
-        sum_y[:, at(j)] = q + below(q)
-        g_x[:, at(j)] = jnp.zeros((tall, LANES), jnp.float32)
-        g_y[:, at(j)] = jnp.zeros((tall, LANES), jnp.float32)
-
-    def face(h, h_k, s, cond, inv):
+    @pl.loop(0, deep, unroll=5)
+    def _(i):
+        b, m, q = (get(tmp, k, i) for k in range(3))
+        put([y - x for x, y in zip(b, right(b))], sb_x, i)
+        put([y - x for x, y in zip(b, get(tmp, 0, i + 1))], sb_y, i)
+        ix = [1.0 / (x + y) for x, y in zip(m, right(m))]
+        iy = [1.0 / (x + y) for x, y in zip(m, get(tmp, 1, i + 1))]
+        put([-x for x in ix], inv_x, i)
+        put([-x for x in iy], inv_y, i)
+        put([x + y for x, y in zip(q, right(q))], q_x, i)
+        put([x + y for x, y in zip(q, get(tmp, 2, i + 1))], q_y, i)
+        for e in range(events):
+            w = get(tmp, 3 + e, i)
+            put([(scale * z) * (x * y) for x, y, z in zip(w, right(w), ix)], cond_x, e, i)
+            put([(scale * z) * (x * y) for x, y, z in zip(w, get(tmp, 3 + e, i + 1), iy)], cond_y, e, i)
+        put([zero] * count, g_x, i)
+        put([zero] * count, g_y, i)
+
+    def face(h, h_k, sb, cond, inv):
         hs = h + h_k
+        s = (h_k - h) + sb
         x = s * s + slope_floor
-        lx = jnp.log(x)
-        p = cond * jnp.exp((2.0 / 3.0) * jnp.log(hs) - 0.25 * lx)
+        y = lax.rsqrt(x)
+        p = cond * (jnp.exp2((2.0 / 3.0 / LN2) * jnp.log(hs)) * (y * lax.rsqrt(y)))
+        ps = p * s
         t = p * hs
-        return (
-            (5.0 / 3.0) * (p * s),
-            t * (0.5 + (0.5 * slope_floor) * jnp.exp(-lx)),
-            -(t * s) * inv,
-        )
+        A = (5.0 / 3.0) * ps
+        B = t * (0.5 + (0.5 * slope_floor) * (y * y))
+        return A - B, A + B, (ps * hs) * inv
 
     curve_ref[...] = jnp.zeros(curve_ref.shape, jnp.float32)
+    put([zero] * count, flow, 0)
 
     @pl.loop(0, events)
     def _(e):
         for t in range(steps):
-
-            @pl.loop(0, count)
-            def _(j):
-                n = after(j)
-                h, b = hx[e, t, :, at(j)], bx[:, at(j)]
-                w = wx[e, :, at(j)]
-                h_n = hx[e, t, :, at(n)]
-                surface = h + b
-                inv = inv_x[:, at(j)]
-                A, B, C = face(
-                    h,
-                    right(h, h_n),
-                    right(surface, h_n + bx[:, at(n)]) - surface,
-                    (scale * inv) * (w * right(w, wx[e, :, at(n)])),
-                    inv,
-                )
-                inv = inv_y[:, at(j)]
-                A2, B2, C2 = face(
-                    h,
-                    below(h),
-                    below(surface) - surface,
-                    (scale * inv) * (w * below(w)),
-                    inv,
-                )
-                c_x[t, :, at(j)] = C
-                c_y[t, :, at(j)] = C2
-                fx = C * sum_x[:, at(j)]
-                fy = C2 * sum_y[:, at(j)]
+            old, new = (tan_a, tan_b) if t % 2 else (tan_b, tan_a)
+
+            @pl.loop(0, deep, unroll=5)
+            def _(i):
+                h = get(hx, e, t, i)
+                h_r, h_d = right(h), get(hx, e, t, i + 1)
                 if t:
-                    a_x[t - 1, :, at(j)] = A
-                    b_x[t - 1, :, at(j)] = B
-                    a_y[t - 1, :, at(j)] = A2
-                    b_y[t - 1, :, at(j)] = B2
-                    d = state[:, at(j)]
-                    k = right(d, state[:, at(n)])
-                    fx += A * (d + k) + B * (k - d)
-                    k = below(d)
-                    fy += A2 * (d + k) + B2 * (k - d)
-                    work[:, at(j)] = d + fx + (fy - above(fy))
-                else:
-                    work[:, at(j)] = fx + (fy - above(fy))
-                flow[:, at(j)] = fx
-
-            @pl.loop(0, count)
-            def _(j):
-                r = work[:, at(j)] - left(flow[:, at(j)], flow[:, at(before(j))])
-                if t == steps - 1:
-                    c = cx[e, :, at(j)] * gauge_weight
-                    s = c * r
-
-                    @pl.when(j < tiles)
-                    def _():
-                        own = (s * r)[SUB : SUB + rows]
-                        total = own[0:SUB]
-                        for i in range(1, rows // SUB):
-                            total += own[i * SUB : (i + 1) * SUB]
-                        curve_ref[...] += total
-
-                    r = s
-                state[:, at(j)] = r
+                    d = get(old, i)
+                    d_r, d_d = right(d), get(old, i + 1)
+                fx, fy = [], []
+                for j in range(count):
+                    A, B, C = face(h[j], h_r[j], sb_x[i, :, J[j]], cond_x[e, i, :, J[j]], inv_x[i, :, J[j]])
+                    f = C * q_x[i, :, J[j]]
+                    c_x[t, i, :, J[j]] = C
+                    if t:
+                        a_x[t - 1, i, :, J[j]] = A
+                        b_x[t - 1, i, :, J[j]] = B
+                        f += A * d[j] + B * d_r[j]
+                    fx.append(f)
+                    A, B, C = face(h[j], h_d[j], sb_y[i, :, J[j]], cond_y[e, i, :, J[j]], inv_y[i, :, J[j]])
+                    f = C * q_y[i, :, J[j]]
+                    c_y[t, i, :, J[j]] = C
+                    if t:
+                        a_y[t - 1, i, :, J[j]] = A
+                        b_y[t - 1, i, :, J[j]] = B
+                        f += A * d[j] + B * d_d[j]
+                    fy.append(f)
+                put(fy, flow, i + 1)
+                before = get(flow, i)
+                fl = left(fx)
+                for j in range(count):
+                    r = (fx[j] - fl[j]) + (fy[j] - before[j])
+                    new[i, :, J[j]] = d[j] + r if t else r
+
+            for j in range(count):
+                new[0, :, J[j]] = new[0, :, J[j]] - down(flow[deep, :, J[j]])
+            wrap(new)
+
+        old, new = (tan_a, tan_b) if steps % 2 else (tan_b, tan_a)
+
+        @pl.loop(0, deep, unroll=5)
+        def _(i):
+            row = sub * deep + i
+            own = (row >= SUB) & (row < SUB + rows)
+            total = zero
+            for j in range(count):
+                r = old[i, :, J[j]]
+                s = (gauge_weight * cnt[e, i, :, J[j]]) * r
+                old[i, :, J[j]] = s
+                if j < tiles:
+                    total += s * r
+            curve_ref[...] += jnp.where(own, total, 0.0)
+
+        wrap(old)
 
         for t in range(steps - 1, -1, -1):
-
-            @pl.loop(0, count)
-            def _(j):
-                n = after(j)
-                l = state[:, at(j)]
-                px = l - right(l, state[:, at(n)])
-                py = l - below(l)
-                g_x[:, at(j)] += c_x[t, :, at(j)] * px
-                g_y[:, at(j)] += c_y[t, :, at(j)] * py
+            back = steps - 1 - t
+            old, new = (tan_a, tan_b) if (steps + back) % 2 else (tan_b, tan_a)
+
+            @pl.loop(0, deep, unroll=5)
+            def _(i):
+                l = get(old, i)
+                l_r, l_d = right(l), get(old, i + 1)
+                acc, kx, ky = [], [], []
+                for j in range(count):
+                    p = l[j] - l_r[j]
+                    g_x[i, :, J[j]] += c_x[t, i, :, J[j]] * p
+                    if t:
+                        a = l[j] + a_x[t - 1, i, :, J[j]] * p
+                        kx.append(b_x[t - 1, i, :, J[j]] * p)
+                    p = l[j] - l_d[j]
+                    g_y[i, :, J[j]] += c_y[t, i, :, J[j]] * p
+                    if t:
+                        acc.append(a + a_y[t - 1, i, :, J[j]] * p)
+                        ky.append(b_y[t - 1, i, :, J[j]] * p)
                 if t:
-                    u, v = a_x[t - 1, :, at(j)] * px, b_x[t - 1, :, at(j)] * px
-                    u2, v2 = a_y[t - 1, :, at(j)] * py, b_y[t - 1, :, at(j)] * py
-                    work[:, at(j)] = l + (u - v) + (u2 - v2) + above(u2 + v2)
-                    flow[:, at(j)] = u + v
+                    put(ky, flow, i + 1)
+                    before = get(flow, i)
+                    kl = left(kx)
+                    for j in range(count):
+                        new[i, :, J[j]] = acc[j] + (kl[j] + before[j])
 
             if t:
-
-                @pl.loop(0, count)
-                def _(j):
-                    state[:, at(j)] = work[:, at(j)] + left(
-                        flow[:, at(j)], flow[:, at(before(j))]
-                    )
-
-    @pl.loop(0, tiles)
-    def _(j):
-        x, y = g_x[:, at(j)], g_y[:, at(j)]
-        g = mx[:, at(j)] * ((x + left(x, g_x[:, at(before(j))])) + (y + above(y)))
-        grad_ref[:, at(j)] = g[SUB : SUB + rows]
+                for j in range(count):
+                    new[0, :, J[j]] = new[0, :, J[j]] + down(flow[deep, :, J[j]])
+                wrap(new)
+
+    put([down(x) for x in get(g_y, deep - 1)], flow, 0)
+
+    @pl.loop(0, deep, unroll=5)
+    def _(i):
+        x, y = get(g_x, i), get(g_y, i)
+        put(y, flow, i + 1)
+        xl, yl = left(x), get(flow, i)
+        for j in range(tiles):
+            g = m_c[i, :, J[j]] * ((x[j] + xl[j]) + (y[j] + yl[j]))
+            nat[0, j, pl.ds(i, SUB, stride=deep), :] = g
+
+    for j in range(tiles):
+        grad_ref[:, J[j]] = nat[0, j, SUB : SUB + rows, :]
 
 
 def model(par, depth, wet, bed, rough, direction, counts, rim_a, rim_b, side_a, side_b):
     events, steps, rows, cols = depth.shape
     tall, wide = rows + 2 * SUB, cols + LANES
-    f32 = functools.partial(pltpu.VMEM, dtype=jnp.float32)
-    vm = lambda *lead: pltpu.VMEM((*lead, tall, wide), jnp.float32)
+    deep = tall // SUB
+    vm = lambda *lead: pltpu.VMEM((*lead, deep, SUB, wide), jnp.float32)
+    more = lambda *lead: pltpu.VMEM((*lead, deep + 1, SUB, wide), jnp.float32)
     vmem = pl.BlockSpec(memory_space=pltpu.VMEM)
+    fields = 3 + events * (steps + 2)
     return pl.pallas_call(
         model_kernel,
         in_specs=[pl.BlockSpec(memory_space=pltpu.SMEM)] + [vmem] * 10,
@@ -359,11 +403,20 @@
             jax.ShapeDtypeStruct((rows, cols), jnp.float32),
             jax.ShapeDtypeStruct((SUB, LANES), jnp.float32),
         ],
-        scratch_shapes=[vm(events, steps), vm(events), vm(), vm(), vm(), vm(events)]
-        + [vm()] * 4
-        + [vm(steps - 1), vm(steps - 1), vm(steps)] * 2
-        + [vm()] * 5,
-        compiler_params=pltpu.CompilerParams(vmem_limit_bytes=56 * 1024 * 1024),
+        scratch_shapes=[
+            pltpu.VMEM((fields, wide // LANES, tall, LANES), jnp.float32),
+            more(events, steps),
+            *[vm()] * 7,
+            *[vm(events)] * 3,
+            *[vm(steps - 1), vm(steps - 1), vm(steps)] * 2,
+            more(),
+            more(),
+            more(),
+            vm(),
+            vm(),
+            more(3 + events),
+        ],
+        compiler_params=pltpu.CompilerParams(vmem_limit_bytes=26 * 1024 * 1024),
         name="model",
     )(par, depth, wet, bed, rough, direction, counts, rim_a, rim_b, side_a, side_b)
 

time: 82.1 us -> 61 us (0.74)
  Pallas kernels: 34.2 us -> 14.7 us
  other arithmetic: 3.67 us -> 2.02 us
  local copies, waits for them, and re-layouts: 2.13 us -> 1.1 us
    pallas_call x1, Pallas kernels: 27.8 us -> 10.2 us  [model(): pl.pallas_call(model_kernel, in_specs=[pl.BlockSpec(memory_space=pltpu.SM...]
    pallas_call x1, Pallas kernels: 2.9 us -> 0.87 us  [edge_columns(): pl.pallas_call(column_kernel, grid_spec=pltpu.PrefetchScalarGridSpec(num_...]
    add x6, other arithmetic: 2.41 us -> 0.77 us  [total_over(): x = x + lax.ppermute(x, axis, [(i, i ^ hop) for i in range(count)])]
    broadcast_in_dim x1, local copies, waits for them, and re-layouts: 0.88 us -> 0.03 us  [local(): rim_b = jnp.zeros_like(rim_a)]
  transfers between devices with their start and end apart: 10 -> 10, of which waited for: 8 -> 8; matrix products, arithmetic and copies ran while one was open for 2% -> 1% of each run, Pallas kernels for 0% -> 0%
where the time goes in v1:
time: 61 us; the launch traced here: 60.8 us
  waiting for transfers between devices  24.5 us (40%)
  starting transfers between devices  17.7 us (29%)
  Pallas kernels  14.7 us (24%)
  other arithmetic  2.02 us (3%)
  local copies, waits for them, and re-layouts  1.1 us (2%)
  between operations  0.78 us (1%)
    ppermute x7, waiting for transfers between devices, total_over(): x = x + lax.ppermute(x, axis, [(i, i ^ hop) for i in range(count)])  13 us
    ppermute x7, starting transfers between devices, total_over(): x = x + lax.ppermute(x, axis, [(i, i ^ hop) for i in range(count)])  12.2 us
    ppermute x3, waiting for transfers between devices, exchange(): return lax.ppermute(x, axis, perm) if perm else None  11.6 us
    pallas_call x1, Pallas kernels, model(): pl.pallas_call(model_kernel, in_specs=[pl.BlockSpec(memory_space=pltpu.SM...  10.2 us
    ppermute x3, starting transfers between devices, exchange(): return lax.ppermute(x, axis, perm) if perm else None  5.48 us
    pallas_call x1, Pallas kernels, gauges_and_rows(): pl.pallas_call(gauge_kernel, grid_spec=pltpu.PrefetchScalarGridSpec(num_s...  3.6 us
  transfers between devices with their start and end apart: 10, of which 8 were waited for; matrix products, arithmetic and copies ran while one was open for 1% of the time, Pallas kernels for 0%

profile of v1, /device:TPU:0, one launch (start us, length us, event | category | flops | bytes accessed | tf_op | source)
XLA Modules:
  0.0 60.8 jit_solution(3492947309160672115)
XLA Ops:
  0.6 0.6 %pad_add_fusion.par = s32[2]{0:T(128)} fusion(s32[1]{0:T(128)} %bitcast.1, s32[1]{0:T(128)} %bitcast), kind=kLoop, calls=%fused_computation.1 | loop fusion | flops 2 | bytes 16 | tf_op jit(solution)/shard_map/stack | solution.py:436
  1.3 0.0 copy-start
  1.3 0.0 copy-start.1
  1.3 0.0 copy-start.2
  1.3 0.0 copy-start.3
  1.3 0.0 copy-start.4
  1.3 0.0 copy-start.7
  1.3 3.6 %gauges_and_rows.1 = (f32[2,64,1024]{2,1,0:T(8,128)}, f32[13,8,1024]{2,1,0:T(8,128)}, f32[13,8,1024]{2,1,0:T(8,128)}) custom-call(s32[2]{0:T(128)} %pad_add_fusion.par, s32[2,1,1024]{2,1,0:T(1,128)} %bitcast.3, f32[2,3,64,1024]{3,2,1,0:T(8,128)} %depth.1, s32[2,64,1024]{2,1,0:T(8,128)} %wet.1, f32[64,1024]{1,0:T(8,128)} %bed.1, f32[64,1024]{1,0:T(8,128)} %rough.1, ...), custom_call_target="tpu_custom_call" | custom-call | tf_op jit(solution)/shard_map/gauges_and_rows/pallas_call | solution.py:83
  4.9 3.0 %collective-permute-start = (f32[13,8,1024]{2,1,0:T(8,128)}, f32[13,8,1024]{2,1,0:T(8,128)S(1)}, u32[]{:S(2)}, u32[]{:S(2)}) collective-permute-start(f32[13,8,1024]{2,1,0:T(8,128)} %get-tuple-element.9), channel_id=1, source_target_pairs={{0,4},{4,0},{1,5},{5,1},{2,6},{6,2},{3,7},{7,3},{8,12},{12,8},{9,1... | collective-permute-start | bytes 1277960 | tf_op jit(solution)/shard_map/ppermute | solution.py:28
  7.9 10.0 %collective-permute-done.refs_12_.refs_14_.rim_a = f32[13,8,1024]{2,1,0:T(8,128)S(1)} collective-permute-done((f32[13,8,1024]{2,1,0:T(8,128)}, f32[13,8,1024]{2,1,0:T(8,128)S(1)}, u32[]{:S(2)}, u32[]{:S(2)}) %collective-permute-start) | collective-permute-done | bytes 426016 | tf_op jit(solution)/shard_map/ppermute | solution.py:28
  18.0 0.0 copy-done
  18.0 0.0 copy-done.1
  18.0 0.0 copy-done.2
  18.0 0.0 copy-done.3
  18.0 0.0 copy-done.4
  18.0 0.0 copy-done.7
  18.0 0.0 copy-start.5
  18.0 1.0 %copy-done.5 = f32[2,64,1024]{2,1,0:T(8,128)S(1)} copy-done((f32[2,64,1024]{2,1,0:T(8,128)S(1)}, f32[2,64,1024]{2,1,0:T(8,128)}, u32[]{:S(2)}) %copy-start.5) | copy-done | bytes 524312
  19.1 0.0 copy-start.6
  19.1 0.9 %edge_columns.1 = (f32[80,128]{1,0:T(8,128)S(1)}, f32[80,128]{1,0:T(8,128)S(1)}) custom-call(s32[2]{0:T(128)S(1)} %copy-done.7, f32[2,3,64,1024]{3,2,1,0:T(8,128)S(1)} %copy-done, s32[2,64,1024]{2,1,0:T(8,128)S(1)} %copy-done.1, f32[64,1024]{1,0:T(8,128)S(1)} %copy-done.2, f32[64,1024]{1,0:T(8,128)S(1)} %copy-done.3, f32[64,1024]{1,0:T(8,128)S(1)} %copy-done.4, ...), custom_call_target="tpu_custom_call" | custom-call | tf_op jit(solution)/shard_map/edge_columns/pallas_call | solution.py:147
  19.9 1.9 %collective-permute-start.1 = (f32[80,128]{1,0:T(8,128)S(1)}, f32[80,128]{1,0:T(8,128)S(1)}, u32[]{:S(2)}, u32[]{:S(2)}) collective-permute-start(f32[80,128]{1,0:T(8,128)S(1)} %get-tuple-element.10), channel_id=1, source_target_pairs={{0,1},{1,0},{2,3},{3,2},{4,5},{5,4},{6,7},{7,6},{8,9},{9,8},{10,11... | collective-permute-start | bytes 122888 | tf_op jit(solution)/shard_map/ppermute | solution.py:28
  21.8 0.7 %collective-permute-start.2 = (f32[80,128]{1,0:T(8,128)S(1)}, f32[80,128]{1,0:T(8,128)S(1)}, u32[]{:S(2)}, u32[]{:S(2)}) collective-permute-start(f32[80,128]{1,0:T(8,128)S(1)} %get-tuple-element.11), channel_id=1, source_target_pairs={{1,2},{2,1},{5,6},{6,5},{9,10},{10,9},{13,14},{14,13},{17,18},{18,... | collective-permute-start | bytes 122888 | tf_op jit(solution)/shard_map/ppermute | solution.py:28
  22.5 1.5 %collective-permute-done.1.side_a = f32[80,128]{1,0:T(8,128)S(1)} collective-permute-done((f32[80,128]{1,0:T(8,128)S(1)}, f32[80,128]{1,0:T(8,128)S(1)}, u32[]{:S(2)}, u32[]{:S(2)}) %collective-permute-start.1) | collective-permute-done | bytes 40992 | tf_op jit(solution)/shard_map/ppermute | solution.py:28
  24.0 0.0 collective-permute-done.2.side_b
  24.0 0.0 copy-done.6
  24.0 10.2 %model.1 = (f32[64,1024]{1,0:T(8,128)S(1)}, f32[8,128]{1,0:T(8,128)S(1)}) custom-call(s32[2]{0:T(128)S(1)} %copy-done.7, f32[2,3,64,1024]{3,2,1,0:T(8,128)S(1)} %copy-done, s32[2,64,1024]{2,1,0:T(8,128)S(1)} %copy-done.1, f32[64,1024]{1,0:T(8,128)S(1)} %copy-done.2, f32[64,1024]{1,0:T(8,128)S(1)} %copy-done.3, f32[64,1024]{1,0:T(8,128)S(1)} %copy-done.4, ...), custom_call_target="tpu_custom_call" | custom-call | tf_op jit(solution)/shard_map/model/pallas_call | solution.py:398
  34.2 0.1 collective-permute-start.3
  34.3 1.5 %collective-permute-done.3 = f32[64,1024]{1,0:T(8,128)S(1)} collective-permute-done((f32[64,1024]{1,0:T(8,128)S(1)}, f32[64,1024]{1,0:T(8,128)S(1)}, u32[]{:S(2)}, u32[]{:S(2)}) %collective-permute-start.3) | collective-permute-done | bytes 262176 | tf_op jit(solution)/shard_map/ppermute | solution.py:428
  35.8 1.8 %collective-permute-start.4 = (f32[64,1024]{1,0:T(8,128)S(1)}, f32[64,1024]{1,0:T(8,128)S(1)}, u32[]{:S(2)}, u32[]{:S(2)}) collective-permute-start(f32[64,1024]{1,0:T(8,128)S(1)} %add.30), channel_id=1, source_target_pairs={{0,16},{8,24},{16,0},{24,8},{1,17},{9,25},{17,1},{25,9},{2,18},{10... | collective-permute-start | bytes 786440 | tf_op jit(solution)/shard_map/ppermute | solution.py:428
  37.6 0.0 collective-permute-start.5
  37.6 1.2 %collective-permute-done.5 = f32[8,128]{1,0:T(8,128)S(1)} collective-permute-done((f32[8,128]{1,0:T(8,128)S(1)}, f32[8,128]{1,0:T(8,128)S(1)}, u32[]{:S(2)}, u32[]{:S(2)}) %collective-permute-start.5) | collective-permute-done | bytes 4128 | tf_op jit(solution)/shard_map/ppermute | solution.py:428
  38.8 0.3 collective-permute-start.6
  39.1 5.2 %collective-permute-done.6 = f32[8,128]{1,0:T(8,128)S(1)} collective-permute-done((f32[8,128]{1,0:T(8,128)S(1)}, f32[8,128]{1,0:T(8,128)S(1)}, u32[]{:S(2)}, u32[]{:S(2)}) %collective-permute-start.6) | collective-permute-done | bytes 4128 | tf_op jit(solution)/shard_map/ppermute | solution.py:428
  44.4 1.7 %collective-permute-start.7 = (f32[8,128]{1,0:T(8,128)S(1)}, f32[8,128]{1,0:T(8,128)S(1)}, u32[]{:S(2)}, u32[]{:S(2)}) collective-permute-start(f32[8,128]{1,0:T(8,128)S(1)} %add.33), channel_id=1, source_target_pairs={{0,4},{4,0},{1,5},{5,1},{2,6},{6,2},{3,7},{7,3},{8,12},{12,8},{9,1... | collective-permute-start | bytes 12296 | tf_op jit(solution)/shard_map/ppermute | solution.py:428
  46.1 1.9 %collective-permute-done.7 = f32[8,128]{1,0:T(8,128)S(1)} collective-permute-done((f32[8,128]{1,0:T(8,128)S(1)}, f32[8,128]{1,0:T(8,128)S(1)}, u32[]{:S(2)}, u32[]{:S(2)}) %collective-permute-start.7) | collective-permute-done | bytes 4128 | tf_op jit(solution)/shard_map/ppermute | solution.py:428
  48.0 4.8 %collective-permute-start.8 = (f32[8,128]{1,0:T(8,128)S(1)}, f32[8,128]{1,0:T(8,128)S(1)}, u32[]{:S(2)}, u32[]{:S(2)}) collective-permute-start(f32[8,128]{1,0:T(8,128)S(1)} %add.34), channel_id=1, source_target_pairs={{0,1},{1,0},{2,3},{3,2},{4,5},{5,4},{6,7},{7,6},{8,9},{9,8},{10,11... | collective-permute-start | bytes 12296 | tf_op jit(solution)/shard_map/ppermute | solution.py:428
  52.8 1.6 %collective-permute-done.8 = f32[8,128]{1,0:T(8,128)S(1)} collective-permute-done((f32[8,128]{1,0:T(8,128)S(1)}, f32[8,128]{1,0:T(8,128)S(1)}, u32[]{:S(2)}, u32[]{:S(2)}) %collective-permute-start.8) | collective-permute-done | bytes 4128 | tf_op jit(solution)/shard_map/ppermute | solution.py:428
  54.4 3.5 %collective-permute-start.9 = (f32[8,128]{1,0:T(8,128)S(1)}, f32[8,128]{1,0:T(8,128)S(1)}, u32[]{:S(2)}, u32[]{:S(2)}) collective-permute-start(f32[8,128]{1,0:T(8,128)S(1)} %add.35), channel_id=1, source_target_pairs={{0,2},{1,3},{2,0},{3,1},{4,6},{5,7},{6,4},{7,5},{8,10},{9,11},{10,... | collective-permute-start | bytes 12296 | tf_op jit(solution)/shard_map/ppermute | solution.py:428
  57.8 1.6 %collective-permute-done.9 = f32[8,128]{1,0:T(8,128)S(1)} collective-permute-done((f32[8,128]{1,0:T(8,128)S(1)}, f32[8,128]{1,0:T(8,128)S(1)}, u32[]{:S(2)}, u32[]{:S(2)}) %collective-permute-start.9) | collective-permute-done | bytes 4128 | tf_op jit(solution)/shard_map/ppermute | solution.py:428
  59.4 0.6 add_reduce_fusion
  60.0 0.0 collective-permute-done.4
  60.0 0.7 %add.31 = f32[64,1024]{1,0:T(8,128)} add(f32[64,1024]{1,0:T(8,128)S(1)} %add.30, f32[64,1024]{1,0:T(8,128)S(1)} %collective-permute-done.4) | non-fusion elementwise | flops 65536 | bytes 786432 | tf_op jit(solution)/shard_map/add | solution.py:428
  (6 shorter events, 0.1 us)
Async XLA Ops:
  1.3 16.7 %copy-start = (f32[2,3,64,1024]{3,2,1,0:T(8,128)S(1)}, f32[2,3,64,1024]{3,2,1,0:T(8,128)}, u32[]{:S(2)}) copy-start(f32[2,3,64,1024]{3,2,1,0:T(8,128)} %depth.1) | copy-start | bytes 4718596
  1.3 16.7 %copy-start.1 = (s32[2,64,1024]{2,1,0:T(8,128)S(1)}, s32[2,64,1024]{2,1,0:T(8,128)}, u32[]{:S(2)}) copy-start(s32[2,64,1024]{2,1,0:T(8,128)} %wet.1) | copy-start | bytes 1572868
  1.3 16.7 %copy-start.2 = (f32[64,1024]{1,0:T(8,128)S(1)}, f32[64,1024]{1,0:T(8,128)}, u32[]{:S(2)}) copy-start(f32[64,1024]{1,0:T(8,128)} %bed.1) | copy-start | bytes 786436
  1.3 16.7 %copy-start.3 = (f32[64,1024]{1,0:T(8,128)S(1)}, f32[64,1024]{1,0:T(8,128)}, u32[]{:S(2)}) copy-start(f32[64,1024]{1,0:T(8,128)} %rough.1) | copy-start | bytes 786436
  1.3 16.7 %copy-start.4 = (f32[64,1024]{1,0:T(8,128)S(1)}, f32[64,1024]{1,0:T(8,128)}, u32[]{:S(2)}) copy-start(f32[64,1024]{1,0:T(8,128)} %direction.1) | copy-start | bytes 786436
  1.3 16.7 %copy-start.7 = (s32[2]{0:T(128)S(1)}, s32[2]{0:T(128)}, u32[]{:S(2)}) copy-start(s32[2]{0:T(128)} %pad_add_fusion.par) | copy-start | bytes 28
  4.9 13.0 %collective-permute-start = (f32[13,8,1024]{2,1,0:T(8,128)}, f32[13,8,1024]{2,1,0:T(8,128)S(1)}, u32[]{:S(2)}, u32[]{:S(2)}) collective-permute-start(f32[13,8,1024]{2,1,0:T(8,128)} %get-tuple-element.9), channel_id=1, source_target_pairs={{0,4},{4,0},{1,5},{5,1},{2,6},{6,2},{3,7},{7,3},{8,12},{12,8},{9,1... | collective-permute-start | bytes 1277960 | tf_op jit(solution)/shard_map/ppermute | solution.py:28
  18.0 1.0 %copy-start.5 = (f32[2,64,1024]{2,1,0:T(8,128)S(1)}, f32[2,64,1024]{2,1,0:T(8,128)}, u32[]{:S(2)}) copy-start(f32[2,64,1024]{2,1,0:T(8,128)} %get-tuple-element.8.refs_5_.refs_11_.counts) | copy-start | bytes 1572868
  19.1 5.0 %copy-start.6 = (f32[2,64,1024]{2,1,0:T(8,128)S(1)}, f32[2,64,1024]{2,1,0:T(8,128)}, u32[]{:S(2)}) copy-start(f32[2,64,1024]{2,1,0:T(8,128)} %get-tuple-element.8.refs_5_.refs_11_.counts) | copy-start | bytes 1572868
  19.9 4.1 %collective-permute-start.1 = (f32[80,128]{1,0:T(8,128)S(1)}, f32[80,128]{1,0:T(8,128)S(1)}, u32[]{:S(2)}, u32[]{:S(2)}) collective-permute-start(f32[80,128]{1,0:T(8,128)S(1)} %get-tuple-element.10), channel_id=1, source_target_pairs={{0,1},{1,0},{2,3},{3,2},{4,5},{5,4},{6,7},{7,6},{8,9},{9,8},{10,11... | collective-permute-start | bytes 122888 | tf_op jit(solution)/shard_map/ppermute | solution.py:28
  21.8 2.2 %collective-permute-start.2 = (f32[80,128]{1,0:T(8,128)S(1)}, f32[80,128]{1,0:T(8,128)S(1)}, u32[]{:S(2)}, u32[]{:S(2)}) collective-permute-start(f32[80,128]{1,0:T(8,128)S(1)} %get-tuple-element.11), channel_id=1, source_target_pairs={{1,2},{2,1},{5,6},{6,5},{9,10},{10,9},{13,14},{14,13},{17,18},{18,... | collective-permute-start | bytes 122888 | tf_op jit(solution)/shard_map/ppermute | solution.py:28
  34.2 1.6 %collective-permute-start.3 = (f32[64,1024]{1,0:T(8,128)S(1)}, f32[64,1024]{1,0:T(8,128)S(1)}, u32[]{:S(2)}, u32[]{:S(2)}) collective-permute-start(f32[64,1024]{1,0:T(8,128)S(1)} %get-tuple-element.12), channel_id=1, source_target_pairs={{0,8},{8,0},{16,24},{24,16},{1,9},{9,1},{17,25},{25,17},{2,10},{10... | collective-permute-start | bytes 786440 | tf_op jit(solution)/shard_map/ppermute | solution.py:428
  35.8 24.2 %collective-permute-start.4 = (f32[64,1024]{1,0:T(8,128)S(1)}, f32[64,1024]{1,0:T(8,128)S(1)}, u32[]{:S(2)}, u32[]{:S(2)}) collective-permute-start(f32[64,1024]{1,0:T(8,128)S(1)} %add.30), channel_id=1, source_target_pairs={{0,16},{8,24},{16,0},{24,8},{1,17},{9,25},{17,1},{25,9},{2,18},{10... | collective-permute-start | bytes 786440 | tf_op jit(solution)/shard_map/ppermute | solution.py:428
  37.6 1.2 %collective-permute-start.5 = (f32[8,128]{1,0:T(8,128)S(1)}, f32[8,128]{1,0:T(8,128)S(1)}, u32[]{:S(2)}, u32[]{:S(2)}) collective-permute-start(f32[8,128]{1,0:T(8,128)S(1)} %get-tuple-element.13), channel_id=1, source_target_pairs={{0,8},{8,0},{16,24},{24,16},{1,9},{9,1},{17,25},{25,17},{2,10},{10... | collective-permute-start | bytes 12296 | tf_op jit(solution)/shard_map/ppermute | solution.py:428
  38.8 5.5 %collective-permute-start.6 = (f32[8,128]{1,0:T(8,128)S(1)}, f32[8,128]{1,0:T(8,128)S(1)}, u32[]{:S(2)}, u32[]{:S(2)}) collective-permute-start(f32[8,128]{1,0:T(8,128)S(1)} %add.32), channel_id=1, source_target_pairs={{0,16},{8,24},{16,0},{24,8},{1,17},{9,25},{17,1},{25,9},{2,18},{10... | collective-permute-start | bytes 12296 | tf_op jit(solution)/shard_map/ppermute | solution.py:428
  44.4 3.6 %collective-permute-start.7 = (f32[8,128]{1,0:T(8,128)S(1)}, f32[8,128]{1,0:T(8,128)S(1)}, u32[]{:S(2)}, u32[]{:S(2)}) collective-permute-start(f32[8,128]{1,0:T(8,128)S(1)} %add.33), channel_id=1, source_target_pairs={{0,4},{4,0},{1,5},{5,1},{2,6},{6,2},{3,7},{7,3},{8,12},{12,8},{9,1... | collective-permute-start | bytes 12296 | tf_op jit(solution)/shard_map/ppermute | solution.py:428
  48.0 6.4 %collective-permute-start.8 = (f32[8,128]{1,0:T(8,128)S(1)}, f32[8,128]{1,0:T(8,128)S(1)}, u32[]{:S(2)}, u32[]{:S(2)}) collective-permute-start(f32[8,128]{1,0:T(8,128)S(1)} %add.34), channel_id=1, source_target_pairs={{0,1},{1,0},{2,3},{3,2},{4,5},{5,4},{6,7},{7,6},{8,9},{9,8},{10,11... | collective-permute-start | bytes 12296 | tf_op jit(solution)/shard_map/ppermute | solution.py:428
  54.4 5.1 %collective-permute-start.9 = (f32[8,128]{1,0:T(8,128)S(1)}, f32[8,128]{1,0:T(8,128)S(1)}, u32[]{:S(2)}, u32[]{:S(2)}) collective-permute-start(f32[8,128]{1,0:T(8,128)S(1)} %add.35), channel_id=1, source_target_pairs={{0,2},{1,3},{2,0},{3,1},{4,6},{5,7},{6,4},{7,5},{8,10},{9,11},{10,... | collective-permute-start | bytes 12296 | tf_op jit(solution)/shard_map/ppermute | solution.py:428

commit v2 on v1

v2 whole, which is shorter than its diff:
```python
import functools

import jax
import jax.numpy as jnp
from jax import lax
from jax.experimental import pallas as pl
from jax.experimental.pallas import tpu as pltpu
from jax.sharding import PartitionSpec as P

time_step = 0.035
slope_floor = 0.01
gauge_weight = 100.0
REACH = 6
LANES = 128
LN2 = 0.6931471805599453
SUB = 8


def pairs(count, first):
    out = []
    for i in range(first, count - 1, 2):
        out += [(i, i + 1), (i + 1, i)]
    return out


def exchange(x, axis, first):
    perm = pairs(lax.axis_size(axis), first)
    return lax.ppermute(x, axis, perm) if perm else None


def lanes_of(shape):
    return lax.broadcasted_iota(jnp.int32, shape, 1)


def plan(events, steps):
    out, slot = [], 0
    for n in [REACH - t for _ in range(events) for t in range(steps)] + [REACH] * (events + 3) + [1] * events:
        out.append((n, slot))
        slot += n
    return out, -(-slot // SUB)


def one_hot(hit):
    return jnp.where(hit, 1.0, 0.0).astype(jnp.bfloat16)


def tally_of(row, col, rows, cols):
    gauges = row.shape[-1]
    tall = rows * (cols // 256)
    inside = (row >= 0) & (row < rows)
    high = jnp.where(inside, (col // 256) * rows + row, -1)
    hits = lax.dot_general(
        one_hot(lax.broadcasted_iota(jnp.int32, (tall, gauges), 0) == high),
        one_hot(lax.broadcasted_iota(jnp.int32, (256, gauges), 0) == col % 256),
        (((1,), (1,)), ((), ())),
        preferred_element_type=jnp.float32,
    )
    return [hits[b * rows : (b + 1) * rows] for b in range(cols // 256)]


def rows_kernel(sides, *refs):
    ins, pays, rest = refs[1:6], refs[6 : 6 + sides], refs[6 + sides :]
    cells, sems = rest[-2:]
    events, steps, rows, cols = ins[0].shape
    even = lax.axis_index("row") % 2 == 0
    slots, count = plan(events, steps)
    sub = lax.broadcasted_iota(jnp.int32, (SUB, cols), 0)
    copies = [pltpu.make_async_copy(refs[0], cells, sems.at[0, 5])]
    copies[0].start()
    for k in range(sides):
        sends_last = even if k == 0 else jnp.logical_not(even)
        edge = pl.multiple_of(jnp.where(sends_last, rows - SUB, 0), SUB)
        for i, x in enumerate(ins):
            lead = (slice(None),) * (len(x.shape) - 2)
            copy = pltpu.make_async_copy(
                x.at[(*lead, pl.ds(edge, SUB), slice(None))], rest[5 * k + i], sems.at[k, i]
            )
            copy.start()
            copies.append(copy)
    for copy in copies:
        copy.wait()
    for k, pay in enumerate(pays):
        d, w, b, r, v = rest[5 * k : 5 * k + 5]
        sends_last = even if k == 0 else jnp.logical_not(even)
        fields = [d[e, t] for e in range(events) for t in range(steps)]
        fields += [w[e].astype(jnp.float32) for e in range(events)] + [b[...], r[...], v[...]]
        fields += [jnp.broadcast_to(cells[e].astype(jnp.float32), (SUB, cols)) for e in range(events)]
        tiles = [jnp.zeros((SUB, cols), jnp.float32)] * count
        for x, (n, slot) in zip(fields, slots):
            if 1 < n < SUB:
                x = jnp.where(sends_last, pltpu.roll(x, n, 0), x)
            for i in range(slot // SUB, (slot + n - 1) // SUB + 1):
                low, high = slot - i * SUB, slot + n - i * SUB
                y = pltpu.roll(x, low % SUB, 0) if low % SUB else x
                tiles[i] = jnp.where((sub >= low) & (sub < high), y, tiles[i])
        for i in range(count):
            pay[i * SUB : (i + 1) * SUB] = tiles[i]


def edge_rows(cells, depth, wet, bed, rough, direction):
    events, steps, _, cols = depth.shape
    sides = 2 if lax.axis_size("row") > 2 else 1
    _, count = plan(events, steps)
    vmem, anywhere = pl.BlockSpec(memory_space=pltpu.VMEM), pl.BlockSpec(memory_space=pl.ANY)
    ins = (depth, wet, bed, rough, direction)
    return pl.pallas_call(
        functools.partial(rows_kernel, sides),
        in_specs=[anywhere] * 6,
        out_specs=[vmem] * sides,
        out_shape=[jax.ShapeDtypeStruct((count * SUB, cols), jnp.float32)] * sides,
        scratch_shapes=[pltpu.VMEM((*x.shape[:-2], SUB, cols), x.dtype) for x in ins] * sides
        + [pltpu.VMEM(cells.shape, cells.dtype), pltpu.SemaphoreType.DMA((sides, 6))],
        compiler_params=pltpu.CompilerParams(vmem_limit_bytes=58 * 1024 * 1024),
        name="edge_rows",
    )(cells, *ins)


def gauge_kernel(cells, cnt):
    events, rows, cols = cnt.shape
    for e in range(events):
        g = cells[e]
        for b, x in enumerate(tally_of(g // cols, g % cols, rows, cols)):
            cnt[e, :, b * 256 : (b + 1) * 256] = x


def gauges(cells, rows, cols):
    vmem = pl.BlockSpec(memory_space=pltpu.VMEM)
    return pl.pallas_call(
        gauge_kernel,
        in_specs=[vmem],
        out_specs=vmem,
        out_shape=jax.ShapeDtypeStruct((cells.shape[0], rows, cols), jnp.float32),
        compiler_params=pltpu.CompilerParams(vmem_limit_bytes=12 * 1024 * 1024),
        cost_estimate=pl.CostEstimate(flops=20000000, bytes_accessed=4000000, transcendentals=0),
        name="gauges",
    )(cells)


def column_kernel(sides, *refs):
    rims_in, own = refs[:sides], (refs[sides : sides + 6], refs[sides + 6 : sides + 12])
    rim_top, rim_bottom, pay_a, pay_b = refs[sides + 12 :]
    events, steps, rows, _ = own[0][0].shape
    cols = rim_top.shape[-1]
    even_row = lax.axis_index("row") % 2 == 0
    even_col = lax.axis_index("col") % 2 == 0
    sub = lax.broadcasted_iota(jnp.int32, (SUB, cols), 0)
    slots, _ = plan(events, steps)
    base = events * (steps + 1) + 3
    nothing = jnp.zeros((SUB, cols), jnp.float32)

    def field(ref, n, slot):
        x = nothing
        for i in range(slot // SUB, (slot + n - 1) // SUB + 1):
            low, high = slot - i * SUB, slot + n - i * SUB
            y = ref[i * SUB : (i + 1) * SUB]
            y = pltpu.roll(y, -low % SUB, 0) if low % SUB else y
            x = jnp.where((sub >= -low) & (sub < min(n, SUB - low)) & (sub >= max(0, -low)), y, x)
        return x

    for f in range(base):
        n, slot = slots[f]
        x = field(rims_in[0], n, slot)
        y = field(rims_in[1], n, slot) if sides > 1 else nothing
        rim_bottom[f] = jnp.where(even_row, x, y)
        rim_top[f] = pltpu.roll(jnp.where(even_row, y, x), SUB - n, 0)
    for e in range(events):
        slot = slots[base + e][1]
        for k in range(2):
            lower = even_row if k == 0 else jnp.logical_not(even_row)
            if k < sides:
                g = rims_in[k][slot : slot + 1].astype(jnp.int32)
                row = g // cols - jnp.where(lower, 0, rows - SUB)
                hits = jnp.concatenate(tally_of(row, g % cols, SUB, cols), axis=1)
            else:
                hits = nothing
            if k == 0:
                first = hits
        rim_bottom[base + e] = jnp.where(even_row, first, hits)
        rim_top[base + e] = jnp.where(even_row, hits, first)

    lane = lanes_of((rows + 2 * SUB, LANES))
    packs = []
    for side in range(2):
        d, w, b, r, v, c = own[side]
        place_of = slice(0, LANES) if side == 0 else slice(cols - LANES, cols)
        pack = jnp.zeros((rows + 2 * SUB, LANES), jnp.float32)
        xs = [d[e, t] for e in range(events) for t in range(steps)]
        xs += [w[e].astype(jnp.float32) for e in range(events)]
        xs += [b[...], r[...], v[...]]
        xs += [c[e] for e in range(events)]
        for f, x in enumerate(xs):
            x = jnp.concatenate([rim_top[f, :, place_of], x, rim_bottom[f, :, place_of]], axis=0)
            place = f * REACH
            shift = (place + REACH if side == 1 else place) % LANES
            if shift:
                x = pltpu.roll(x, shift, 1)
            pack = jnp.where((lane >= place) & (lane < place + REACH), x, pack)
        packs.append(pack)
    pay_a[...] = jnp.where(even_col, packs[1], packs[0])
    pay_b[...] = jnp.where(even_col, packs[0], packs[1])


def rims_and_columns(rims, depth, wet, bed, rough, direction, counts):
    events, steps, rows, cols = depth.shape
    last = cols // LANES - 1

    def side(j):
        return [
            pl.BlockSpec((events, steps, rows, LANES), lambda i: (0, 0, 0, j)),
            pl.BlockSpec((events, rows, LANES), lambda i: (0, 0, j)),
            pl.BlockSpec((rows, LANES), lambda i: (0, j)),
            pl.BlockSpec((rows, LANES), lambda i: (0, j)),
            pl.BlockSpec((rows, LANES), lambda i: (0, j)),
            pl.BlockSpec((events, rows, LANES), lambda i: (0, 0, j)),
        ]

    whole = lambda shape: pl.BlockSpec(shape, lambda i: (0,) * len(shape))
    tall = (rows + 2 * SUB, LANES)
    rim = (events * (steps + 2) + 3, SUB, cols)
    own = (depth, wet, bed, rough, direction, counts)
    return pl.pallas_call(
        functools.partial(column_kernel, len(rims)),
        grid=(1,),
        in_specs=[whole(r.shape) for r in rims] + side(0) + side(last),
        out_specs=[whole(rim)] * 2 + [whole(tall)] * 2,
        out_shape=[jax.ShapeDtypeStruct(rim, jnp.float32)] * 2 + [jax.ShapeDtypeStruct(tall, jnp.float32)] * 2,
        compiler_params=pltpu.CompilerParams(vmem_limit_bytes=12 * 1024 * 1024),
        name="rims_and_columns",
    )(*rims, *own, *own)


def up(x):
    return pltpu.roll(x, SUB - 1, 0)


def down(x):
    return pltpu.roll(x, 1, 0)


def right(xs):
    last = lanes_of((SUB, LANES)) == LANES - 1
    r = [pltpu.roll(x, LANES - 1, 1) for x in xs]
    return [jnp.where(last, r[(j + 1) % len(xs)], r[j]) for j in range(len(xs))]


def left(xs):
    first = lanes_of((SUB, LANES)) == 0
    r = [pltpu.roll(x, 1, 1) for x in xs]
    return [jnp.where(first, r[j - 1], r[j]) for j in range(len(xs))]


def at_lanes(j):
    return slice(j * LANES, (j + 1) * LANES)


def get(ref, *at):
    return [ref[(*at, slice(None), at_lanes(j))] for j in range(ref.shape[-1] // LANES)]


def put(xs, ref, *at):
    for j, x in enumerate(xs):
        ref[(*at, slice(None), at_lanes(j))] = x


def wrap(ref, *at):
    deep = ref.shape[-3] - 1
    put([up(x) for x in get(ref, *at, 0)], ref, *at, deep)


def tangent_kernel(
    depth, wet, bed, rough, direction, counts, rim_top, rim_bottom, side_a, side_b,
    curve_ref, m_c, source, a_x, b_x, c_x, a_y, b_y, c_y,
    nat, hx, sb_x, sb_y, q_x, q_y, inv_x, inv_y, cond_x, cond_y, cnt,
    tan_a, tan_b, flow, tmp,
):
    events, steps, rows, cols = depth.shape
    tall = rows + 2 * SUB
    deep = tall // SUB
    tiles = cols // LANES
    count = tiles + 1
    even_col = lax.axis_index("col") % 2 == 0
    lane_t = lanes_of((tall, LANES))
    sub = lax.broadcasted_iota(jnp.int32, (SUB, LANES), 0)
    right_rim = jnp.where(even_col, side_a[...], side_b[...])
    left_rim = jnp.where(even_col, side_b[...], side_a[...])
    J = [slice(j * LANES, (j + 1) * LANES) for j in range(count)]
    zero = jnp.zeros((SUB, LANES), jnp.float32)

    def assemble(f, own, k):
        for j in range(tiles):
            nat[k, j, 0:SUB, :] = rim_top[f, :, J[j]]
            nat[k, j, SUB : SUB + rows, :] = own[:, J[j]]
            nat[k, j, SUB + rows : tall, :] = rim_bottom[f, :, J[j]]
        place = f * REACH
        r = pltpu.roll(right_rim, (LANES - place) % LANES, 1) if place else right_rim
        l = pltpu.roll(left_rim, (LANES - REACH - place) % LANES, 1)
        extra = jnp.where(lane_t < REACH, r, jnp.where(lane_t >= LANES - REACH, l, 0.0))
        nat[k, tiles] = extra

    def spread(k, i):
        return [nat[k, j, pl.ds(i, SUB, stride=deep), :] for j in range(count)]

    base = events * (steps + 1)
    for k, (f, x) in enumerate(((base, bed), (base + 1, rough), (base + 2, direction))):
        assemble(f, x[...], k)
    for e in range(events):
        assemble(events * steps + e, wet[e].astype(jnp.float32), 3 + e)
        assemble(base + 3 + e, counts[e], 3 + events + e)
        for t in range(steps):
            assemble(e * steps + t, depth[e, t], 3 + 2 * events + e * steps + t)

    @pl.loop(0, deep, unroll=5)
    def _(i):
        m = [jnp.exp(x) for x in spread(1, i)]
        put(spread(0, i), tmp, 0, i)
        put(m, tmp, 1, i)
        put(m, m_c, i)
        put([x * y for x, y in zip(m, spread(2, i))], tmp, 2, i)
        for e in range(events):
            put(spread(3 + e, i), tmp, 3 + e, i)
            put(spread(3 + events + e, i), cnt, e, i)
            for t in range(steps):
                put(spread(3 + 2 * events + e * steps + t, i), hx, e, t, i)

    for k in range(3 + events):
        wrap(tmp, k)
    for e in range(events):
        for t in range(steps):
            wrap(hx, e, t)

    scale = time_step * 2.0 ** (-2.0 / 3.0)

    @pl.loop(0, deep, unroll=5)
    def _(i):
        b, m, q = (get(tmp, k, i) for k in range(3))
        put([y - x for x, y in zip(b, right(b))], sb_x, i)
        put([y - x for x, y in zip(b, get(tmp, 0, i + 1))], sb_y, i)
        ix = [1.0 / (x + y) for x, y in zip(m, right(m))]
        iy = [1.0 / (x + y) for x, y in zip(m, get(tmp, 1, i + 1))]
        put([-x for x in ix], inv_x, i)
        put([-x for x in iy], inv_y, i)
        put([x + y for x, y in zip(q, right(q))], q_x, i)
        put([x + y for x, y in zip(q, get(tmp, 2, i + 1))], q_y, i)
        for e in range(events):
            w = get(tmp, 3 + e, i)
            put([(scale * z) * (x * y) for x, y, z in zip(w, right(w), ix)], cond_x, e, i)
            put([(scale * z) * (x * y) for x, y, z in zip(w, get(tmp, 3 + e, i + 1), iy)], cond_y, e, i)

    def face(h, h_k, sb, cond, inv):
        hs = h + h_k
        s = (h_k - h) + sb
        x = s * s + slope_floor
        y = lax.rsqrt(x)
        p = cond * (jnp.exp2((2.0 / 3.0 / LN2) * jnp.log(hs)) * (y * lax.rsqrt(y)))
        ps = p * s
        t = p * hs
        A = (5.0 / 3.0) * ps
        B = t * (0.5 + (0.5 * slope_floor) * (y * y))
        return A - B, A + B, (ps * hs) * inv

    curve_ref[...] = jnp.zeros(curve_ref.shape, jnp.float32)
    put([zero] * count, flow, 0)

    @pl.loop(0, events)
    def _(e):
        for t in range(steps):
            old, new = (tan_a, tan_b) if t % 2 else (tan_b, tan_a)

            @pl.loop(0, deep, unroll=5)
            def _(i):
                h = get(hx, e, t, i)
                h_r, h_d = right(h), get(hx, e, t, i + 1)
                if t:
                    d = get(old, i)
                    d_r, d_d = right(d), get(old, i + 1)
                fx, fy = [], []
                for j in range(count):
                    A, B, C = face(h[j], h_r[j], sb_x[i, :, J[j]], cond_x[e, i, :, J[j]], inv_x[i, :, J[j]])
                    f = C * q_x[i, :, J[j]]
                    c_x[e, t, i, :, J[j]] = C
                    if t:
                        a_x[e, t - 1, i, :, J[j]] = A
                        b_x[e, t - 1, i, :, J[j]] = B
                        f += A * d[j] + B * d_r[j]
                    fx.append(f)
                    A, B, C = face(h[j], h_d[j], sb_y[i, :, J[j]], cond_y[e, i, :, J[j]], inv_y[i, :, J[j]])
                    f = C * q_y[i, :, J[j]]
                    c_y[e, t, i, :, J[j]] = C
                    if t:
                        a_y[e, t - 1, i, :, J[j]] = A
                        b_y[e, t - 1, i, :, J[j]] = B
                        f += A * d[j] + B * d_d[j]
                    fy.append(f)
                put(fy, flow, i + 1)
                before = get(flow, i)
                fl = left(fx)
                for j in range(count):
                    r = (fx[j] - fl[j]) + (fy[j] - before[j])
                    new[i, :, J[j]] = d[j] + r if t else r

            for j in range(count):
                new[0, :, J[j]] = new[0, :, J[j]] - down(flow[deep, :, J[j]])
            wrap(new)

        old = tan_a if steps % 2 else tan_b

        @pl.loop(0, deep, unroll=5)
        def _(i):
            row = sub * deep + i
            own = (row >= SUB) & (row < SUB + rows)
            total = zero
            for j in range(count):
                r = old[i, :, J[j]]
                s = (gauge_weight * cnt[e, i, :, J[j]]) * r
                source[e, i, :, J[j]] = s
                if j < tiles:
                    total += s * r
            curve_ref[...] += jnp.where(own, total, 0.0)

        wrap(source, e)


def adjoint_kernel(first_event, last_event, m_c, source, a_x, b_x, c_x, a_y, b_y, c_y, *refs):
    sums = () if first_event else refs[:2]
    outs = refs[len(sums) : len(sums) + (1 if last_event else 2)]
    nat, adj_a, adj_b, flow, *own = refs[len(sums) + len(outs) :]
    g_x, g_y = own if last_event else outs
    steps, deep, _, wide = c_x.shape
    count = wide // LANES
    J = [at_lanes(j) for j in range(count)]
    zero = jnp.zeros((SUB, LANES), jnp.float32)
    put([zero] * count, flow, 0)

    for t in range(steps - 1, -1, -1):
        old, new = (adj_a, adj_b) if t % 2 else (adj_b, adj_a)
        if t == steps - 1:
            old = source
            base_x, base_y = sums if sums else (None, None)
        else:
            base_x, base_y = g_x, g_y

        @pl.loop(0, deep, unroll=5)
        def _(i):
            l = get(old, i)
            l_r, l_d = right(l), get(old, i + 1)
            acc, kx, ky = [], [], []
            for j in range(count):
                p = l[j] - l_r[j]
                g = c_x[t, i, :, J[j]] * p
                g_x[i, :, J[j]] = g + base_x[i, :, J[j]] if base_x is not None else g
                if t:
                    a = l[j] + a_x[t - 1, i, :, J[j]] * p
                    kx.append(b_x[t - 1, i, :, J[j]] * p)
                p = l[j] - l_d[j]
                g = c_y[t, i, :, J[j]] * p
                g_y[i, :, J[j]] = g + base_y[i, :, J[j]] if base_y is not None else g
                if t:
                    acc.append(a + a_y[t - 1, i, :, J[j]] * p)
                    ky.append(b_y[t - 1, i, :, J[j]] * p)
            if t:
                put(ky, flow, i + 1)
                before = get(flow, i)
                kl = left(kx)
                for j in range(count):
                    new[i, :, J[j]] = acc[j] + (kl[j] + before[j])

        if t:
            for j in range(count):
                new[0, :, J[j]] = new[0, :, J[j]] + down(flow[deep, :, J[j]])
            wrap(new)

    if last_event:
        (grad_ref,) = outs
        rows, cols = grad_ref.shape
        tiles = cols // LANES
        put([down(x) for x in get(g_y, deep - 1)], flow, 0)

        @pl.loop(0, deep, unroll=5)
        def _(i):
            x, y = get(g_x, i), get(g_y, i)
            put(y, flow, i + 1)
            xl, yl = left(x), get(flow, i)
            for j in range(tiles):
                g = m_c[i, :, J[j]] * ((x[j] + xl[j]) + (y[j] + yl[j]))
                nat[j, pl.ds(i, SUB, stride=deep), :] = g

        for j in range(tiles):
            grad_ref[:, J[j]] = nat[j, SUB : SUB + rows, :]


def tangents(depth, wet, bed, rough, direction, counts, rim_top, rim_bottom, side_a, side_b):
    events, steps, rows, cols = depth.shape
    tall, wide = rows + 2 * SUB, cols + LANES
    deep = tall // SUB
    shape = lambda *lead: (*lead, deep, SUB, wide)
    vm = lambda *lead: pltpu.VMEM(shape(*lead), jnp.float32)
    more = lambda *lead: pltpu.VMEM((*lead, deep + 1, SUB, wide), jnp.float32)
    out = lambda *lead: jax.ShapeDtypeStruct(shape(*lead), jnp.float32)
    vmem = pl.BlockSpec(memory_space=pltpu.VMEM)
    fields = 3 + events * (steps + 2)
    return pl.pallas_call(
        tangent_kernel,
        in_specs=[vmem] * 10,
        out_specs=[vmem] * 9,
        out_shape=[
            jax.ShapeDtypeStruct((SUB, LANES), jnp.float32),
            out(),
            jax.ShapeDtypeStruct((events, deep + 1, SUB, wide), jnp.float32),
            *[out(events, steps - 1), out(events, steps - 1), out(events, steps)] * 2,
        ],
        scratch_shapes=[
            pltpu.VMEM((fields, wide // LANES, tall, LANES), jnp.float32),
            more(events, steps),
            *[vm()] * 6,
            *[vm(events)] * 3,
            *[more()] * 3,
            more(3 + events),
        ],
        compiler_params=pltpu.CompilerParams(vmem_limit_bytes=20 * 1024 * 1024),
        name="tangents",
    )(depth, wet, bed, rough, direction, counts, rim_top, rim_bottom, side_a, side_b)


def gradient(e, rows, cols, sums, m_c, source, *coefficients):
    events, _, _, wide = source.shape
    deep = m_c.shape[0]
    first, last = e == 0, e == events - 1
    vm = (deep, SUB, wide)
    more = pltpu.VMEM((deep + 1, SUB, wide), jnp.float32)
    vmem = pl.BlockSpec(memory_space=pltpu.VMEM)
    own = lambda x: pl.BlockSpec((None, *x.shape[1:]), lambda i: (e,) + (0,) * (x.ndim - 1))
    whole = lambda shape: pl.BlockSpec(shape, lambda i: (0,) * len(shape))
    return pl.pallas_call(
        functools.partial(adjoint_kernel, first, last),
        grid=(1,),
        in_specs=[whole(m_c.shape), own(source)] + [own(x) for x in coefficients] + [whole(vm)] * len(sums),
        out_specs=whole((rows, cols)) if last else [whole(vm)] * 2,
        out_shape=jax.ShapeDtypeStruct((rows, cols), jnp.float32)
        if last
        else [jax.ShapeDtypeStruct(vm, jnp.float32)] * 2,
        scratch_shapes=[pltpu.VMEM((cols // LANES, deep * SUB, LANES), jnp.float32), more, more, more]
        + [pltpu.VMEM(vm, jnp.float32)] * (2 if last else 0),
        compiler_params=pltpu.CompilerParams(vmem_limit_bytes=16 * 1024 * 1024),
        cost_estimate=pl.CostEstimate(flops=40000000, bytes_accessed=12000000, transcendentals=0),
        name="gradient",
    )(m_c, source, *coefficients, *sums)


def hops_over(axis):
    count, hop, out = lax.axis_size(axis), 1, []
    while hop < count:
        out.append((axis, hop))
        hop *= 2
    return out


def hop_sum(x, axis, hop):
    return x + lax.ppermute(x, axis, [(i, i ^ hop) for i in range(lax.axis_size(axis))])


def local(depth, wet, bed, rough, direction, gauge_cells):
    events, steps, rows, cols = depth.shape
    cells = gauge_cells.reshape(events, 1, -1)
    pays = edge_rows(cells, depth, wet, bed, rough, direction)
    rims = [exchange(x, "row", k) for k, x in enumerate(pays)]
    counts = gauges(cells, rows, cols)
    rim_top, rim_bottom, send_a, send_b = rims_and_columns(
        rims, depth, wet, bed, rough, direction, counts
    )
    side_b = exchange(send_b, "col", 1)
    side_a = exchange(send_a, "col", 0)
    curve, *coefficients = tangents(
        depth, wet, bed, rough, direction, counts, rim_top, rim_bottom, side_a, side_b
    )
    hops = hops_over("event") + hops_over("row") + hops_over("col")
    sums = ()
    for e in range(events):
        sums = gradient(e, rows, cols, sums, *coefficients)
        if hops:
            curve = hop_sum(curve, *hops.pop(0))
            sums, curve = lax.optimization_barrier((sums, curve))
    grad = sums
    for axis, hop in hops_over("event"):
        grad = hop_sum(grad, axis, hop)
    for axis, hop in hops:
        curve = hop_sum(curve, axis, hop)
    return (grad, jnp.sum(curve))


def solution(mesh):
    placed = (
        P("event", None, "row", "col"),
        P("event", "row", "col"),
        P("row", "col"),
        P("row", "col"),
        P("row", "col"),
        P("event", "row", "col", None),
    )
    return jax.shard_map(
        local, mesh=mesh, in_specs=placed, out_specs=(P("row", "col"), P()), check_vma=False
    )
```

time: 61 us -> 48.4 us (0.79)
  waiting for transfers between devices: 24.5 us -> 14.7 us
  Pallas kernels: 14.7 us -> 12.6 us
  local copies, waits for them, and re-layouts: 1.1 us -> 0.03 us
  starting transfers between devices: 17.7 us -> 18.7 us
  other arithmetic: 2.02 us -> 1.37 us
    ppermute x7, waiting for transfers between devices: 13 us -> 7.17 us  [hop_sum(): lax.ppermute(x, axis, [(i, i ^ hop) for i in range(lax.axis_size(axis))])]
    ppermute x3, waiting for transfers between devices: 11.6 us -> 7.56 us  [exchange(): return lax.ppermute(x, axis, perm) if perm else None]
    pallas_call x3 -> x6, Pallas kernels: 14.7 us -> 12.6 us  [the longest x1 6.98 us: tangents(): pl.pallas_call(tangent_kernel, in_specs=[vmem] * 10, out_specs=[vmem] * 9...]
    unnamed x16 -> x12, local copies, waits for them, and re-layouts: 1.06 us -> 0.03 us
    ppermute x7, starting transfers between devices: 12.2 us -> 13.2 us  [hop_sum(): lax.ppermute(x, axis, [(i, i ^ hop) for i in range(lax.axis_size(axis))])]
    another operation x1 -> x0, other arithmetic: 0.65 us -> none  [local(): jnp.stack([1 - lax.axis_index('row') % 2, 1 - lax.axis_index('col') % 2])]
  transfers between devices with their start and end apart: 10 -> 10, of which waited for: 8 -> 7; matrix products, arithmetic and copies ran while one was open for 1% -> 1% of each run, Pallas kernels for 0% -> 7%
where the time goes in v2:
time: 48.4 us; the launch traced here: 48.2 us
  starting transfers between devices  18.7 us (39%)
  waiting for transfers between devices  14.7 us (30%)
  Pallas kernels  12.6 us (26%)
  other arithmetic  1.37 us (3%)
  between operations  0.78 us (2%)
    ppermute x7, starting transfers between devices, hop_sum(): lax.ppermute(x, axis, [(i, i ^ hop) for i in range(lax.axis_size(axis))])  13.2 us
    ppermute x3, waiting for transfers between devices, exchange(): return lax.ppermute(x, axis, perm) if perm else None  7.56 us
    ppermute x7, waiting for transfers between devices, hop_sum(): lax.ppermute(x, axis, [(i, i ^ hop) for i in range(lax.axis_size(axis))])  7.17 us
    pallas_call x1, Pallas kernels, tangents(): pl.pallas_call(tangent_kernel, in_specs=[vmem] * 10, out_specs=[vmem] * 9...  6.98 us
    ppermute x3, starting transfers between devices, exchange(): return lax.ppermute(x, axis, perm) if perm else None  5.5 us
    pallas_call x2, Pallas kernels, gradient(): pl.pallas_call(functools.partial(adjoint_kernel, first, last), grid=(1,),...  2.67 us
    pallas_call x1, Pallas kernels, edge_rows(): pl.pallas_call(functools.partial(rows_kernel, sides), in_specs=[anywhere]...  1.92 us
  transfers between devices with their start and end apart: 10, of which 7 were waited for; matrix products, arithmetic and copies ran while one was open for 1% of the time, Pallas kernels for 7%

profile of v2, /device:TPU:0, one launch (start us, length us, event | category | flops | bytes accessed | tf_op | source)
XLA Modules:
  0.0 48.2 jit_solution(5129949617049576380)
XLA Ops:
  0.6 0.0 copy-start.5
  0.6 0.0 copy-start
  0.7 0.0 copy-start.1
  0.7 0.0 copy-start.2
  0.7 0.0 copy-start.3
  0.7 0.0 copy-start.4
  0.7 1.9 %edge_rows.1 = f32[64,1024]{1,0:T(8,128)} custom-call(s32[2,1,1024]{2,1,0:T(1,128)} %bitcast.1, f32[2,3,64,1024]{3,2,1,0:T(8,128)} %depth.1, s32[2,64,1024]{2,1,0:T(8,128)} %wet.1, f32[64,1024]{1,0:T(8,128)} %bed.1, f32[64,1024]{1,0:T(8,128)} %rough.1, f32[64,1024]{1,0:T(8,128)} %direction.1), custom_call_target="tpu_custom_call" | custom-call | tf_op jit(solution)/shard_map/edge_rows/pallas_call | solution.py:106
  2.6 3.0 %collective-permute-start = (f32[64,1024]{1,0:T(8,128)}, f32[64,1024]{1,0:T(8,128)S(1)}, u32[]{:S(2)}, u32[]{:S(2)}) collective-permute-start(f32[64,1024]{1,0:T(8,128)} %edge_rows.1), channel_id=1, source_target_pairs={{0,4},{4,0},{1,5},{5,1},{2,6},{6,2},{3,7},{7,3},{8,12},{12,8},{9,1... | collective-permute-start | bytes 786440 | tf_op jit(solution)/shard_map/ppermute | solution.py:28
  5.7 0.0 copy-done.5
  5.7 0.5 %gauges.1.refs_6_.refs_12_.counts = f32[2,64,1024]{2,1,0:T(8,128)S(1)} custom-call(s32[2,1,1024]{2,1,0:T(1,128)S(1)} %bitcast.2), custom_call_target="tpu_custom_call" | custom-call | flops 20000000 | bytes 4000000 | tf_op jit(solution)/shard_map/gauges/pallas_call | solution.py:128
  6.2 6.0 %collective-permute-done.refs_0_ = f32[64,1024]{1,0:T(8,128)S(1)} collective-permute-done((f32[64,1024]{1,0:T(8,128)}, f32[64,1024]{1,0:T(8,128)S(1)}, u32[]{:S(2)}, u32[]{:S(2)}) %collective-permute-start) | collective-permute-done | bytes 262176 | tf_op jit(solution)/shard_map/ppermute | solution.py:28
  12.2 0.0 copy-done
  12.2 0.0 copy-done.1
  12.2 0.0 copy-done.2
  12.2 0.0 copy-done.3
  12.2 0.0 copy-done.4
  12.2 0.5 %rims_and_columns.1 = (f32[13,8,1024]{2,1,0:T(8,128)S(1)}, f32[13,8,1024]{2,1,0:T(8,128)S(1)}, f32[80,128]{1,0:T(8,128)S(1)}, f32[80,128]{1,0:T(8,128)S(1)}) custom-call(f32[64,1024]{1,0:T(8,128)S(1)} %collective-permute-done.refs_0_, f32[2,3,64,1024]{3,2,1,0:T(8,128)S(1)} %copy-done, s32[2,64,1024]{2,1,0:T(8,128)S(1)} %copy-done.1, ...), custom_call_target="tpu_custom_call" | custom-call | tf_op jit(solution)/shard_map/rims_and_columns/pallas_call | solution.py:221
  12.7 1.8 %collective-permute-start.1 = (f32[80,128]{1,0:T(8,128)S(1)}, f32[80,128]{1,0:T(8,128)S(1)}, u32[]{:S(2)}, u32[]{:S(2)}) collective-permute-start(f32[80,128]{1,0:T(8,128)S(1)} %get-tuple-element.24), channel_id=1, source_target_pairs={{0,1},{1,0},{2,3},{3,2},{4,5},{5,4},{6,7},{7,6},{8,9},{9,8},{10,11... | collective-permute-start | bytes 122888 | tf_op jit(solution)/shard_map/ppermute | solution.py:28
  14.6 0.7 %collective-permute-start.2 = (f32[80,128]{1,0:T(8,128)S(1)}, f32[80,128]{1,0:T(8,128)S(1)}, u32[]{:S(2)}, u32[]{:S(2)}) collective-permute-start(f32[80,128]{1,0:T(8,128)S(1)} %get-tuple-element.25), channel_id=1, source_target_pairs={{1,2},{2,1},{5,6},{6,5},{9,10},{10,9},{13,14},{14,13},{17,18},{18,... | collective-permute-start | bytes 122888 | tf_op jit(solution)/shard_map/ppermute | solution.py:28
  15.2 1.5 %collective-permute-done.1.side_a = f32[80,128]{1,0:T(8,128)S(1)} collective-permute-done((f32[80,128]{1,0:T(8,128)S(1)}, f32[80,128]{1,0:T(8,128)S(1)}, u32[]{:S(2)}, u32[]{:S(2)}) %collective-permute-start.1) | collective-permute-done | bytes 40992 | tf_op jit(solution)/shard_map/ppermute | solution.py:28
  16.8 0.0 collective-permute-done.2.side_b
  16.8 7.0 %tangents.1 = (f32[8,128]{1,0:T(8,128)S(1)}, f32[10,8,1152]{2,1,0:T(8,128)S(1)}, f32[2,11,8,1152]{3,2,1,0:T(8,128)S(1)}, f32[2,2,10,8,1152]{4,3,2,1,0:T(8,128)S(...) custom-call(f32[2,3,64,1024]{3,2,1,0:T(8,128)S(1)} %copy-done, ...), custom_call_target="tpu_custom_call" | custom-call | tf_op jit(solution)/shard_map/tangents/pallas_call | solution.py:501
  23.8 0.1 collective-permute-start.3
  23.8 1.2 %gradient.2 = (f32[10,8,1152]{2,1,0:T(8,128)S(1)}, f32[10,8,1152]{2,1,0:T(8,128)S(1)}) custom-call(f32[10,8,1152]{2,1,0:T(8,128)S(1)} %get-tuple-element.26.m_c, f32[2,11,8,1152]{3,2,1,0:T(8,128)S(1)} %get-tuple-element.27.source, f32[2,2,10,8,1152]{4,3,2,1,0:T(8,128)S(1)} %get-tuple-element.28.a_x, f32[2,2,10,8,1152]{4,3,2,1,0:T(8,128)S(1)} %get-tuple-element.29.b_x, ...), custom_call_target="tpu_custom_call" | custom-call | flops 40000000 | bytes 12000000 | tf_op jit(solution)/shard_map/gradient/pallas_call | solution.py:533
  25.0 0.0 collective-permute-done.3
  25.0 1.8 %collective-permute-start.4 = (f32[8,128]{1,0:T(8,128)S(1)}, f32[8,128]{1,0:T(8,128)S(1)}, u32[]{:S(2)}, u32[]{:S(2)}) collective-permute-start(f32[8,128]{1,0:T(8,128)S(1)} %add.21), channel_id=1, source_target_pairs={{0,16},{8,24},{16,0},{24,8},{1,17},{9,25},{17,1},{25,9},{2,18},{10... | collective-permute-start | bytes 12296 | tf_op jit(solution)/shard_map/ppermute | solution.py:558
  26.8 1.5 %gradient.3 = f32[64,1024]{1,0:T(8,128)S(1)} custom-call(f32[10,8,1152]{2,1,0:T(8,128)S(1)} %get-tuple-element.26.m_c, f32[2,11,8,1152]{3,2,1,0:T(8,128)S(1)} %get-tuple-element.27.source, f32[2,2,10,8,1152]{4,3,2,1,0:T(8,128)S(1)} %get-tuple-element.28.a_x, f32[2,2,10,8,1152]{4,3,2,1,0:T(8,128)S(1)} %get-tuple-element.29.b_x, ...), custom_call_target="tpu_custom_call" | custom-call | flops 40000000 | bytes 12000000 | tf_op jit(solution)/shard_map/gradient/pallas_call | solution.py:533
  28.3 0.4 collective-permute-done.4
  28.7 0.0 collective-permute-start.5
  28.7 1.5 %collective-permute-done.5 = f32[64,1024]{1,0:T(8,128)S(1)} collective-permute-done((f32[64,1024]{1,0:T(8,128)S(1)}, f32[64,1024]{1,0:T(8,128)S(1)}, u32[]{:S(2)}, u32[]{:S(2)}) %collective-permute-start.5) | collective-permute-done | bytes 262176 | tf_op jit(solution)/shard_map/ppermute | solution.py:558
  30.3 1.8 %collective-permute-start.6 = (f32[64,1024]{1,0:T(8,128)S(1)}, f32[64,1024]{1,0:T(8,128)S(1)}, u32[]{:S(2)}, u32[]{:S(2)}) collective-permute-start(f32[64,1024]{1,0:T(8,128)S(1)} %add.23), channel_id=1, source_target_pairs={{0,16},{8,24},{16,0},{24,8},{1,17},{9,25},{17,1},{25,9},{2,18},{10... | collective-permute-start | bytes 786440 | tf_op jit(solution)/shard_map/ppermute | solution.py:558
  32.1 1.5 %collective-permute-start.7 = (f32[8,128]{1,0:T(8,128)S(1)}, f32[8,128]{1,0:T(8,128)S(1)}, u32[]{:S(2)}, u32[]{:S(2)}) collective-permute-start(f32[8,128]{1,0:T(8,128)S(1)} %add.22), channel_id=1, source_target_pairs={{0,4},{4,0},{1,5},{5,1},{2,6},{6,2},{3,7},{7,3},{8,12},{12,8},{9,1... | collective-permute-start | bytes 12296 | tf_op jit(solution)/shard_map/ppermute | solution.py:558
  33.6 2.1 %collective-permute-done.7 = f32[8,128]{1,0:T(8,128)S(1)} collective-permute-done((f32[8,128]{1,0:T(8,128)S(1)}, f32[8,128]{1,0:T(8,128)S(1)}, u32[]{:S(2)}, u32[]{:S(2)}) %collective-permute-start.7) | collective-permute-done | bytes 4128 | tf_op jit(solution)/shard_map/ppermute | solution.py:558
  35.7 4.6 %collective-permute-start.8 = (f32[8,128]{1,0:T(8,128)S(1)}, f32[8,128]{1,0:T(8,128)S(1)}, u32[]{:S(2)}, u32[]{:S(2)}) collective-permute-start(f32[8,128]{1,0:T(8,128)S(1)} %add.25), channel_id=1, source_target_pairs={{0,1},{1,0},{2,3},{3,2},{4,5},{5,4},{6,7},{7,6},{8,9},{9,8},{10,11... | collective-permute-start | bytes 12296 | tf_op jit(solution)/shard_map/ppermute | solution.py:558
  40.3 1.6 %collective-permute-done.8 = f32[8,128]{1,0:T(8,128)S(1)} collective-permute-done((f32[8,128]{1,0:T(8,128)S(1)}, f32[8,128]{1,0:T(8,128)S(1)}, u32[]{:S(2)}, u32[]{:S(2)}) %collective-permute-start.8) | collective-permute-done | bytes 4128 | tf_op jit(solution)/shard_map/ppermute | solution.py:558
  41.8 3.5 %collective-permute-start.9 = (f32[8,128]{1,0:T(8,128)S(1)}, f32[8,128]{1,0:T(8,128)S(1)}, u32[]{:S(2)}, u32[]{:S(2)}) collective-permute-start(f32[8,128]{1,0:T(8,128)S(1)} %add.26), channel_id=1, source_target_pairs={{0,2},{1,3},{2,0},{3,1},{4,6},{5,7},{6,4},{7,5},{8,10},{9,11},{10,... | collective-permute-start | bytes 12296 | tf_op jit(solution)/shard_map/ppermute | solution.py:558
  45.3 1.6 %collective-permute-done.9 = f32[8,128]{1,0:T(8,128)S(1)} collective-permute-done((f32[8,128]{1,0:T(8,128)S(1)}, f32[8,128]{1,0:T(8,128)S(1)}, u32[]{:S(2)}, u32[]{:S(2)}) %collective-permute-start.9) | collective-permute-done | bytes 4128 | tf_op jit(solution)/shard_map/ppermute | solution.py:558
  46.9 0.6 %add_reduce_fusion = f32[]{:T(128)} fusion(f32[8,128]{1,0:T(8,128)S(1)} %add.26, f32[8,128]{1,0:T(8,128)S(1)} %collective-permute-done.9), kind=kLoop, calls=%fused_computation | loop fusion | flops 2047 | bytes 8196 | tf_op jit(solution)/shard_map/reduce_sum | solution.py:587
  47.5 0.0 collective-permute-done.6
  47.5 0.7 %add.24 = f32[64,1024]{1,0:T(8,128)} add(f32[64,1024]{1,0:T(8,128)S(1)} %add.23, f32[64,1024]{1,0:T(8,128)S(1)} %collective-permute-done.6) | non-fusion elementwise | flops 65536 | bytes 786432 | tf_op jit(solution)/shard_map/add | solution.py:558
  (5 shorter events, 0.0 us)
Async XLA Ops:
  0.6 5.0 %copy-start.5 = (s32[2,1,1,1024]{3,2,1,0:T(1,128)S(1)}, s32[2,1,1,1024]{3,2,1,0:T(1,128)}, u32[]{:S(2)}) copy-start(s32[2,1,1,1024]{3,2,1,0:T(1,128)} %param.11) | copy-start | bytes 24580
  0.6 11.5 %copy-start = (f32[2,3,64,1024]{3,2,1,0:T(8,128)S(1)}, f32[2,3,64,1024]{3,2,1,0:T(8,128)}, u32[]{:S(2)}) copy-start(f32[2,3,64,1024]{3,2,1,0:T(8,128)} %depth.1) | copy-start | bytes 4718596
  0.7 11.5 %copy-start.1 = (s32[2,64,1024]{2,1,0:T(8,128)S(1)}, s32[2,64,1024]{2,1,0:T(8,128)}, u32[]{:S(2)}) copy-start(s32[2,64,1024]{2,1,0:T(8,128)} %wet.1) | copy-start | bytes 1572868
  0.7 11.5 %copy-start.2 = (f32[64,1024]{1,0:T(8,128)S(1)}, f32[64,1024]{1,0:T(8,128)}, u32[]{:S(2)}) copy-start(f32[64,1024]{1,0:T(8,128)} %bed.1) | copy-start | bytes 786436
  0.7 11.5 %copy-start.3 = (f32[64,1024]{1,0:T(8,128)S(1)}, f32[64,1024]{1,0:T(8,128)}, u32[]{:S(2)}) copy-start(f32[64,1024]{1,0:T(8,128)} %rough.1) | copy-start | bytes 786436
  0.7 11.5 %copy-start.4 = (f32[64,1024]{1,0:T(8,128)S(1)}, f32[64,1024]{1,0:T(8,128)}, u32[]{:S(2)}) copy-start(f32[64,1024]{1,0:T(8,128)} %direction.1) | copy-start | bytes 786436
  2.6 9.5 %collective-permute-start = (f32[64,1024]{1,0:T(8,128)}, f32[64,1024]{1,0:T(8,128)S(1)}, u32[]{:S(2)}, u32[]{:S(2)}) collective-permute-start(f32[64,1024]{1,0:T(8,128)} %edge_rows.1), channel_id=1, source_target_pairs={{0,4},{4,0},{1,5},{5,1},{2,6},{6,2},{3,7},{7,3},{8,12},{12,8},{9,1... | collective-permute-start | bytes 786440 | tf_op jit(solution)/shard_map/ppermute | solution.py:28
  12.7 4.0 %collective-permute-start.1 = (f32[80,128]{1,0:T(8,128)S(1)}, f32[80,128]{1,0:T(8,128)S(1)}, u32[]{:S(2)}, u32[]{:S(2)}) collective-permute-start(f32[80,128]{1,0:T(8,128)S(1)} %get-tuple-element.24), channel_id=1, source_target_pairs={{0,1},{1,0},{2,3},{3,2},{4,5},{5,4},{6,7},{7,6},{8,9},{9,8},{10,11... | collective-permute-start | bytes 122888 | tf_op jit(solution)/shard_map/ppermute | solution.py:28
  14.6 2.2 %collective-permute-start.2 = (f32[80,128]{1,0:T(8,128)S(1)}, f32[80,128]{1,0:T(8,128)S(1)}, u32[]{:S(2)}, u32[]{:S(2)}) collective-permute-start(f32[80,128]{1,0:T(8,128)S(1)} %get-tuple-element.25), channel_id=1, source_target_pairs={{1,2},{2,1},{5,6},{6,5},{9,10},{10,9},{13,14},{14,13},{17,18},{18,... | collective-permute-start | bytes 122888 | tf_op jit(solution)/shard_map/ppermute | solution.py:28
  23.8 1.2 %collective-permute-start.3 = (f32[8,128]{1,0:T(8,128)S(1)}, f32[8,128]{1,0:T(8,128)S(1)}, u32[]{:S(2)}, u32[]{:S(2)}) collective-permute-start(f32[8,128]{1,0:T(8,128)S(1)} %get-tuple-element.36), channel_id=1, source_target_pairs={{0,8},{8,0},{16,24},{24,16},{1,9},{9,1},{17,25},{25,17},{2,10},{10... | collective-permute-start | bytes 12296 | tf_op jit(solution)/shard_map/ppermute | solution.py:558
  25.0 3.7 %collective-permute-start.4 = (f32[8,128]{1,0:T(8,128)S(1)}, f32[8,128]{1,0:T(8,128)S(1)}, u32[]{:S(2)}, u32[]{:S(2)}) collective-permute-start(f32[8,128]{1,0:T(8,128)S(1)} %add.21), channel_id=1, source_target_pairs={{0,16},{8,24},{16,0},{24,8},{1,17},{9,25},{17,1},{25,9},{2,18},{10... | collective-permute-start | bytes 12296 | tf_op jit(solution)/shard_map/ppermute | solution.py:558
  28.7 1.5 %collective-permute-start.5 = (f32[64,1024]{1,0:T(8,128)S(1)}, f32[64,1024]{1,0:T(8,128)S(1)}, u32[]{:S(2)}, u32[]{:S(2)}) collective-permute-start(f32[64,1024]{1,0:T(8,128)S(1)} %gradient.3), channel_id=1, source_target_pairs={{0,8},{8,0},{16,24},{24,16},{1,9},{9,1},{17,25},{25,17},{2,10},{10... | collective-permute-start | bytes 786440 | tf_op jit(solution)/shard_map/ppermute | solution.py:558
  30.3 17.2 %collective-permute-start.6 = (f32[64,1024]{1,0:T(8,128)S(1)}, f32[64,1024]{1,0:T(8,128)S(1)}, u32[]{:S(2)}, u32[]{:S(2)}) collective-permute-start(f32[64,1024]{1,0:T(8,128)S(1)} %add.23), channel_id=1, source_target_pairs={{0,16},{8,24},{16,0},{24,8},{1,17},{9,25},{17,1},{25,9},{2,18},{10... | collective-permute-start | bytes 786440 | tf_op jit(solution)/shard_map/ppermute | solution.py:558
  32.1 3.6 %collective-permute-start.7 = (f32[8,128]{1,0:T(8,128)S(1)}, f32[8,128]{1,0:T(8,128)S(1)}, u32[]{:S(2)}, u32[]{:S(2)}) collective-permute-start(f32[8,128]{1,0:T(8,128)S(1)} %add.22), channel_id=1, source_target_pairs={{0,4},{4,0},{1,5},{5,1},{2,6},{6,2},{3,7},{7,3},{8,12},{12,8},{9,1... | collective-permute-start | bytes 12296 | tf_op jit(solution)/shard_map/ppermute | solution.py:558
  35.7 6.2 %collective-permute-start.8 = (f32[8,128]{1,0:T(8,128)S(1)}, f32[8,128]{1,0:T(8,128)S(1)}, u32[]{:S(2)}, u32[]{:S(2)}) collective-permute-start(f32[8,128]{1,0:T(8,128)S(1)} %add.25), channel_id=1, source_target_pairs={{0,1},{1,0},{2,3},{3,2},{4,5},{5,4},{6,7},{7,6},{8,9},{9,8},{10,11... | collective-permute-start | bytes 12296 | tf_op jit(solution)/shard_map/ppermute | solution.py:558
  41.8 5.1 %collective-permute-start.9 = (f32[8,128]{1,0:T(8,128)S(1)}, f32[8,128]{1,0:T(8,128)S(1)}, u32[]{:S(2)}, u32[]{:S(2)}) collective-permute-start(f32[8,128]{1,0:T(8,128)S(1)} %add.26), channel_id=1, source_target_pairs={{0,2},{1,3},{2,0},{3,1},{4,6},{5,7},{6,4},{7,5},{8,10},{9,11},{10,... | collective-permute-start | bytes 12296 | tf_op jit(solution)/shard_map/ppermute | solution.py:558

commit v3 on v2

--- a/solution.py
+++ b/solution.py
@@ -138,7 +138,7 @@
 
 def column_kernel(sides, *refs):
     rims_in, own = refs[:sides], (refs[sides : sides + 6], refs[sides + 6 : sides + 12])
-    rim_top, rim_bottom, pay_a, pay_b = refs[sides + 12 :]
+    rim_top, rim_bottom, pay_b, pay_a = refs[sides + 12 :]
     events, steps, rows, _ = own[0][0].shape
     cols = rim_top.shape[-1]
     even_row = lax.axis_index("row") % 2 == 0
@@ -268,7 +268,7 @@
 
 
 def tangent_kernel(
-    depth, wet, bed, rough, direction, counts, rim_top, rim_bottom, side_a, side_b,
+    depth, wet, bed, rough, direction, counts, rim_top, rim_bottom, side_b, side_a,
     curve_ref, m_c, source, a_x, b_x, c_x, a_y, b_y, c_y,
     nat, hx, sb_x, sb_y, q_x, q_y, inv_x, inv_y, cond_x, cond_y, cnt,
     tan_a, tan_b, flow, tmp,
@@ -488,7 +488,7 @@
             grad_ref[:, J[j]] = nat[j, SUB : SUB + rows, :]
 
 
-def tangents(depth, wet, bed, rough, direction, counts, rim_top, rim_bottom, side_a, side_b):
+def tangents(depth, wet, bed, rough, direction, counts, rim_top, rim_bottom, side_b, side_a):
     events, steps, rows, cols = depth.shape
     tall, wide = rows + 2 * SUB, cols + LANES
     deep = tall // SUB
@@ -518,7 +518,7 @@
         ],
         compiler_params=pltpu.CompilerParams(vmem_limit_bytes=20 * 1024 * 1024),
         name="tangents",
-    )(depth, wet, bed, rough, direction, counts, rim_top, rim_bottom, side_a, side_b)
+    )(depth, wet, bed, rough, direction, counts, rim_top, rim_bottom, side_b, side_a)
 
 
 def gradient(e, rows, cols, sums, m_c, source, *coefficients):
@@ -554,8 +554,30 @@
     return out
 
 
+def from_hop(x, axis, hop):
+    return lax.ppermute(x, axis, [(i, i ^ hop) for i in range(lax.axis_size(axis))])
+
+
 def hop_sum(x, axis, hop):
-    return x + lax.ppermute(x, axis, [(i, i ^ hop) for i in range(lax.axis_size(axis))])
+    return x + from_hop(x, axis, hop)
+
+
+def finish_kernel(grad, arrived, curve, curve_arrived, hess, total):
+    hess[...] = grad[...] + arrived[...]
+    total[...] = jnp.sum(curve[...] + curve_arrived[...], keepdims=True)
+
+
+def finish(grad, arrived, curve, curve_arrived):
+    vmem = pl.BlockSpec(memory_space=pltpu.VMEM)
+    hess, total = pl.pallas_call(
+        finish_kernel,
+        in_specs=[vmem] * 4,
+        out_specs=[vmem] * 2,
+        out_shape=[jax.ShapeDtypeStruct(grad.shape, grad.dtype), jax.ShapeDtypeStruct((1, 1), curve.dtype)],
+        compiler_params=pltpu.CompilerParams(vmem_limit_bytes=4 * 1024 * 1024),
+        name="finish",
+    )(grad, arrived, curve, curve_arrived)
+    return (hess, total.reshape(()))
 
 
 def local(depth, wet, bed, rough, direction, gauge_cells):
@@ -564,13 +586,13 @@
     pays = edge_rows(cells, depth, wet, bed, rough, direction)
     rims = [exchange(x, "row", k) for k, x in enumerate(pays)]
     counts = gauges(cells, rows, cols)
-    rim_top, rim_bottom, send_a, send_b = rims_and_columns(
+    rim_top, rim_bottom, send_b, send_a = rims_and_columns(
         rims, depth, wet, bed, rough, direction, counts
     )
     side_b = exchange(send_b, "col", 1)
     side_a = exchange(send_a, "col", 0)
     curve, *coefficients = tangents(
-        depth, wet, bed, rough, direction, counts, rim_top, rim_bottom, side_a, side_b
+        depth, wet, bed, rough, direction, counts, rim_top, rim_bottom, side_b, side_a
     )
     hops = hops_over("event") + hops_over("row") + hops_over("col")
     sums = ()
@@ -579,12 +601,17 @@
         if hops:
             curve = hop_sum(curve, *hops.pop(0))
             sums, curve = lax.optimization_barrier((sums, curve))
-    grad = sums
+    grad, arrived = sums, None
     for axis, hop in hops_over("event"):
-        grad = hop_sum(grad, axis, hop)
-    for axis, hop in hops:
-        curve = hop_sum(curve, axis, hop)
-    return (grad, jnp.sum(curve))
+        if arrived is not None:
+            grad = grad + arrived
+            if hops:
+                curve = hop_sum(curve, *hops.pop(0))
+                grad, curve = lax.optimization_barrier((grad, curve))
+        arrived = from_hop(grad, axis, hop)
+    while len(hops) > 1:
+        curve = hop_sum(curve, *hops.pop(0))
+    return finish(grad, arrived, curve, from_hop(curve, *hops[0]))
 
 
 def solution(mesh):

time: 48.4 us -> 46.2 us (0.955)
  starting transfers between devices: 18.7 us -> 17 us
  other arithmetic: 1.37 us -> 0.04 us
  Pallas kernels: 12.6 us -> 13.3 us
    ppermute x7, starting transfers between devices: 13.2 us -> 8.63 us  [from_hop(): lax.ppermute(x, axis, [(i, i ^ hop) for i in range(lax.axis_size(axis))])]
    ppermute x3, starting transfers between devices: 5.5 us -> 8.37 us  [exchange(): return lax.ppermute(x, axis, perm) if perm else None]
    pallas_call x0 -> x1, Pallas kernels: none -> 0.73 us  [finish(): pl.pallas_call(finish_kernel, in_specs=[vmem] * 4, out_specs=[vmem] * 2,...]
    add x6 -> x5, other arithmetic: 0.78 us -> 0.04 us  [the longest x1 0.03 us: local(): grad = grad + arrived]
    reduce_sum x1 -> x0, other arithmetic: 0.6 us -> none  [local(): return (grad, jnp.sum(curve))]
  transfers between devices with their start and end apart: 10 -> 10, of which waited for: 7 -> 6; matrix products, arithmetic and copies ran while one was open for 1% -> 0% of each run, Pallas kernels for 7% -> 7%
where the time goes in v3:
time: 46.2 us; the launch traced here: 46.1 us
  starting transfers between devices  17 us (37%)
  waiting for transfers between devices  14.9 us (32%)
  Pallas kernels  13.3 us (29%)
  between operations  0.78 us (2%)
    ppermute x7, starting transfers between devices, from_hop(): lax.ppermute(x, axis, [(i, i ^ hop) for i in range(lax.axis_size(axis))])  8.63 us
    ppermute x3, starting transfers between devices, exchange(): return lax.ppermute(x, axis, perm) if perm else None  8.37 us
    ppermute x3, waiting for transfers between devices, exchange(): return lax.ppermute(x, axis, perm) if perm else None  8 us
    pallas_call x1, Pallas kernels, tangents(): pl.pallas_call(tangent_kernel, in_specs=[vmem] * 10, out_specs=[vmem] * 9...  6.98 us
    ppermute x7, waiting for transfers between devices, from_hop(): lax.ppermute(x, axis, [(i, i ^ hop) for i in range(lax.axis_size(axis))])  6.88 us
    pallas_call x2, Pallas kernels, gradient(): pl.pallas_call(functools.partial(adjoint_kernel, first, last), grid=(1,),...  2.67 us
    pallas_call x1, Pallas kernels, edge_rows(): pl.pallas_call(functools.partial(rows_kernel, sides), in_specs=[anywhere]...  1.92 us
  transfers between devices with their start and end apart: 10, of which 6 were waited for; matrix products, arithmetic and copies ran while one was open for 0% of the time, Pallas kernels for 7%

profile of v3, /device:TPU:0, one launch (start us, length us, event | category | flops | bytes accessed | tf_op | source)
XLA Modules:
  0.0 46.1 jit_solution(13744523331577605577)
XLA Ops:
  0.6 0.0 copy-start.5
  0.6 0.0 copy-start
  0.7 0.0 copy-start.1
  0.7 0.0 copy-start.2
  0.7 0.0 copy-start.3
  0.7 0.0 copy-start.4
  0.7 1.9 %edge_rows.1 = f32[64,1024]{1,0:T(8,128)} custom-call(s32[2,1,1024]{2,1,0:T(1,128)} %bitcast.2, f32[2,3,64,1024]{3,2,1,0:T(8,128)} %depth.1, s32[2,64,1024]{2,1,0:T(8,128)} %wet.1, f32[64,1024]{1,0:T(8,128)} %bed.1, f32[64,1024]{1,0:T(8,128)} %rough.1, f32[64,1024]{1,0:T(8,128)} %direction.1), custom_call_target="tpu_custom_call" | custom-call | tf_op jit(solution)/shard_map/edge_rows/pallas_call | solution.py:106
  2.6 3.0 %collective-permute-start = (f32[64,1024]{1,0:T(8,128)}, f32[64,1024]{1,0:T(8,128)S(1)}, u32[]{:S(2)}, u32[]{:S(2)}) collective-permute-start(f32[64,1024]{1,0:T(8,128)} %edge_rows.1), channel_id=1, source_target_pairs={{0,4},{4,0},{1,5},{5,1},{2,6},{6,2},{3,7},{7,3},{8,12},{12,8},{9,1... | collective-permute-start | bytes 786440 | tf_op jit(solution)/shard_map/ppermute | solution.py:28
  5.7 0.0 copy-done.5
  5.7 0.5 %gauges.1.refs_6_.refs_12_.counts = f32[2,64,1024]{2,1,0:T(8,128)S(1)} custom-call(s32[2,1,1024]{2,1,0:T(1,128)S(1)} %bitcast.3), custom_call_target="tpu_custom_call" | custom-call | flops 20000000 | bytes 4000000 | tf_op jit(solution)/shard_map/gauges/pallas_call | solution.py:128
  6.2 6.0 %collective-permute-done.refs_0_ = f32[64,1024]{1,0:T(8,128)S(1)} collective-permute-done((f32[64,1024]{1,0:T(8,128)}, f32[64,1024]{1,0:T(8,128)S(1)}, u32[]{:S(2)}, u32[]{:S(2)}) %collective-permute-start) | collective-permute-done | bytes 262176 | tf_op jit(solution)/shard_map/ppermute | solution.py:28
  12.2 0.0 copy-done
  12.2 0.0 copy-done.1
  12.2 0.0 copy-done.2
  12.2 0.0 copy-done.3
  12.2 0.0 copy-done.4
  12.2 0.5 %rims_and_columns.1 = (f32[13,8,1024]{2,1,0:T(8,128)S(1)}, f32[13,8,1024]{2,1,0:T(8,128)S(1)}, f32[80,128]{1,0:T(8,128)S(1)}, f32[80,128]{1,0:T(8,128)S(1)}) custom-call(f32[64,1024]{1,0:T(8,128)S(1)} %collective-permute-done.refs_0_, f32[2,3,64,1024]{3,2,1,0:T(8,128)S(1)} %copy-done, s32[2,64,1024]{2,1,0:T(8,128)S(1)} %copy-done.1, ...), custom_call_target="tpu_custom_call" | custom-call | tf_op jit(solution)/shard_map/rims_and_columns/pallas_call | solution.py:221
  12.7 0.7 %collective-permute-start.1 = (f32[80,128]{1,0:T(8,128)S(1)}, f32[80,128]{1,0:T(8,128)S(1)}, u32[]{:S(2)}, u32[]{:S(2)}) collective-permute-start(f32[80,128]{1,0:T(8,128)S(1)} %get-tuple-element.28), channel_id=1, source_target_pairs={{1,2},{2,1},{5,6},{6,5},{9,10},{10,9},{13,14},{14,13},{17,18},{18,... | collective-permute-start | bytes 122888 | tf_op jit(solution)/shard_map/ppermute | solution.py:28
  13.4 4.7 %collective-permute-start.2 = (f32[80,128]{1,0:T(8,128)S(1)}, f32[80,128]{1,0:T(8,128)S(1)}, u32[]{:S(2)}, u32[]{:S(2)}) collective-permute-start(f32[80,128]{1,0:T(8,128)S(1)} %get-tuple-element.29), channel_id=1, source_target_pairs={{0,1},{1,0},{2,3},{3,2},{4,5},{5,4},{6,7},{7,6},{8,9},{9,8},{10,11... | collective-permute-start | bytes 122888 | tf_op jit(solution)/shard_map/ppermute | solution.py:28
  18.1 0.0 collective-permute-done.1.side_b
  18.1 2.0 %collective-permute-done.2.side_a = f32[80,128]{1,0:T(8,128)S(1)} collective-permute-done((f32[80,128]{1,0:T(8,128)S(1)}, f32[80,128]{1,0:T(8,128)S(1)}, u32[]{:S(2)}, u32[]{:S(2)}) %collective-permute-start.2) | collective-permute-done | bytes 40992 | tf_op jit(solution)/shard_map/ppermute | solution.py:28
  20.1 7.0 %tangents.1 = (f32[8,128]{1,0:T(8,128)S(1)}, f32[10,8,1152]{2,1,0:T(8,128)S(1)}, f32[2,11,8,1152]{3,2,1,0:T(8,128)S(1)}, f32[2,2,10,8,1152]{4,3,2,1,0:T(8,128)S(...) custom-call(f32[2,3,64,1024]{3,2,1,0:T(8,128)S(1)} %copy-done, ...), custom_call_target="tpu_custom_call" | custom-call | tf_op jit(solution)/shard_map/tangents/pallas_call | solution.py:501
  27.1 0.1 collective-permute-start.3
  27.1 1.2 %gradient.2 = (f32[10,8,1152]{2,1,0:T(8,128)S(1)}, f32[10,8,1152]{2,1,0:T(8,128)S(1)}) custom-call(f32[10,8,1152]{2,1,0:T(8,128)S(1)} %get-tuple-element.30.m_c, f32[2,11,8,1152]{3,2,1,0:T(8,128)S(1)} %get-tuple-element.31.source, f32[2,2,10,8,1152]{4,3,2,1,0:T(8,128)S(1)} %get-tuple-element.32.a_x, f32[2,2,10,8,1152]{4,3,2,1,0:T(8,128)S(1)} %get-tuple-element.33.b_x, ...), custom_call_target="tpu_custom_call" | custom-call | flops 40000000 | bytes 12000000 | tf_op jit(solution)/shard_map/gradient/pallas_call | solution.py:533
  28.3 0.0 collective-permute-done.3
  28.3 1.6 %collective-permute-start.4 = (f32[8,128]{1,0:T(8,128)S(1)}, f32[8,128]{1,0:T(8,128)S(1)}, u32[]{:S(2)}, u32[]{:S(2)}) collective-permute-start(f32[8,128]{1,0:T(8,128)S(1)} %add.15), channel_id=1, source_target_pairs={{0,16},{8,24},{16,0},{24,8},{1,17},{9,25},{17,1},{25,9},{2,18},{10... | collective-permute-start | bytes 12296 | tf_op jit(solution)/shard_map/ppermute | solution.py:558
  29.9 1.5 %gradient.3 = f32[64,1024]{1,0:T(8,128)S(1)} custom-call(f32[10,8,1152]{2,1,0:T(8,128)S(1)} %get-tuple-element.30.m_c, f32[2,11,8,1152]{3,2,1,0:T(8,128)S(1)} %get-tuple-element.31.source, f32[2,2,10,8,1152]{4,3,2,1,0:T(8,128)S(1)} %get-tuple-element.32.a_x, f32[2,2,10,8,1152]{4,3,2,1,0:T(8,128)S(1)} %get-tuple-element.33.b_x, ...), custom_call_target="tpu_custom_call" | custom-call | flops 40000000 | bytes 12000000 | tf_op jit(solution)/shard_map/gradient/pallas_call | solution.py:533
  31.4 0.6 %collective-permute-done.4 = f32[8,128]{1,0:T(8,128)S(1)} collective-permute-done((f32[8,128]{1,0:T(8,128)S(1)}, f32[8,128]{1,0:T(8,128)S(1)}, u32[]{:S(2)}, u32[]{:S(2)}) %collective-permute-start.4) | collective-permute-done | bytes 4128 | tf_op jit(solution)/shard_map/ppermute | solution.py:558
  32.0 0.0 collective-permute-start.5
  32.0 1.5 %collective-permute-start.6 = (f32[8,128]{1,0:T(8,128)S(1)}, f32[8,128]{1,0:T(8,128)S(1)}, u32[]{:S(2)}, u32[]{:S(2)}) collective-permute-start(f32[8,128]{1,0:T(8,128)S(1)} %add.16), channel_id=1, source_target_pairs={{0,4},{4,0},{1,5},{5,1},{2,6},{6,2},{3,7},{7,3},{8,12},{12,8},{9,1... | collective-permute-start | bytes 12296 | tf_op jit(solution)/shard_map/ppermute | solution.py:558
  33.5 2.1 %collective-permute-done.6 = f32[8,128]{1,0:T(8,128)S(1)} collective-permute-done((f32[8,128]{1,0:T(8,128)S(1)}, f32[8,128]{1,0:T(8,128)S(1)}, u32[]{:S(2)}, u32[]{:S(2)}) %collective-permute-start.6) | collective-permute-done | bytes 4128 | tf_op jit(solution)/shard_map/ppermute | solution.py:558
  35.6 0.0 collective-permute-done.5
  35.7 1.6 %collective-permute-start.7 = (f32[64,1024]{1,0:T(8,128)S(1)}, f32[64,1024]{1,0:T(8,128)S(1)}, u32[]{:S(2)}, u32[]{:S(2)}) collective-permute-start(f32[64,1024]{1,0:T(8,128)S(1)} %add.17.grad), channel_id=1, source_target_pairs={{0,16},{8,24},{16,0},{24,8},{1,17},{9,25},{17,1},{25,9},{2,18},{10... | collective-permute-start | bytes 786440 | tf_op jit(solution)/shard_map/ppermute | solution.py:558
  37.2 2.0 %collective-permute-start.8 = (f32[8,128]{1,0:T(8,128)S(1)}, f32[8,128]{1,0:T(8,128)S(1)}, u32[]{:S(2)}, u32[]{:S(2)}) collective-permute-start(f32[8,128]{1,0:T(8,128)S(1)} %add.18), channel_id=1, source_target_pairs={{0,1},{1,0},{2,3},{3,2},{4,5},{5,4},{6,7},{7,6},{8,9},{9,8},{10,11... | collective-permute-start | bytes 12296 | tf_op jit(solution)/shard_map/ppermute | solution.py:558
  39.2 1.6 %collective-permute-done.8 = f32[8,128]{1,0:T(8,128)S(1)} collective-permute-done((f32[8,128]{1,0:T(8,128)S(1)}, f32[8,128]{1,0:T(8,128)S(1)}, u32[]{:S(2)}, u32[]{:S(2)}) %collective-permute-start.8) | collective-permute-done | bytes 4128 | tf_op jit(solution)/shard_map/ppermute | solution.py:558
  40.8 1.9 %collective-permute-start.9 = (f32[8,128]{1,0:T(8,128)S(1)}, f32[8,128]{1,0:T(8,128)S(1)}, u32[]{:S(2)}, u32[]{:S(2)}) collective-permute-start(f32[8,128]{1,0:T(8,128)S(1)} %add.19.curve), channel_id=1, source_target_pairs={{0,2},{1,3},{2,0},{3,1},{4,6},{5,7},{6,4},{7,5},{8,10},{9,11},{10,... | collective-permute-start | bytes 12296 | tf_op jit(solution)/shard_map/ppermute | solution.py:558
  42.7 2.6 %collective-permute-done.9.curve_arrived = f32[8,128]{1,0:T(8,128)S(1)} collective-permute-done((f32[8,128]{1,0:T(8,128)S(1)}, f32[8,128]{1,0:T(8,128)S(1)}, u32[]{:S(2)}, u32[]{:S(2)}) %collective-permute-start.9) | collective-permute-done | bytes 4128 | tf_op jit(solution)/shard_map/ppermute | solution.py:558
  45.3 0.0 collective-permute-done.7.arrived
  45.3 0.7 %finish.1 = (f32[64,1024]{1,0:T(8,128)}, f32[1,1]{1,0:T(1,128)}) custom-call(f32[64,1024]{1,0:T(8,128)S(1)} %add.17.grad, f32[64,1024]{1,0:T(8,128)S(1)} %collective-permute-done.7.arrived, f32[8,128]{1,0:T(8,128)S(1)} %add.19.curve, f32[8,128]{1,0:T(8,128)S(1)} %collective-permute-done.9.curve_arrived), custom_call_target="tpu_custom_call" | custom-call | tf_op jit(solution)/shard_map/finish/pallas_call | solution.py:572
  (5 shorter events, 0.0 us)
Async XLA Ops:
  0.6 5.0 %copy-start.5 = (s32[2,1,1,1024]{3,2,1,0:T(1,128)S(1)}, s32[2,1,1,1024]{3,2,1,0:T(1,128)}, u32[]{:S(2)}) copy-start(s32[2,1,1,1024]{3,2,1,0:T(1,128)} %param.11) | copy-start | bytes 24580
  0.6 11.5 %copy-start = (f32[2,3,64,1024]{3,2,1,0:T(8,128)S(1)}, f32[2,3,64,1024]{3,2,1,0:T(8,128)}, u32[]{:S(2)}) copy-start(f32[2,3,64,1024]{3,2,1,0:T(8,128)} %depth.1) | copy-start | bytes 4718596
  0.7 11.5 %copy-start.1 = (s32[2,64,1024]{2,1,0:T(8,128)S(1)}, s32[2,64,1024]{2,1,0:T(8,128)}, u32[]{:S(2)}) copy-start(s32[2,64,1024]{2,1,0:T(8,128)} %wet.1) | copy-start | bytes 1572868
  0.7 11.5 %copy-start.2 = (f32[64,1024]{1,0:T(8,128)S(1)}, f32[64,1024]{1,0:T(8,128)}, u32[]{:S(2)}) copy-start(f32[64,1024]{1,0:T(8,128)} %bed.1) | copy-start | bytes 786436
  0.7 11.5 %copy-start.3 = (f32[64,1024]{1,0:T(8,128)S(1)}, f32[64,1024]{1,0:T(8,128)}, u32[]{:S(2)}) copy-start(f32[64,1024]{1,0:T(8,128)} %rough.1) | copy-start | bytes 786436
  0.7 11.5 %copy-start.4 = (f32[64,1024]{1,0:T(8,128)S(1)}, f32[64,1024]{1,0:T(8,128)}, u32[]{:S(2)}) copy-start(f32[64,1024]{1,0:T(8,128)} %direction.1) | copy-start | bytes 786436
  2.6 9.5 %collective-permute-start = (f32[64,1024]{1,0:T(8,128)}, f32[64,1024]{1,0:T(8,128)S(1)}, u32[]{:S(2)}, u32[]{:S(2)}) collective-permute-start(f32[64,1024]{1,0:T(8,128)} %edge_rows.1), channel_id=1, source_target_pairs={{0,4},{4,0},{1,5},{5,1},{2,6},{6,2},{3,7},{7,3},{8,12},{12,8},{9,1... | collective-permute-start | bytes 786440 | tf_op jit(solution)/shard_map/ppermute | solution.py:28
  12.7 5.4 %collective-permute-start.1 = (f32[80,128]{1,0:T(8,128)S(1)}, f32[80,128]{1,0:T(8,128)S(1)}, u32[]{:S(2)}, u32[]{:S(2)}) collective-permute-start(f32[80,128]{1,0:T(8,128)S(1)} %get-tuple-element.28), channel_id=1, source_target_pairs={{1,2},{2,1},{5,6},{6,5},{9,10},{10,9},{13,14},{14,13},{17,18},{18,... | collective-permute-start | bytes 122888 | tf_op jit(solution)/shard_map/ppermute | solution.py:28
  13.4 6.7 %collective-permute-start.2 = (f32[80,128]{1,0:T(8,128)S(1)}, f32[80,128]{1,0:T(8,128)S(1)}, u32[]{:S(2)}, u32[]{:S(2)}) collective-permute-start(f32[80,128]{1,0:T(8,128)S(1)} %get-tuple-element.29), channel_id=1, source_target_pairs={{0,1},{1,0},{2,3},{3,2},{4,5},{5,4},{6,7},{7,6},{8,9},{9,8},{10,11... | collective-permute-start | bytes 122888 | tf_op jit(solution)/shard_map/ppermute | solution.py:28
  27.1 1.2 %collective-permute-start.3 = (f32[8,128]{1,0:T(8,128)S(1)}, f32[8,128]{1,0:T(8,128)S(1)}, u32[]{:S(2)}, u32[]{:S(2)}) collective-permute-start(f32[8,128]{1,0:T(8,128)S(1)} %get-tuple-element.40), channel_id=1, source_target_pairs={{0,8},{8,0},{16,24},{24,16},{1,9},{9,1},{17,25},{25,17},{2,10},{10... | collective-permute-start | bytes 12296 | tf_op jit(solution)/shard_map/ppermute | solution.py:558
  28.3 3.7 %collective-permute-start.4 = (f32[8,128]{1,0:T(8,128)S(1)}, f32[8,128]{1,0:T(8,128)S(1)}, u32[]{:S(2)}, u32[]{:S(2)}) collective-permute-start(f32[8,128]{1,0:T(8,128)S(1)} %add.15), channel_id=1, source_target_pairs={{0,16},{8,24},{16,0},{24,8},{1,17},{9,25},{17,1},{25,9},{2,18},{10... | collective-permute-start | bytes 12296 | tf_op jit(solution)/shard_map/ppermute | solution.py:558
  32.0 3.6 %collective-permute-start.5 = (f32[64,1024]{1,0:T(8,128)S(1)}, f32[64,1024]{1,0:T(8,128)S(1)}, u32[]{:S(2)}, u32[]{:S(2)}) collective-permute-start(f32[64,1024]{1,0:T(8,128)S(1)} %gradient.3), channel_id=1, source_target_pairs={{0,8},{8,0},{16,24},{24,16},{1,9},{9,1},{17,25},{25,17},{2,10},{10... | collective-permute-start | bytes 786440 | tf_op jit(solution)/shard_map/ppermute | solution.py:558
  32.0 3.6 %collective-permute-start.6 = (f32[8,128]{1,0:T(8,128)S(1)}, f32[8,128]{1,0:T(8,128)S(1)}, u32[]{:S(2)}, u32[]{:S(2)}) collective-permute-start(f32[8,128]{1,0:T(8,128)S(1)} %add.16), channel_id=1, source_target_pairs={{0,4},{4,0},{1,5},{5,1},{2,6},{6,2},{3,7},{7,3},{8,12},{12,8},{9,1... | collective-permute-start | bytes 12296 | tf_op jit(solution)/shard_map/ppermute | solution.py:558
  35.7 9.7 %collective-permute-start.7 = (f32[64,1024]{1,0:T(8,128)S(1)}, f32[64,1024]{1,0:T(8,128)S(1)}, u32[]{:S(2)}, u32[]{:S(2)}) collective-permute-start(f32[64,1024]{1,0:T(8,128)S(1)} %add.17.grad), channel_id=1, source_target_pairs={{0,16},{8,24},{16,0},{24,8},{1,17},{9,25},{17,1},{25,9},{2,18},{10... | collective-permute-start | bytes 786440 | tf_op jit(solution)/shard_map/ppermute | solution.py:558
  37.2 3.6 %collective-permute-start.8 = (f32[8,128]{1,0:T(8,128)S(1)}, f32[8,128]{1,0:T(8,128)S(1)}, u32[]{:S(2)}, u32[]{:S(2)}) collective-permute-start(f32[8,128]{1,0:T(8,128)S(1)} %add.18), channel_id=1, source_target_pairs={{0,1},{1,0},{2,3},{3,2},{4,5},{5,4},{6,7},{7,6},{8,9},{9,8},{10,11... | collective-permute-start | bytes 12296 | tf_op jit(solution)/shard_map/ppermute | solution.py:558
  40.8 4.5 %collective-permute-start.9 = (f32[8,128]{1,0:T(8,128)S(1)}, f32[8,128]{1,0:T(8,128)S(1)}, u32[]{:S(2)}, u32[]{:S(2)}) collective-permute-start(f32[8,128]{1,0:T(8,128)S(1)} %add.19.curve), channel_id=1, source_target_pairs={{0,2},{1,3},{2,0},{3,1},{4,6},{5,7},{6,4},{7,5},{8,10},{9,11},{10,... | collective-permute-start | bytes 12296 | tf_op jit(solution)/shard_map/ppermute | solution.py:558

commit v4 on v3

--- a/solution.py
+++ b/solution.py
@@ -267,96 +267,265 @@
     put([up(x) for x in get(ref, *at, 0)], ref, *at, deep)
 
 
-def tangent_kernel(
-    depth, wet, bed, rough, direction, counts, rim_top, rim_bottom, side_b, side_a,
-    curve_ref, m_c, source, a_x, b_x, c_x, a_y, b_y, c_y,
-    nat, hx, sb_x, sb_y, q_x, q_y, inv_x, inv_y, cond_x, cond_y, cnt,
-    tan_a, tan_b, flow, tmp,
+def up(x):
+    return pltpu.roll(x, SUB - 1, 0)
+
+
+def down(x):
+    return pltpu.roll(x, 1, 0)
+
+
+def sublanes():
+    return lax.broadcasted_iota(jnp.int32, (SUB, LANES), 0)
+
+
+def to_right(x, nxt):
+    last = lanes_of((SUB, LANES)) == LANES - 1
+    return jnp.where(last, pltpu.roll(nxt, LANES - 1, 1), pltpu.roll(x, LANES - 1, 1))
+
+
+def right(xs):
+    last = lanes_of((SUB, LANES)) == LANES - 1
+    r = [pltpu.roll(x, LANES - 1, 1) for x in xs]
+    return [jnp.where(last, r[(j + 1) % len(xs)], r[j]) for j in range(len(xs))]
+
+
+def left(xs):
+    first = lanes_of((SUB, LANES)) == 0
+    r = [pltpu.roll(x, 1, 1) for x in xs]
+    return [jnp.where(first, r[j - 1], r[j]) for j in range(len(xs))]
+
+
+def at_lanes(j):
+    return slice(j * LANES, (j + 1) * LANES)
+
+
+def get(ref, *at):
+    return [ref[(*at, slice(None), at_lanes(j))] for j in range(ref.shape[-1] // LANES)]
+
+
+def put(xs, ref, *at):
+    for j, x in enumerate(xs):
+        ref[(*at, slice(None), at_lanes(j))] = x
+
+
+def followers(first, below, above):
+    last = sublanes() == SUB - 1
+    f, b, a = up(first), up(below), up(above)
+    return jnp.where(last, b, f), b, jnp.where(last, f, a)
+
+
+def follow(ref, *at):
+    deep = ref.shape[-3] - 5
+    sets = zip(get(ref, *at, 0), get(ref, *at, deep), get(ref, *at, deep + 1))
+    for k, xs in enumerate(zip(*[followers(*x) for x in sets])):
+        put(xs, ref, *at, deep + 2 + k)
+
+
+def preceding(ref, deep, passed):
+    first = sublanes() == 0
+    last, below, above = get(ref, deep), get(ref, deep + 1), get(ref, deep + 2)
+    return (
+        [jnp.where(first, down(a), down(l)) for a, l in zip(above, last)],
+        [jnp.where(first, down(l), down(b)) - l for b, l in zip(below, last)],
+        [down(a) - b for a, b in zip(above, below)],
+    )
+
+
+def face(h, h_k, sb, cond, inv):
+    hs = h + h_k
+    s = (h_k - h) + sb
+    x = s * s + slope_floor
+    y = lax.rsqrt(x)
+    p = cond * (jnp.exp2((2.0 / 3.0 / LN2) * jnp.log(hs)) * (y * lax.rsqrt(y)))
+    ps = p * s
+    t = p * hs
+    A = (5.0 / 3.0) * ps
+    B = t * (0.5 + (0.5 * slope_floor) * (y * y))
+    return A - B, A + B, (ps * hs) * inv
+
+
+scale = time_step * 2.0 ** (-2.0 / 3.0)
+
+
+def inner_kernel(
+    depth, wet, bed, rough, direction, counts,
+    prim, cnt, a_x, b_x, c_x, a_y, b_y, c_y, q_x, q_y,
+    nat, sb_x, sb_y, inv_x, inv_y, cond_x, cond_y,
 ):
     events, steps, rows, cols = depth.shape
-    tall = rows + 2 * SUB
-    deep = tall // SUB
-    tiles = cols // LANES
-    count = tiles + 1
+    deep, count = rows // SUB, cols // LANES
+    fields = [bed, rough, direction] + [wet.at[e] for e in range(events)]
+    fields += [depth.at[e, t] for e in range(events) for t in range(steps)]
+    fields += [counts.at[e] for e in range(events)]
+    for k, x in enumerate(fields):
+        for j in range(count):
+            nat[k, j] = x[:, at_lanes(j)].astype(jnp.float32)
+
+    @pl.loop(0, deep, unroll=4)
+    def _(i):
+        spread = lambda k: [nat[k, j, pl.ds(i, SUB, stride=deep), :] for j in range(count)]
+        m = [jnp.exp(x) for x in spread(1)]
+        put(spread(0), prim, 0, i)
+        put(m, prim, 1, i)
+        put([x * y for x, y in zip(m, spread(2))], prim, 2, i)
+        for k in range(3, 3 + events * (steps + 1)):
+            put(spread(k), prim, k, i)
+        for e in range(events):
+            put(spread(3 + events * (steps + 1) + e), cnt, e, i)
+
+    for k in range(3 + events * (steps + 1)):
+        put([up(x) for x in get(prim, k, 0)], prim, k, deep)
+
+    @pl.loop(0, deep, unroll=4)
+    def _(i):
+        b, m, q = (get(prim, k, i) for k in range(3))
+        put([y - x for x, y in zip(b, right(b))], sb_x, i)
+        put([y - x for x, y in zip(b, get(prim, 0, i + 1))], sb_y, i)
+        ix = [1.0 / (x + y) for x, y in zip(m, right(m))]
+        iy = [1.0 / (x + y) for x, y in zip(m, get(prim, 1, i + 1))]
+        put([-x for x in ix], inv_x, i)
+        put([-x for x in iy], inv_y, i)
+        put([x + y for x, y in zip(q, right(q))], q_x, i)
+        put([x + y for x, y in zip(q, get(prim, 2, i + 1))], q_y, i)
+        for e in range(events):
+            w = get(prim, 3 + e, i)
+            put([(scale * z) * (x * y) for x, y, z in zip(w, right(w), ix)], cond_x, e, i)
+            put([(scale * z) * (x * y) for x, y, z in zip(w, get(prim, 3 + e, i + 1), iy)], cond_y, e, i)
+
+    @pl.loop(0, events)
+    def _(e):
+        for t in range(steps):
+
+            @pl.loop(0, deep, unroll=4)
+            def _(i):
+                k = 3 + events + e * steps + t
+                h = get(prim, k, i)
+                h_r, h_d = right(h), get(prim, k, i + 1)
+                for j in range(count):
+                    J = at_lanes(j)
+                    for h_k, sb, cond, inv, a, b, c in (
+                        (h_r, sb_x, cond_x, inv_x, a_x, b_x, c_x),
+                        (h_d, sb_y, cond_y, inv_y, a_y, b_y, c_y),
+                    ):
+                        A, B, C = face(h[j], h_k[j], sb[i, :, J], cond[e, i, :, J], inv[i, :, J])
+                        c[e, t, i, :, J] = C
+                        if t:
+                            a[e, t - 1, i, :, J] = A
+                            b[e, t - 1, i, :, J] = B
+
+
+def inner(depth, wet, bed, rough, direction, counts):
+    events, steps, rows, cols = depth.shape
+    deep = rows // SUB
+    shape = lambda *lead: (*lead, deep, SUB, cols)
+    vm = lambda *lead: pltpu.VMEM(shape(*lead), jnp.float32)
+    out = lambda *lead: jax.ShapeDtypeStruct(shape(*lead), jnp.float32)
+    vmem = pl.BlockSpec(memory_space=pltpu.VMEM)
+    fields = 3 + events * (steps + 1)
+    return pl.pallas_call(
+        inner_kernel,
+        in_specs=[vmem] * 6,
+        out_specs=[vmem] * 10,
+        out_shape=[
+            jax.ShapeDtypeStruct((fields, deep + 1, SUB, cols), jnp.float32),
+            out(events),
+            *[out(events, steps - 1), out(events, steps - 1), out(events, steps)] * 2,
+            out(),
+            out(),
+        ],
+        scratch_shapes=[
+            pltpu.VMEM((fields + events, cols // LANES, rows, LANES), jnp.float32),
+            *[vm()] * 4,
+            *[vm(events)] * 2,
+        ],
+        compiler_params=pltpu.CompilerParams(vmem_limit_bytes=12 * 1024 * 1024),
+        cost_estimate=pl.CostEstimate(flops=100000000, bytes_accessed=16000000, transcendentals=0),
+        name="inner",
+    )(depth, wet, bed, rough, direction, counts)
+
+
+def tangent_kernel(
+    prim, cnt, ia_x, ib_x, ic_x, ia_y, ib_y, ic_y, iq_x, iq_y, rim_top, rim_bottom, side_b, side_a,
+    curve_ref, source, a_x, b_x, c_x, a_y, b_y, c_y,
+    nat, ext, xcnt, sb_x, sb_y, q_x, q_y, inv_x, inv_y, cond_x, cond_y, tan_a, tan_b, flow,
+):
+    events, steps, deep, _, cols = ic_x.shape
+    rows, tiles = deep * SUB, cols // LANES
+    count, tall = tiles + 1, rows + 2 * SUB
     even_col = lax.axis_index("col") % 2 == 0
     lane_t = lanes_of((tall, LANES))
-    sub = lax.broadcasted_iota(jnp.int32, (SUB, LANES), 0)
     right_rim = jnp.where(even_col, side_a[...], side_b[...])
     left_rim = jnp.where(even_col, side_b[...], side_a[...])
-    J = [slice(j * LANES, (j + 1) * LANES) for j in range(count)]
+    J = [at_lanes(j) for j in range(count)]
     zero = jnp.zeros((SUB, LANES), jnp.float32)
-
-    def assemble(f, own, k):
-        for j in range(tiles):
-            nat[k, j, 0:SUB, :] = rim_top[f, :, J[j]]
-            nat[k, j, SUB : SUB + rows, :] = own[:, J[j]]
-            nat[k, j, SUB + rows : tall, :] = rim_bottom[f, :, J[j]]
+    below, above = deep, deep + 1
+    fields = prim.shape[0]
+
+    place_in = [events * (steps + 1) + k for k in range(3)]
+    place_in += [events * steps + e for e in range(events)]
+    place_in += [e * steps + t for e in range(events) for t in range(steps)]
+    place_in += [events * (steps + 1) + 3 + e for e in range(events)]
+    for k, f in enumerate(place_in):
         place = f * REACH
         r = pltpu.roll(right_rim, (LANES - place) % LANES, 1) if place else right_rim
         l = pltpu.roll(left_rim, (LANES - REACH - place) % LANES, 1)
-        extra = jnp.where(lane_t < REACH, r, jnp.where(lane_t >= LANES - REACH, l, 0.0))
-        nat[k, tiles] = extra
-
-    def spread(k, i):
-        return [nat[k, j, pl.ds(i, SUB, stride=deep), :] for j in range(count)]
-
-    base = events * (steps + 1)
-    for k, (f, x) in enumerate(((base, bed), (base + 1, rough), (base + 2, direction))):
-        assemble(f, x[...], k)
-    for e in range(events):
-        assemble(events * steps + e, wet[e].astype(jnp.float32), 3 + e)
-        assemble(base + 3 + e, counts[e], 3 + events + e)
-        for t in range(steps):
-            assemble(e * steps + t, depth[e, t], 3 + 2 * events + e * steps + t)
-
-    @pl.loop(0, deep, unroll=5)
+        x = jnp.where(lane_t < REACH, r, jnp.where(lane_t >= LANES - REACH, l, 0.0))
+        if k == 1:
+            m_side = x = jnp.exp(x)
+        if k == 2:
+            x = m_side * x
+        nat[k] = x
+        to, n = (ext, k) if k < fields else (xcnt, k - fields)
+        for i in range(deep):
+            to[n, i, :, J[tiles]] = nat[k, pl.ds(SUB + i, SUB, stride=deep), :]
+        for i, rim, at in ((below, rim_bottom, SUB + rows), (above, rim_top, 0)):
+            xs = get(rim, f)
+            if k == 1:
+                xs = [jnp.exp(x) for x in xs]
+            if k == 2:
+                xs = [x * y for x, y in zip(xs, get(ext, 1, i))]
+            put(xs, to, n, i)
+            to[n, i, :, J[tiles]] = nat[k, at : at + SUB, :]
+
+    def value(k, i, j):
+        return ext[k, i, :, J[j]] if j == tiles or (isinstance(i, int) and i >= deep) else prim[k, i, :, J[j]]
+
+    def next_rows(k, j):
+        return followers(value(k, 0, j), value(k, below, j), value(k, above, j))
+
+    for k in range(fields):
+        ext[k, deep + 2, :, J[tiles]] = next_rows(k, tiles)[0]
+
+    def derive(i, j, along, k_of):
+        sb, inv, q, cond = (sb_x, inv_x, q_x, cond_x) if along else (sb_y, inv_y, q_y, cond_y)
+        x, y = k_of(0)
+        sb[i, :, J[j]] = y - x
+        x, y = k_of(1)
+        z = 1.0 / (x + y)
+        inv[i, :, J[j]] = -z
+        x, y = k_of(2)
+        q[i, :, J[j]] = x + y
+        for e in range(events):
+            x, y = k_of(3 + e)
+            cond[e, i, :, J[j]] = (scale * z) * (x * y)
+
+    def across(i, j):
+        return lambda k: (value(k, i, j), to_right(value(k, i, j), value(k, i, (j + 1) % count)))
+
+    @pl.loop(0, deep, unroll=4)
     def _(i):
-        m = [jnp.exp(x) for x in spread(1, i)]
-        put(spread(0, i), tmp, 0, i)
-        put(m, tmp, 1, i)
-        put(m, m_c, i)
-        put([x * y for x, y in zip(m, spread(2, i))], tmp, 2, i)
-        for e in range(events):
-            put(spread(3 + e, i), tmp, 3 + e, i)
-            put(spread(3 + events + e, i), cnt, e, i)
-            for t in range(steps):
-                put(spread(3 + 2 * events + e * steps + t, i), hx, e, t, i)
-
-    for k in range(3 + events):
-        wrap(tmp, k)
-    for e in range(events):
-        for t in range(steps):
-            wrap(hx, e, t)
-
-    scale = time_step * 2.0 ** (-2.0 / 3.0)
-
-    @pl.loop(0, deep, unroll=5)
-    def _(i):
-        b, m, q = (get(tmp, k, i) for k in range(3))
-        put([y - x for x, y in zip(b, right(b))], sb_x, i)
-        put([y - x for x, y in zip(b, get(tmp, 0, i + 1))], sb_y, i)
-        ix = [1.0 / (x + y) for x, y in zip(m, right(m))]
-        iy = [1.0 / (x + y) for x, y in zip(m, get(tmp, 1, i + 1))]
-        put([-x for x in ix], inv_x, i)
-        put([-x for x in iy], inv_y, i)
-        put([x + y for x, y in zip(q, right(q))], q_x, i)
-        put([x + y for x, y in zip(q, get(tmp, 2, i + 1))], q_y, i)
-        for e in range(events):
-            w = get(tmp, 3 + e, i)
-            put([(scale * z) * (x * y) for x, y, z in zip(w, right(w), ix)], cond_x, e, i)
-            put([(scale * z) * (x * y) for x, y, z in zip(w, get(tmp, 3 + e, i + 1), iy)], cond_y, e, i)
-
-    def face(h, h_k, sb, cond, inv):
-        hs = h + h_k
-        s = (h_k - h) + sb
-        x = s * s + slope_floor
-        y = lax.rsqrt(x)
-        p = cond * (jnp.exp2((2.0 / 3.0 / LN2) * jnp.log(hs)) * (y * lax.rsqrt(y)))
-        ps = p * s
-        t = p * hs
-        A = (5.0 / 3.0) * ps
-        B = t * (0.5 + (0.5 * slope_floor) * (y * y))
-        return A - B, A + B, (ps * hs) * inv
+        for j in (tiles - 1, tiles):
+            derive(i, j, True, across(i, j))
+        n = jnp.where(i == deep - 1, deep + 2, i + 1)
+        derive(i, tiles, False, lambda k: (value(k, i, tiles), ext[k, n, :, J[tiles]]))
+
+    for i in (below, above):
+        for j in range(count):
+            derive(i, j, True, across(i, j))
+    for n, i in enumerate((deep - 1, below, above)):
+        for j in range(tiles if n == 0 else count):
+            derive(i, j, False, lambda k: (value(k, i, j), next_rows(k, j)[n]))
 
     curve_ref[...] = jnp.zeros(curve_ref.shape, jnp.float32)
     put([zero] * count, flow, 0)
@@ -365,26 +534,50 @@
     def _(e):
         for t in range(steps):
             old, new = (tan_a, tan_b) if t % 2 else (tan_b, tan_a)
-
-            @pl.loop(0, deep, unroll=5)
-            def _(i):
-                h = get(hx, e, t, i)
-                h_r, h_d = right(h), get(hx, e, t, i + 1)
+            k = 3 + events + e * steps + t
+
+            def row(i):
+                static = isinstance(i, int)
+                rim = static and i >= deep
+                nxt = i + 3 if static and i >= deep - 1 else i + 1
                 if t:
                     d = get(old, i)
-                    d_r, d_d = right(d), get(old, i + 1)
+                    d_r, d_d = right(d), get(old, nxt)
                 fx, fy = [], []
+                here = lambda j: ext[k, i, :, J[j]] if rim or j == tiles else prim[k, i, :, J[j]]
                 for j in range(count):
-                    A, B, C = face(h[j], h_r[j], sb_x[i, :, J[j]], cond_x[e, i, :, J[j]], inv_x[i, :, J[j]])
-                    f = C * q_x[i, :, J[j]]
+                    inside = not rim and j < tiles - 1
+                    if inside:
+                        A, B = (ia_x[e, t - 1, i, :, J[j]], ib_x[e, t - 1, i, :, J[j]]) if t else (None, None)
+                        C = ic_x[e, t, i, :, J[j]]
+                        f = C * iq_x[i, :, J[j]]
+                    else:
+                        h = here(j)
+                        A, B, C = face(
+                            h, to_right(h, here((j + 1) % count)),
+                            sb_x[i, :, J[j]], cond_x[e, i, :, J[j]], inv_x[i, :, J[j]],
+                        )
+                        f = C * q_x[i, :, J[j]]
                     c_x[e, t, i, :, J[j]] = C
                     if t:
                         a_x[e, t - 1, i, :, J[j]] = A
                         b_x[e, t - 1, i, :, J[j]] = B
                         f += A * d[j] + B * d_r[j]
                     fx.append(f)
-                    A, B, C = face(h[j], h_d[j], sb_y[i, :, J[j]], cond_y[e, i, :, J[j]], inv_y[i, :, J[j]])
-                    f = C * q_y[i, :, J[j]]
+                    inside = not (static and i >= deep - 1) and j < tiles
+                    if inside:
+                        A, B = (ia_y[e, t - 1, i, :, J[j]], ib_y[e, t - 1, i, :, J[j]]) if t else (None, None)
+                        C = ic_y[e, t, i, :, J[j]]
+                        f = C * iq_y[i, :, J[j]]
+                    else:
+                        h = here(j)
+                        if static and i >= deep - 1:
+                            first = ext[k, 0, :, J[j]] if j == tiles else prim[k, 0, :, J[j]]
+                            h_d = followers(first, ext[k, below, :, J[j]], ext[k, above, :, J[j]])[i - deep + 1]
+                        else:
+                            h_d = ext[k, i + 1, :, J[j]]
+                        A, B, C = face(h, h_d, sb_y[i, :, J[j]], cond_y[e, i, :, J[j]], inv_y[i, :, J[j]])
+                        f = C * q_y[i, :, J[j]]
                     c_y[e, t, i, :, J[j]] = C
                     if t:
                         a_y[e, t - 1, i, :, J[j]] = A
@@ -398,26 +591,59 @@
                     r = (fx[j] - fl[j]) + (fy[j] - before[j])
                     new[i, :, J[j]] = d[j] + r if t else r
 
+            main = deep - 2
+            pl.loop(0, main, unroll=3 if main % 3 == 0 else 1)(row)
+            for i in range(main, deep + 2):
+                row(i)
+            for i, lack in zip((0, below, above), preceding(flow, deep, zero)):
+                put([x - y for x, y in zip(get(new, i), lack)], new, i)
+            follow(new)
+
+        old = tan_a if steps % 2 else tan_b
+        total = zero
+        for i in range(deep + 2):
             for j in range(count):
-                new[0, :, J[j]] = new[0, :, J[j]] - down(flow[deep, :, J[j]])
-            wrap(new)
-
-        old = tan_a if steps % 2 else tan_b
-
-        @pl.loop(0, deep, unroll=5)
-        def _(i):
-            row = sub * deep + i
-            own = (row >= SUB) & (row < SUB + rows)
-            total = zero
-            for j in range(count):
+                own = i < deep and j < tiles
+                n = cnt[e, i, :, J[j]] if own else xcnt[e, i, :, J[j]]
                 r = old[i, :, J[j]]
-                s = (gauge_weight * cnt[e, i, :, J[j]]) * r
+                s = (gauge_weight * n) * r
                 source[e, i, :, J[j]] = s
-                if j < tiles:
+                if own:
                     total += s * r
-            curve_ref[...] += jnp.where(own, total, 0.0)
-
-        wrap(source, e)
+        curve_ref[...] += total
+        follow(source, e)
+
+
+def tangents(prim, cnt, *more_inputs):
+    fields, _, _, cols = prim.shape
+    events, deep = cnt.shape[:2]
+    steps = more_inputs[2].shape[1]
+    wide = cols + LANES
+    regs = deep + 2
+    vm = lambda *lead: pltpu.VMEM((*lead, regs, SUB, wide), jnp.float32)
+    more = lambda *lead: pltpu.VMEM((*lead, regs + 3, SUB, wide), jnp.float32)
+    out = lambda *lead: jax.ShapeDtypeStruct((*lead, regs, SUB, wide), jnp.float32)
+    vmem = pl.BlockSpec(memory_space=pltpu.VMEM)
+    return pl.pallas_call(
+        tangent_kernel,
+        in_specs=[vmem] * (2 + len(more_inputs)),
+        out_specs=[vmem] * 8,
+        out_shape=[
+            jax.ShapeDtypeStruct((SUB, LANES), jnp.float32),
+            jax.ShapeDtypeStruct((events, regs + 3, SUB, wide), jnp.float32),
+            *[out(events, steps - 1), out(events, steps - 1), out(events, steps)] * 2,
+        ],
+        scratch_shapes=[
+            pltpu.VMEM((fields + events, deep * SUB + 2 * SUB, LANES), jnp.float32),
+            more(fields),
+            vm(events),
+            *[vm()] * 6,
+            *[vm(events)] * 2,
+            *[more()] * 3,
+        ],
+        compiler_params=pltpu.CompilerParams(vmem_limit_bytes=16 * 1024 * 1024),
+        name="tangents",
+    )(prim, cnt, *more_inputs)
 
 
 def adjoint_kernel(first_event, last_event, m_c, source, a_x, b_x, c_x, a_y, b_y, c_y, *refs):
@@ -425,7 +651,8 @@
     outs = refs[len(sums) : len(sums) + (1 if last_event else 2)]
     nat, adj_a, adj_b, flow, *own = refs[len(sums) + len(outs) :]
     g_x, g_y = own if last_event else outs
-    steps, deep, _, wide = c_x.shape
+    steps, regs, _, wide = c_x.shape
+    deep = regs - 2
     count = wide // LANES
     J = [at_lanes(j) for j in range(count)]
     zero = jnp.zeros((SUB, LANES), jnp.float32)
@@ -439,10 +666,10 @@
         else:
             base_x, base_y = g_x, g_y
 
-        @pl.loop(0, deep, unroll=5)
+        @pl.loop(0, regs, unroll=5 if regs % 5 == 0 else 1)
         def _(i):
             l = get(old, i)
-            l_r, l_d = right(l), get(old, i + 1)
+            l_r, l_d = right(l), get(old, jnp.where(i < deep - 1, i + 1, i + 3))
             acc, kx, ky = [], [], []
             for j in range(count):
                 p = l[j] - l_r[j]
@@ -465,17 +692,21 @@
                     new[i, :, J[j]] = acc[j] + (kl[j] + before[j])
 
         if t:
-            for j in range(count):
-                new[0, :, J[j]] = new[0, :, J[j]] + down(flow[deep, :, J[j]])
-            wrap(new)
+            for i, lack in zip((0, deep, deep + 1), preceding(flow, deep, zero)):
+                put([x + y for x, y in zip(get(new, i), lack)], new, i)
+            follow(new)
 
     if last_event:
         (grad_ref,) = outs
-        rows, cols = grad_ref.shape
-        tiles = cols // LANES
-        put([down(x) for x in get(g_y, deep - 1)], flow, 0)
-
-        @pl.loop(0, deep, unroll=5)
+        tiles = grad_ref.shape[-1] // LANES
+        first = sublanes() == 0
+        put(
+            [jnp.where(first, down(a), down(l)) for a, l in zip(get(g_y, deep + 1), get(g_y, deep - 1))],
+            flow,
+            0,
+        )
+
+        @pl.loop(0, deep, unroll=4)
         def _(i):
             x, y = get(g_x, i), get(g_y, i)
             put(y, flow, i + 1)
@@ -485,65 +716,34 @@
                 nat[j, pl.ds(i, SUB, stride=deep), :] = g
 
         for j in range(tiles):
-            grad_ref[:, J[j]] = nat[j, SUB : SUB + rows, :]
-
-
-def tangents(depth, wet, bed, rough, direction, counts, rim_top, rim_bottom, side_b, side_a):
-    events, steps, rows, cols = depth.shape
-    tall, wide = rows + 2 * SUB, cols + LANES
-    deep = tall // SUB
-    shape = lambda *lead: (*lead, deep, SUB, wide)
-    vm = lambda *lead: pltpu.VMEM(shape(*lead), jnp.float32)
-    more = lambda *lead: pltpu.VMEM((*lead, deep + 1, SUB, wide), jnp.float32)
-    out = lambda *lead: jax.ShapeDtypeStruct(shape(*lead), jnp.float32)
-    vmem = pl.BlockSpec(memory_space=pltpu.VMEM)
-    fields = 3 + events * (steps + 2)
-    return pl.pallas_call(
-        tangent_kernel,
-        in_specs=[vmem] * 10,
-        out_specs=[vmem] * 9,
-        out_shape=[
-            jax.ShapeDtypeStruct((SUB, LANES), jnp.float32),
-            out(),
-            jax.ShapeDtypeStruct((events, deep + 1, SUB, wide), jnp.float32),
-            *[out(events, steps - 1), out(events, steps - 1), out(events, steps)] * 2,
-        ],
-        scratch_shapes=[
-            pltpu.VMEM((fields, wide // LANES, tall, LANES), jnp.float32),
-            more(events, steps),
-            *[vm()] * 6,
-            *[vm(events)] * 3,
-            *[more()] * 3,
-            more(3 + events),
-        ],
-        compiler_params=pltpu.CompilerParams(vmem_limit_bytes=20 * 1024 * 1024),
-        name="tangents",
-    )(depth, wet, bed, rough, direction, counts, rim_top, rim_bottom, side_b, side_a)
-
-
-def gradient(e, rows, cols, sums, m_c, source, *coefficients):
-    events, _, _, wide = source.shape
-    deep = m_c.shape[0]
+            grad_ref[:, J[j]] = nat[j]
+
+
+def gradient(e, sums, prim, source, *coefficients):
+    events, entries, _, wide = source.shape
+    cols, regs = prim.shape[-1], entries - 3
+    rows = (regs - 2) * SUB
     first, last = e == 0, e == events - 1
-    vm = (deep, SUB, wide)
-    more = pltpu.VMEM((deep + 1, SUB, wide), jnp.float32)
-    vmem = pl.BlockSpec(memory_space=pltpu.VMEM)
+    vm = (regs, SUB, wide)
+    more = pltpu.VMEM((entries, SUB, wide), jnp.float32)
     own = lambda x: pl.BlockSpec((None, *x.shape[1:]), lambda i: (e,) + (0,) * (x.ndim - 1))
     whole = lambda shape: pl.BlockSpec(shape, lambda i: (0,) * len(shape))
     return pl.pallas_call(
         functools.partial(adjoint_kernel, first, last),
         grid=(1,),
-        in_specs=[whole(m_c.shape), own(source)] + [own(x) for x in coefficients] + [whole(vm)] * len(sums),
+        in_specs=[pl.BlockSpec((None, *prim.shape[1:]), lambda i: (1, 0, 0, 0)), own(source)]
+        + [own(x) for x in coefficients]
+        + [whole(vm)] * len(sums),
         out_specs=whole((rows, cols)) if last else [whole(vm)] * 2,
         out_shape=jax.ShapeDtypeStruct((rows, cols), jnp.float32)
         if last
         else [jax.ShapeDtypeStruct(vm, jnp.float32)] * 2,
-        scratch_shapes=[pltpu.VMEM((cols // LANES, deep * SUB, LANES), jnp.float32), more, more, more]
+        scratch_shapes=[pltpu.VMEM((cols // LANES, rows, LANES), jnp.float32), more, more, more]
         + [pltpu.VMEM(vm, jnp.float32)] * (2 if last else 0),
         compiler_params=pltpu.CompilerParams(vmem_limit_bytes=16 * 1024 * 1024),
         cost_estimate=pl.CostEstimate(flops=40000000, bytes_accessed=12000000, transcendentals=0),
         name="gradient",
-    )(m_c, source, *coefficients, *sums)
+    )(prim, source, *coefficients, *sums)
 
 
 def hops_over(axis):
@@ -586,18 +786,18 @@
     pays = edge_rows(cells, depth, wet, bed, rough, direction)
     rims = [exchange(x, "row", k) for k, x in enumerate(pays)]
     counts = gauges(cells, rows, cols)
+    block = inner(depth, wet, bed, rough, direction, counts)
+    rims, block = lax.optimization_barrier((rims, block))
     rim_top, rim_bottom, send_b, send_a = rims_and_columns(
         rims, depth, wet, bed, rough, direction, counts
     )
     side_b = exchange(send_b, "col", 1)
     side_a = exchange(send_a, "col", 0)
-    curve, *coefficients = tangents(
-        depth, wet, bed, rough, direction, counts, rim_top, rim_bottom, side_b, side_a
-    )
+    curve, *coefficients = tangents(*block, rim_top, rim_bottom, side_b, side_a)
     hops = hops_over("event") + hops_over("row") + hops_over("col")
     sums = ()
     for e in range(events):
-        sums = gradient(e, rows, cols, sums, *coefficients)
+        sums = gradient(e, sums, block[0], *coefficients)
         if hops:
             curve = hop_sum(curve, *hops.pop(0))
             sums, curve = lax.optimization_barrier((sums, curve))

time: 46.2 us -> 44.6 us (0.965)
  waiting for transfers between devices: 14.9 us -> 10.7 us
  Pallas kernels: 13.3 us -> 15.8 us
    ppermute x3, waiting for transfers between devices: 8 us -> 3.84 us  [exchange(): return lax.ppermute(x, axis, perm) if perm else None]
    pallas_call x1 -> x2, Pallas kernels: 6.98 us -> 9.41 us  [the longest x1 5.31 us: tangents(): pl.pallas_call(tangent_kernel, in_specs=[vmem] * (2 + len(more_inputs)),...]
  transfers between devices with their start and end apart: 10 -> 10, of which waited for: 6 -> 6; matrix products, arithmetic and copies ran while one was open for 0% -> 0% of each run, Pallas kernels for 7% -> 16%
where the time goes in v4:
time: 44.6 us; the launch traced here: 44.4 us
  starting transfers between devices  17 us (38%)
  Pallas kernels  15.8 us (35%)
  waiting for transfers between devices  10.7 us (24%)
  between operations  0.81 us (2%)
    ppermute x7, starting transfers between devices, from_hop(): lax.ppermute(x, axis, [(i, i ^ hop) for i in range(lax.axis_size(axis))])  8.63 us
    ppermute x3, starting transfers between devices, exchange(): return lax.ppermute(x, axis, perm) if perm else None  8.37 us
    ppermute x7, waiting for transfers between devices, from_hop(): lax.ppermute(x, axis, [(i, i ^ hop) for i in range(lax.axis_size(axis))])  6.88 us
    pallas_call x1, Pallas kernels, tangents(): pl.pallas_call(tangent_kernel, in_specs=[vmem] * (2 + len(more_inputs)),...  5.31 us
    pallas_call x1, Pallas kernels, inner(): pl.pallas_call(inner_kernel, in_specs=[vmem] * 6, out_specs=[vmem] * 10,...  4.1 us
    ppermute x3, waiting for transfers between devices, exchange(): return lax.ppermute(x, axis, perm) if perm else None  3.84 us
    pallas_call x2, Pallas kernels, gradient(): pl.pallas_call(functools.partial(adjoint_kernel, first, last), grid=(1,),...  2.74 us
    pallas_call x1, Pallas kernels, edge_rows(): pl.pallas_call(functools.partial(rows_kernel, sides), in_specs=[anywhere]...  1.92 us
  transfers between devices with their start and end apart: 10, of which 6 were waited for; matrix products, arithmetic and copies ran while one was open for 0% of the time, Pallas kernels for 16%

profile of v4, /device:TPU:0, one launch (start us, length us, event | category | flops | bytes accessed | tf_op | source)
XLA Modules:
  0.0 44.4 jit_solution(1051912027552633384)
XLA Ops:
  0.6 0.0 copy-start.5
  0.6 0.0 copy-start
  0.7 0.0 copy-start.1
  0.7 0.0 copy-start.2
  0.7 0.0 copy-start.3
  0.7 0.0 copy-start.4
  0.7 1.9 %edge_rows.1 = f32[64,1024]{1,0:T(8,128)} custom-call(s32[2,1,1024]{2,1,0:T(1,128)} %bitcast.2, f32[2,3,64,1024]{3,2,1,0:T(8,128)} %refs_7_.1, s32[2,64,1024]{2,1,0:T(8,128)} %refs_8_.1, f32[64,1024]{1,0:T(8,128)} %refs_9_.1, f32[64,1024]{1,0:T(8,128)} %refs_10_.1, f32[64,1024]{1,0:T(8,128)} %refs_11_.1), custom_call_target="tpu_custom_call" | custom-call | tf_op jit(solution)/shard_map/edge_rows/pallas_call | solution.py:106
  2.6 3.0 %collective-permute-start = (f32[64,1024]{1,0:T(8,128)}, f32[64,1024]{1,0:T(8,128)S(1)}, u32[]{:S(2)}, u32[]{:S(2)}) collective-permute-start(f32[64,1024]{1,0:T(8,128)} %edge_rows.1), channel_id=1, source_target_pairs={{0,4},{4,0},{1,5},{5,1},{2,6},{6,2},{3,7},{7,3},{8,12},{12,8},{9,1... | collective-permute-start | bytes 786440 | tf_op jit(solution)/shard_map/ppermute | solution.py:28
  5.7 0.0 copy-done.5
  5.7 0.5 %gauges.1.counts.refs_6_.refs_12_ = f32[2,64,1024]{2,1,0:T(8,128)S(1)} custom-call(s32[2,1,1024]{2,1,0:T(1,128)S(1)} %bitcast.3), custom_call_target="tpu_custom_call" | custom-call | flops 20000000 | bytes 4000000 | tf_op jit(solution)/shard_map/gauges/pallas_call | solution.py:128
  6.2 0.0 copy-done
  6.2 0.0 copy-done.1
  6.2 0.0 copy-done.2
  6.2 0.0 copy-done.3
  6.2 0.0 copy-done.4
  6.2 4.1 %inner.1 = (f32[11,9,8,1024]{3,2,1,0:T(8,128)S(1)}, f32[2,8,8,1024]{3,2,1,0:T(8,128)S(1)}, f32[2,2,8,8,1024]{4,3,2,1,0:T(8,128)S(1)}, f32[2,2,8,8,1024]{4,3,2,1,...) custom-call(f32[2,3,64,1024]{3,2,1,0:T(8,128)S(1)} %copy-done, ...), custom_call_target="tpu_custom_call" | custom-call | flops 100000000 | bytes 16000000 | tf_op jit(solution)/shard_map/inner/pallas_call | solution.py:426
  10.3 1.9 %collective-permute-done.refs_0_ = f32[64,1024]{1,0:T(8,128)S(1)} collective-permute-done((f32[64,1024]{1,0:T(8,128)}, f32[64,1024]{1,0:T(8,128)S(1)}, u32[]{:S(2)}, u32[]{:S(2)}) %collective-permute-start) | collective-permute-done | bytes 262176 | tf_op jit(solution)/shard_map/ppermute | solution.py:28
  12.2 0.5 %rims_and_columns.1 = (f32[13,8,1024]{2,1,0:T(8,128)S(1)}, f32[13,8,1024]{2,1,0:T(8,128)S(1)}, f32[80,128]{1,0:T(8,128)S(1)}, f32[80,128]{1,0:T(8,128)S(1)}) custom-call(f32[64,1024]{1,0:T(8,128)S(1)} %collective-permute-done.refs_0_, f32[2,3,64,1024]{3,2,1,0:T(8,128)S(1)} %copy-done, s32[2,64,1024]{2,1,0:T(8,128)S(1)} %copy-done.1, ...), custom_call_target="tpu_custom_call" | custom-call | tf_op jit(solution)/shard_map/rims_and_columns/pallas_call | solution.py:221
  12.7 0.7 %collective-permute-start.1 = (f32[80,128]{1,0:T(8,128)S(1)}, f32[80,128]{1,0:T(8,128)S(1)}, u32[]{:S(2)}, u32[]{:S(2)}) collective-permute-start(f32[80,128]{1,0:T(8,128)S(1)} %get-tuple-element.69), channel_id=1, source_target_pairs={{1,2},{2,1},{5,6},{6,5},{9,10},{10,9},{13,14},{14,13},{17,18},{18,... | collective-permute-start | bytes 122888 | tf_op jit(solution)/shard_map/ppermute | solution.py:28
  13.4 4.7 %collective-permute-start.2 = (f32[80,128]{1,0:T(8,128)S(1)}, f32[80,128]{1,0:T(8,128)S(1)}, u32[]{:S(2)}, u32[]{:S(2)}) collective-permute-start(f32[80,128]{1,0:T(8,128)S(1)} %get-tuple-element.70), channel_id=1, source_target_pairs={{0,1},{1,0},{2,3},{3,2},{4,5},{5,4},{6,7},{7,6},{8,9},{9,8},{10,11... | collective-permute-start | bytes 122888 | tf_op jit(solution)/shard_map/ppermute | solution.py:28
  18.1 0.0 collective-permute-done.1.side_b
  18.1 2.0 %collective-permute-done.2.side_a = f32[80,128]{1,0:T(8,128)S(1)} collective-permute-done((f32[80,128]{1,0:T(8,128)S(1)}, f32[80,128]{1,0:T(8,128)S(1)}, u32[]{:S(2)}, u32[]{:S(2)}) %collective-permute-start.2) | collective-permute-done | bytes 40992 | tf_op jit(solution)/shard_map/ppermute | solution.py:28
  20.0 5.3 %tangents.1 = (f32[8,128]{1,0:T(8,128)S(1)}, f32[2,13,8,1152]{3,2,1,0:T(8,128)S(1)}, f32[2,2,10,8,1152]{4,3,2,1,0:T(8,128)S(1)}, f32[2,2,10,8,1152]{4,3,2,1,0:T(...) custom-call(f32[11,9,8,1024]{3,2,1,0:T(8,128)S(1)} %get-tuple-elemen, ...), custom_call_target="tpu_custom_call" | custom-call | tf_op jit(solution)/shard_map/tangents/pallas_call | solution.py:627
  25.3 0.1 collective-permute-start.3
  25.4 1.2 %gradient.2 = (f32[10,8,1152]{2,1,0:T(8,128)S(1)}, f32[10,8,1152]{2,1,0:T(8,128)S(1)}) custom-call(f32[11,9,8,1024]{3,2,1,0:T(8,128)S(1)} %get-tuple-element.56.prim.m_c, f32[2,13,8,1152]{3,2,1,0:T(8,128)S(1)} %get-tuple-element.71.source, f32[2,2,10,8,1152]{4,3,2,1,0:T(8,128)S(1)} %get-tuple-element.72.a_x, ...), custom_call_target="tpu_custom_call" | custom-call | flops 40000000 | bytes 12000000 | tf_op jit(solution)/shard_map/gradient/pallas_call | solution.py:731
  26.7 0.0 collective-permute-done.3
  26.7 1.6 %collective-permute-start.4 = (f32[8,128]{1,0:T(8,128)S(1)}, f32[8,128]{1,0:T(8,128)S(1)}, u32[]{:S(2)}, u32[]{:S(2)}) collective-permute-start(f32[8,128]{1,0:T(8,128)S(1)} %add.15), channel_id=1, source_target_pairs={{0,16},{8,24},{16,0},{24,8},{1,17},{9,25},{17,1},{25,9},{2,18},{10... | collective-permute-start | bytes 12296 | tf_op jit(solution)/shard_map/ppermute | solution.py:758
  28.2 1.5 %gradient.3 = f32[64,1024]{1,0:T(8,128)S(1)} custom-call(f32[11,9,8,1024]{3,2,1,0:T(8,128)S(1)} %get-tuple-element.56.prim.m_c, f32[2,13,8,1152]{3,2,1,0:T(8,128)S(1)} %get-tuple-element.71.source, f32[2,2,10,8,1152]{4,3,2,1,0:T(8,128)S(1)} %get-tuple-element.72.a_x, f32[2,2,10,8,1152]{4,3,2,1,0:T(8,128)S(1)} %get-tuple-element.73.b_x, ...), custom_call_target="tpu_custom_call" | custom-call | flops 40000000 | bytes 12000000 | tf_op jit(solution)/shard_map/gradient/pallas_call | solution.py:731
  29.8 0.6 %collective-permute-done.4 = f32[8,128]{1,0:T(8,128)S(1)} collective-permute-done((f32[8,128]{1,0:T(8,128)S(1)}, f32[8,128]{1,0:T(8,128)S(1)}, u32[]{:S(2)}, u32[]{:S(2)}) %collective-permute-start.4) | collective-permute-done | bytes 4128 | tf_op jit(solution)/shard_map/ppermute | solution.py:758
  30.4 0.0 collective-permute-start.5
  30.4 1.5 %collective-permute-start.6 = (f32[8,128]{1,0:T(8,128)S(1)}, f32[8,128]{1,0:T(8,128)S(1)}, u32[]{:S(2)}, u32[]{:S(2)}) collective-permute-start(f32[8,128]{1,0:T(8,128)S(1)} %add.16), channel_id=1, source_target_pairs={{0,4},{4,0},{1,5},{5,1},{2,6},{6,2},{3,7},{7,3},{8,12},{12,8},{9,1... | collective-permute-start | bytes 12296 | tf_op jit(solution)/shard_map/ppermute | solution.py:758
  31.9 2.1 %collective-permute-done.6 = f32[8,128]{1,0:T(8,128)S(1)} collective-permute-done((f32[8,128]{1,0:T(8,128)S(1)}, f32[8,128]{1,0:T(8,128)S(1)}, u32[]{:S(2)}, u32[]{:S(2)}) %collective-permute-start.6) | collective-permute-done | bytes 4128 | tf_op jit(solution)/shard_map/ppermute | solution.py:758
  34.0 0.0 collective-permute-done.5
  34.0 1.6 %collective-permute-start.7 = (f32[64,1024]{1,0:T(8,128)S(1)}, f32[64,1024]{1,0:T(8,128)S(1)}, u32[]{:S(2)}, u32[]{:S(2)}) collective-permute-start(f32[64,1024]{1,0:T(8,128)S(1)} %add.17.grad), channel_id=1, source_target_pairs={{0,16},{8,24},{16,0},{24,8},{1,17},{9,25},{17,1},{25,9},{2,18},{10... | collective-permute-start | bytes 786440 | tf_op jit(solution)/shard_map/ppermute | solution.py:758
  35.6 2.0 %collective-permute-start.8 = (f32[8,128]{1,0:T(8,128)S(1)}, f32[8,128]{1,0:T(8,128)S(1)}, u32[]{:S(2)}, u32[]{:S(2)}) collective-permute-start(f32[8,128]{1,0:T(8,128)S(1)} %add.18), channel_id=1, source_target_pairs={{0,1},{1,0},{2,3},{3,2},{4,5},{5,4},{6,7},{7,6},{8,9},{9,8},{10,11... | collective-permute-start | bytes 12296 | tf_op jit(solution)/shard_map/ppermute | solution.py:758
  37.6 1.6 %collective-permute-done.8 = f32[8,128]{1,0:T(8,128)S(1)} collective-permute-done((f32[8,128]{1,0:T(8,128)S(1)}, f32[8,128]{1,0:T(8,128)S(1)}, u32[]{:S(2)}, u32[]{:S(2)}) %collective-permute-start.8) | collective-permute-done | bytes 4128 | tf_op jit(solution)/shard_map/ppermute | solution.py:758
  39.2 1.9 %collective-permute-start.9 = (f32[8,128]{1,0:T(8,128)S(1)}, f32[8,128]{1,0:T(8,128)S(1)}, u32[]{:S(2)}, u32[]{:S(2)}) collective-permute-start(f32[8,128]{1,0:T(8,128)S(1)} %add.19.curve), channel_id=1, source_target_pairs={{0,2},{1,3},{2,0},{3,1},{4,6},{5,7},{6,4},{7,5},{8,10},{9,11},{10,... | collective-permute-start | bytes 12296 | tf_op jit(solution)/shard_map/ppermute | solution.py:758
  41.1 2.6 %collective-permute-done.9.curve_arrived = f32[8,128]{1,0:T(8,128)S(1)} collective-permute-done((f32[8,128]{1,0:T(8,128)S(1)}, f32[8,128]{1,0:T(8,128)S(1)}, u32[]{:S(2)}, u32[]{:S(2)}) %collective-permute-start.9) | collective-permute-done | bytes 4128 | tf_op jit(solution)/shard_map/ppermute | solution.py:758
  43.7 0.0 collective-permute-done.7.arrived
  43.7 0.7 %finish.1 = (f32[64,1024]{1,0:T(8,128)}, f32[1,1]{1,0:T(1,128)}) custom-call(f32[64,1024]{1,0:T(8,128)S(1)} %add.17.grad, f32[64,1024]{1,0:T(8,128)S(1)} %collective-permute-done.7.arrived, f32[8,128]{1,0:T(8,128)S(1)} %add.19.curve, f32[8,128]{1,0:T(8,128)S(1)} %collective-permute-done.9.curve_arrived), custom_call_target="tpu_custom_call" | custom-call | tf_op jit(solution)/shard_map/finish/pallas_call | solution.py:772
  (5 shorter events, 0.0 us)
Async XLA Ops:
  0.6 5.0 %copy-start.5 = (s32[2,1,1,1024]{3,2,1,0:T(1,128)S(1)}, s32[2,1,1,1024]{3,2,1,0:T(1,128)}, u32[]{:S(2)}) copy-start(s32[2,1,1,1024]{3,2,1,0:T(1,128)} %param.11) | copy-start | bytes 24580
  0.6 5.5 %copy-start = (f32[2,3,64,1024]{3,2,1,0:T(8,128)S(1)}, f32[2,3,64,1024]{3,2,1,0:T(8,128)}, u32[]{:S(2)}) copy-start(f32[2,3,64,1024]{3,2,1,0:T(8,128)} %refs_7_.1) | copy-start | bytes 4718596
  0.7 5.5 %copy-start.1 = (s32[2,64,1024]{2,1,0:T(8,128)S(1)}, s32[2,64,1024]{2,1,0:T(8,128)}, u32[]{:S(2)}) copy-start(s32[2,64,1024]{2,1,0:T(8,128)} %refs_8_.1) | copy-start | bytes 1572868
  0.7 5.5 %copy-start.2 = (f32[64,1024]{1,0:T(8,128)S(1)}, f32[64,1024]{1,0:T(8,128)}, u32[]{:S(2)}) copy-start(f32[64,1024]{1,0:T(8,128)} %refs_9_.1) | copy-start | bytes 786436
  0.7 5.5 %copy-start.3 = (f32[64,1024]{1,0:T(8,128)S(1)}, f32[64,1024]{1,0:T(8,128)}, u32[]{:S(2)}) copy-start(f32[64,1024]{1,0:T(8,128)} %refs_10_.1) | copy-start | bytes 786436
  0.7 5.5 %copy-start.4 = (f32[64,1024]{1,0:T(8,128)S(1)}, f32[64,1024]{1,0:T(8,128)}, u32[]{:S(2)}) copy-start(f32[64,1024]{1,0:T(8,128)} %refs_11_.1) | copy-start | bytes 786436
  2.6 9.5 %collective-permute-start = (f32[64,1024]{1,0:T(8,128)}, f32[64,1024]{1,0:T(8,128)S(1)}, u32[]{:S(2)}, u32[]{:S(2)}) collective-permute-start(f32[64,1024]{1,0:T(8,128)} %edge_rows.1), channel_id=1, source_target_pairs={{0,4},{4,0},{1,5},{5,1},{2,6},{6,2},{3,7},{7,3},{8,12},{12,8},{9,1... | collective-permute-start | bytes 786440 | tf_op jit(solution)/shard_map/ppermute | solution.py:28
  12.7 5.4 %collective-permute-start.1 = (f32[80,128]{1,0:T(8,128)S(1)}, f32[80,128]{1,0:T(8,128)S(1)}, u32[]{:S(2)}, u32[]{:S(2)}) collective-permute-start(f32[80,128]{1,0:T(8,128)S(1)} %get-tuple-element.69), channel_id=1, source_target_pairs={{1,2},{2,1},{5,6},{6,5},{9,10},{10,9},{13,14},{14,13},{17,18},{18,... | collective-permute-start | bytes 122888 | tf_op jit(solution)/shard_map/ppermute | solution.py:28
  13.4 6.7 %collective-permute-start.2 = (f32[80,128]{1,0:T(8,128)S(1)}, f32[80,128]{1,0:T(8,128)S(1)}, u32[]{:S(2)}, u32[]{:S(2)}) collective-permute-start(f32[80,128]{1,0:T(8,128)S(1)} %get-tuple-element.70), channel_id=1, source_target_pairs={{0,1},{1,0},{2,3},{3,2},{4,5},{5,4},{6,7},{7,6},{8,9},{9,8},{10,11... | collective-permute-start | bytes 122888 | tf_op jit(solution)/shard_map/ppermute | solution.py:28
  25.3 1.3 %collective-permute-start.3 = (f32[8,128]{1,0:T(8,128)S(1)}, f32[8,128]{1,0:T(8,128)S(1)}, u32[]{:S(2)}, u32[]{:S(2)}) collective-permute-start(f32[8,128]{1,0:T(8,128)S(1)} %get-tuple-element.80), channel_id=1, source_target_pairs={{0,8},{8,0},{16,24},{24,16},{1,9},{9,1},{17,25},{25,17},{2,10},{10... | collective-permute-start | bytes 12296 | tf_op jit(solution)/shard_map/ppermute | solution.py:758
  26.7 3.7 %collective-permute-start.4 = (f32[8,128]{1,0:T(8,128)S(1)}, f32[8,128]{1,0:T(8,128)S(1)}, u32[]{:S(2)}, u32[]{:S(2)}) collective-permute-start(f32[8,128]{1,0:T(8,128)S(1)} %add.15), channel_id=1, source_target_pairs={{0,16},{8,24},{16,0},{24,8},{1,17},{9,25},{17,1},{25,9},{2,18},{10... | collective-permute-start | bytes 12296 | tf_op jit(solution)/shard_map/ppermute | solution.py:758
  30.4 3.6 %collective-permute-start.5 = (f32[64,1024]{1,0:T(8,128)S(1)}, f32[64,1024]{1,0:T(8,128)S(1)}, u32[]{:S(2)}, u32[]{:S(2)}) collective-permute-start(f32[64,1024]{1,0:T(8,128)S(1)} %gradient.3), channel_id=1, source_target_pairs={{0,8},{8,0},{16,24},{24,16},{1,9},{9,1},{17,25},{25,17},{2,10},{10... | collective-permute-start | bytes 786440 | tf_op jit(solution)/shard_map/ppermute | solution.py:758
  30.4 3.6 %collective-permute-start.6 = (f32[8,128]{1,0:T(8,128)S(1)}, f32[8,128]{1,0:T(8,128)S(1)}, u32[]{:S(2)}, u32[]{:S(2)}) collective-permute-start(f32[8,128]{1,0:T(8,128)S(1)} %add.16), channel_id=1, source_target_pairs={{0,4},{4,0},{1,5},{5,1},{2,6},{6,2},{3,7},{7,3},{8,12},{12,8},{9,1... | collective-permute-start | bytes 12296 | tf_op jit(solution)/shard_map/ppermute | solution.py:758
  34.0 9.7 %collective-permute-start.7 = (f32[64,1024]{1,0:T(8,128)S(1)}, f32[64,1024]{1,0:T(8,128)S(1)}, u32[]{:S(2)}, u32[]{:S(2)}) collective-permute-start(f32[64,1024]{1,0:T(8,128)S(1)} %add.17.grad), channel_id=1, source_target_pairs={{0,16},{8,24},{16,0},{24,8},{1,17},{9,25},{17,1},{25,9},{2,18},{10... | collective-permute-start | bytes 786440 | tf_op jit(solution)/shard_map/ppermute | solution.py:758
  35.6 3.6 %collective-permute-start.8 = (f32[8,128]{1,0:T(8,128)S(1)}, f32[8,128]{1,0:T(8,128)S(1)}, u32[]{:S(2)}, u32[]{:S(2)}) collective-permute-start(f32[8,128]{1,0:T(8,128)S(1)} %add.18), channel_id=1, source_target_pairs={{0,1},{1,0},{2,3},{3,2},{4,5},{5,4},{6,7},{7,6},{8,9},{9,8},{10,11... | collective-permute-start | bytes 12296 | tf_op jit(solution)/shard_map/ppermute | solution.py:758
  39.2 4.5 %collective-permute-start.9 = (f32[8,128]{1,0:T(8,128)S(1)}, f32[8,128]{1,0:T(8,128)S(1)}, u32[]{:S(2)}, u32[]{:S(2)}) collective-permute-start(f32[8,128]{1,0:T(8,128)S(1)} %add.19.curve), channel_id=1, source_target_pairs={{0,2},{1,3},{2,0},{3,1},{4,6},{5,7},{6,4},{7,5},{8,10},{9,11},{10,... | collective-permute-start | bytes 12296 | tf_op jit(solution)/shard_map/ppermute | solution.py:758

commit v5 on v4

--- a/solution.py
+++ b/solution.py
@@ -58,37 +58,52 @@
     return [hits[b * rows : (b + 1) * rows] for b in range(cols // 256)]
 
 
-def rows_kernel(sides, *refs):
-    ins, pays, rest = refs[1:6], refs[6 : 6 + sides], refs[6 + sides :]
+def edge_kernel(sides, *refs):
+    ins, outs, rest = refs[1:6], refs[6 : 9 + 3 * sides], refs[9 + 3 * sides :]
+    cnt, pay_a, pay_b, *more = outs
+    pays, corners = more[:sides], more[sides:]
     cells, sems = rest[-2:]
     events, steps, rows, cols = ins[0].shape
     even = lax.axis_index("row") % 2 == 0
+    even_col = lax.axis_index("col") % 2 == 0
     slots, count = plan(events, steps)
     sub = lax.broadcasted_iota(jnp.int32, (SUB, cols), 0)
     copies = [pltpu.make_async_copy(refs[0], cells, sems.at[0, 5])]
-    copies[0].start()
+    edges = []
     for k in range(sides):
         sends_last = even if k == 0 else jnp.logical_not(even)
         edge = pl.multiple_of(jnp.where(sends_last, rows - SUB, 0), SUB)
+        edges.append((sends_last, edge))
         for i, x in enumerate(ins):
             lead = (slice(None),) * (len(x.shape) - 2)
-            copy = pltpu.make_async_copy(
-                x.at[(*lead, pl.ds(edge, SUB), slice(None))], rest[5 * k + i], sems.at[k, i]
-            )
-            copy.start()
-            copies.append(copy)
+            at = x.at[(*lead, pl.ds(edge, SUB), slice(None))]
+            copies.append(pltpu.make_async_copy(at, rest[5 * k + i], sems.at[k, i]))
+    columns = (rest[5 * sides : 5 * sides + 5], rest[5 * sides + 5 : 5 * sides + 10])
+    for k in range(2):
+        for i, x in enumerate(ins):
+            lead = (slice(None),) * (len(x.shape) - 1)
+            at = x.at[(*lead, slice(0, LANES) if k == 0 else slice(cols - LANES, cols))]
+            copies.append(pltpu.make_async_copy(at, columns[k][i], sems.at[sides + k, i]))
     for copy in copies:
+        copy.start()
+    copies[0].wait()
+    for e in range(events):
+        g = cells[e]
+        for b, x in enumerate(tally_of(g // cols, g % cols, rows, cols)):
+            for j in range(256 // LANES):
+                cnt[e, b * (256 // LANES) + j] = x[:, j * LANES : (j + 1) * LANES]
+    for copy in copies[1:]:
         copy.wait()
+
     for k, pay in enumerate(pays):
         d, w, b, r, v = rest[5 * k : 5 * k + 5]
-        sends_last = even if k == 0 else jnp.logical_not(even)
         fields = [d[e, t] for e in range(events) for t in range(steps)]
         fields += [w[e].astype(jnp.float32) for e in range(events)] + [b[...], r[...], v[...]]
         fields += [jnp.broadcast_to(cells[e].astype(jnp.float32), (SUB, cols)) for e in range(events)]
         tiles = [jnp.zeros((SUB, cols), jnp.float32)] * count
         for x, (n, slot) in zip(fields, slots):
             if 1 < n < SUB:
-                x = jnp.where(sends_last, pltpu.roll(x, n, 0), x)
+                x = jnp.where(edges[k][0], pltpu.roll(x, n, 0), x)
             for i in range(slot // SUB, (slot + n - 1) // SUB + 1):
                 low, high = slot - i * SUB, slot + n - i * SUB
                 y = pltpu.roll(x, low % SUB, 0) if low % SUB else x
@@ -96,53 +111,65 @@
         for i in range(count):
             pay[i * SUB : (i + 1) * SUB] = tiles[i]
 
-
-def edge_rows(cells, depth, wet, bed, rough, direction):
-    events, steps, _, cols = depth.shape
+    lane = lanes_of((rows, LANES))
+    packs = []
+    for side in range(2):
+        d, w, b, r, v = columns[side]
+        pack = jnp.zeros((rows, LANES), jnp.float32)
+        xs = [d[e, t] for e in range(events) for t in range(steps)]
+        xs += [w[e].astype(jnp.float32) for e in range(events)]
+        xs += [b[...], r[...], v[...]]
+        xs += [cnt[e, 0 if side == 0 else cols // LANES - 1] for e in range(events)]
+        for f, x in enumerate(xs):
+            place = f * REACH
+            shift = (place + REACH if side == 1 else place) % LANES
+            if shift:
+                x = pltpu.roll(x, shift, 1)
+            pack = jnp.where((lane >= place) & (lane < place + REACH), x, pack)
+        packs.append(pack)
+    pay_a[...] = jnp.where(even_col, packs[1], packs[0])
+    pay_b[...] = jnp.where(even_col, packs[0], packs[1])
+    for k in range(sides):
+        corners[2 * k][...] = pay_a[pl.ds(edges[k][1], SUB), :]
+        corners[2 * k + 1][...] = pay_b[pl.ds(edges[k][1], SUB), :]
+
+
+def edges_and_gauges(cells, depth, wet, bed, rough, direction):
+    events, steps, rows, cols = depth.shape
     sides = 2 if lax.axis_size("row") > 2 else 1
     _, count = plan(events, steps)
     vmem, anywhere = pl.BlockSpec(memory_space=pltpu.VMEM), pl.BlockSpec(memory_space=pl.ANY)
     ins = (depth, wet, bed, rough, direction)
+    shapes = [(events, cols // LANES, rows, LANES)] + [(rows, LANES)] * 2
+    shapes += [(count * SUB, cols)] * sides + [(SUB, LANES)] * (2 * sides)
     return pl.pallas_call(
-        functools.partial(rows_kernel, sides),
+        functools.partial(edge_kernel, sides),
         in_specs=[anywhere] * 6,
-        out_specs=[vmem] * sides,
-        out_shape=[jax.ShapeDtypeStruct((count * SUB, cols), jnp.float32)] * sides,
+        out_specs=[vmem] * len(shapes),
+        out_shape=[jax.ShapeDtypeStruct(x, jnp.float32) for x in shapes],
         scratch_shapes=[pltpu.VMEM((*x.shape[:-2], SUB, cols), x.dtype) for x in ins] * sides
-        + [pltpu.VMEM(cells.shape, cells.dtype), pltpu.SemaphoreType.DMA((sides, 6))],
+        + [pltpu.VMEM((*x.shape[:-1], LANES), x.dtype) for x in ins] * 2
+        + [pltpu.VMEM(cells.shape, cells.dtype), pltpu.SemaphoreType.DMA((sides + 2, 6))],
         compiler_params=pltpu.CompilerParams(vmem_limit_bytes=58 * 1024 * 1024),
-        name="edge_rows",
+        name="edges",
     )(cells, *ins)
 
 
-def gauge_kernel(cells, cnt):
-    events, rows, cols = cnt.shape
-    for e in range(events):
-        g = cells[e]
-        for b, x in enumerate(tally_of(g // cols, g % cols, rows, cols)):
-            cnt[e, :, b * 256 : (b + 1) * 256] = x
-
-
-def gauges(cells, rows, cols):
-    vmem = pl.BlockSpec(memory_space=pltpu.VMEM)
-    return pl.pallas_call(
-        gauge_kernel,
-        in_specs=[vmem],
-        out_specs=vmem,
-        out_shape=jax.ShapeDtypeStruct((cells.shape[0], rows, cols), jnp.float32),
-        compiler_params=pltpu.CompilerParams(vmem_limit_bytes=12 * 1024 * 1024),
-        cost_estimate=pl.CostEstimate(flops=20000000, bytes_accessed=4000000, transcendentals=0),
-        name="gauges",
-    )(cells)
-
-
-def column_kernel(sides, *refs):
-    rims_in, own = refs[:sides], (refs[sides : sides + 6], refs[sides + 6 : sides + 12])
-    rim_top, rim_bottom, pay_b, pay_a = refs[sides + 12 :]
-    events, steps, rows, _ = own[0][0].shape
+def diagonal(x, first_row, first_col):
+    count = lax.axis_size("col")
+    perm = [
+        (a * count + c, b * count + d)
+        for a, b in pairs(lax.axis_size("row"), first_row)
+        for c, d in pairs(count, first_col)
+    ]
+    return lax.ppermute(x, ("row", "col"), perm)
+
+
+def rim_kernel(sides, events, steps, rows, *refs):
+    rims_in = refs[:sides]
+    rim_top, rim_bottom = refs[sides:]
     cols = rim_top.shape[-1]
     even_row = lax.axis_index("row") % 2 == 0
-    even_col = lax.axis_index("col") % 2 == 0
     sub = lax.broadcasted_iota(jnp.int32, (SUB, cols), 0)
     slots, _ = plan(events, steps)
     base = events * (steps + 1) + 3
@@ -178,93 +205,18 @@
         rim_bottom[base + e] = jnp.where(even_row, first, hits)
         rim_top[base + e] = jnp.where(even_row, hits, first)
 
-    lane = lanes_of((rows + 2 * SUB, LANES))
-    packs = []
-    for side in range(2):
-        d, w, b, r, v, c = own[side]
-        place_of = slice(0, LANES) if side == 0 else slice(cols - LANES, cols)
-        pack = jnp.zeros((rows + 2 * SUB, LANES), jnp.float32)
-        xs = [d[e, t] for e in range(events) for t in range(steps)]
-        xs += [w[e].astype(jnp.float32) for e in range(events)]
-        xs += [b[...], r[...], v[...]]
-        xs += [c[e] for e in range(events)]
-        for f, x in enumerate(xs):
-            x = jnp.concatenate([rim_top[f, :, place_of], x, rim_bottom[f, :, place_of]], axis=0)
-            place = f * REACH
-            shift = (place + REACH if side == 1 else place) % LANES
-            if shift:
-                x = pltpu.roll(x, shift, 1)
-            pack = jnp.where((lane >= place) & (lane < place + REACH), x, pack)
-        packs.append(pack)
-    pay_a[...] = jnp.where(even_col, packs[1], packs[0])
-    pay_b[...] = jnp.where(even_col, packs[0], packs[1])
-
-
-def rims_and_columns(rims, depth, wet, bed, rough, direction, counts):
-    events, steps, rows, cols = depth.shape
-    last = cols // LANES - 1
-
-    def side(j):
-        return [
-            pl.BlockSpec((events, steps, rows, LANES), lambda i: (0, 0, 0, j)),
-            pl.BlockSpec((events, rows, LANES), lambda i: (0, 0, j)),
-            pl.BlockSpec((rows, LANES), lambda i: (0, j)),
-            pl.BlockSpec((rows, LANES), lambda i: (0, j)),
-            pl.BlockSpec((rows, LANES), lambda i: (0, j)),
-            pl.BlockSpec((events, rows, LANES), lambda i: (0, 0, j)),
-        ]
-
-    whole = lambda shape: pl.BlockSpec(shape, lambda i: (0,) * len(shape))
-    tall = (rows + 2 * SUB, LANES)
-    rim = (events * (steps + 2) + 3, SUB, cols)
-    own = (depth, wet, bed, rough, direction, counts)
+
+def row_rims(rims, events, steps, rows):
+    vmem = pl.BlockSpec(memory_space=pltpu.VMEM)
+    rim = jax.ShapeDtypeStruct((events * (steps + 2) + 3, SUB, rims[0].shape[-1]), jnp.float32)
     return pl.pallas_call(
-        functools.partial(column_kernel, len(rims)),
-        grid=(1,),
-        in_specs=[whole(r.shape) for r in rims] + side(0) + side(last),
-        out_specs=[whole(rim)] * 2 + [whole(tall)] * 2,
-        out_shape=[jax.ShapeDtypeStruct(rim, jnp.float32)] * 2 + [jax.ShapeDtypeStruct(tall, jnp.float32)] * 2,
-        compiler_params=pltpu.CompilerParams(vmem_limit_bytes=12 * 1024 * 1024),
-        name="rims_and_columns",
-    )(*rims, *own, *own)
-
-
-def up(x):
-    return pltpu.roll(x, SUB - 1, 0)
-
-
-def down(x):
-    return pltpu.roll(x, 1, 0)
-
-
-def right(xs):
-    last = lanes_of((SUB, LANES)) == LANES - 1
-    r = [pltpu.roll(x, LANES - 1, 1) for x in xs]
-    return [jnp.where(last, r[(j + 1) % len(xs)], r[j]) for j in range(len(xs))]
-
-
-def left(xs):
-    first = lanes_of((SUB, LANES)) == 0
-    r = [pltpu.roll(x, 1, 1) for x in xs]
-    return [jnp.where(first, r[j - 1], r[j]) for j in range(len(xs))]
-
-
-def at_lanes(j):
-    return slice(j * LANES, (j + 1) * LANES)
-
-
-def get(ref, *at):
-    return [ref[(*at, slice(None), at_lanes(j))] for j in range(ref.shape[-1] // LANES)]
-
-
-def put(xs, ref, *at):
-    for j, x in enumerate(xs):
-        ref[(*at, slice(None), at_lanes(j))] = x
-
-
-def wrap(ref, *at):
-    deep = ref.shape[-3] - 1
-    put([up(x) for x in get(ref, *at, 0)], ref, *at, deep)
+        functools.partial(rim_kernel, len(rims), events, steps, rows),
+        in_specs=[vmem] * len(rims),
+        out_specs=[vmem] * 2,
+        out_shape=[rim] * 2,
+        compiler_params=pltpu.CompilerParams(vmem_limit_bytes=4 * 1024 * 1024),
+        name="row_rims",
+    )(*rims)
 
 
 def up(x):
@@ -349,15 +301,14 @@
 
 
 def inner_kernel(
-    depth, wet, bed, rough, direction, counts,
-    prim, cnt, a_x, b_x, c_x, a_y, b_y, c_y, q_x, q_y,
+    depth, wet, bed, rough, direction,
+    prim, a_x, b_x, c_x, a_y, b_y, c_y, q_x, q_y,
     nat, sb_x, sb_y, inv_x, inv_y, cond_x, cond_y,
 ):
     events, steps, rows, cols = depth.shape
     deep, count = rows // SUB, cols // LANES
     fields = [bed, rough, direction] + [wet.at[e] for e in range(events)]
     fields += [depth.at[e, t] for e in range(events) for t in range(steps)]
-    fields += [counts.at[e] for e in range(events)]
     for k, x in enumerate(fields):
         for j in range(count):
             nat[k, j] = x[:, at_lanes(j)].astype(jnp.float32)
@@ -371,8 +322,6 @@
         put([x * y for x, y in zip(m, spread(2))], prim, 2, i)
         for k in range(3, 3 + events * (steps + 1)):
             put(spread(k), prim, k, i)
-        for e in range(events):
-            put(spread(3 + events * (steps + 1) + e), cnt, e, i)
 
     for k in range(3 + events * (steps + 1)):
         put([up(x) for x in get(prim, k, 0)], prim, k, deep)
@@ -415,7 +364,7 @@
                             b[e, t - 1, i, :, J] = B
 
 
-def inner(depth, wet, bed, rough, direction, counts):
+def inner(depth, wet, bed, rough, direction):
     events, steps, rows, cols = depth.shape
     deep = rows // SUB
     shape = lambda *lead: (*lead, deep, SUB, cols)
@@ -425,29 +374,28 @@
     fields = 3 + events * (steps + 1)
     return pl.pallas_call(
         inner_kernel,
-        in_specs=[vmem] * 6,
-        out_specs=[vmem] * 10,
+        in_specs=[vmem] * 5,
+        out_specs=[vmem] * 9,
         out_shape=[
             jax.ShapeDtypeStruct((fields, deep + 1, SUB, cols), jnp.float32),
-            out(events),
             *[out(events, steps - 1), out(events, steps - 1), out(events, steps)] * 2,
             out(),
             out(),
         ],
         scratch_shapes=[
-            pltpu.VMEM((fields + events, cols // LANES, rows, LANES), jnp.float32),
+            pltpu.VMEM((fields, cols // LANES, rows, LANES), jnp.float32),
             *[vm()] * 4,
             *[vm(events)] * 2,
         ],
         compiler_params=pltpu.CompilerParams(vmem_limit_bytes=12 * 1024 * 1024),
         cost_estimate=pl.CostEstimate(flops=100000000, bytes_accessed=16000000, transcendentals=0),
         name="inner",
-    )(depth, wet, bed, rough, direction, counts)
+    )(depth, wet, bed, rough, direction)
 
 
 def tangent_kernel(
-    prim, cnt, ia_x, ib_x, ic_x, ia_y, ib_y, ic_y, iq_x, iq_y, rim_top, rim_bottom, side_b, side_a,
-    curve_ref, source, a_x, b_x, c_x, a_y, b_y, c_y,
+    prim, cnt, ia_x, ib_x, ic_x, ia_y, ib_y, ic_y, iq_x, iq_y, rim_top, rim_bottom, side_a, side_b,
+    corner_aa, corner_ab, corner_ba, corner_bb, curve_ref, source, a_x, b_x, c_x, a_y, b_y, c_y,
     nat, ext, xcnt, sb_x, sb_y, q_x, q_y, inv_x, inv_y, cond_x, cond_y, tan_a, tan_b, flow,
 ):
     events, steps, deep, _, cols = ic_x.shape
@@ -455,8 +403,16 @@
     count, tall = tiles + 1, rows + 2 * SUB
     even_col = lax.axis_index("col") % 2 == 0
     lane_t = lanes_of((tall, LANES))
-    right_rim = jnp.where(even_col, side_a[...], side_b[...])
-    left_rim = jnp.where(even_col, side_b[...], side_a[...])
+    even_row = lax.axis_index("row") % 2 == 0
+
+    def whole_side(side, corner_a, corner_b):
+        above = jnp.where(even_row, corner_b[...], corner_a[...])
+        below = jnp.where(even_row, corner_a[...], corner_b[...])
+        return jnp.concatenate([above, side[...], below], axis=0)
+
+    full_a, full_b = whole_side(side_a, corner_aa, corner_ba), whole_side(side_b, corner_ab, corner_bb)
+    right_rim = jnp.where(even_col, full_a, full_b)
+    left_rim = jnp.where(even_col, full_b, full_a)
     J = [at_lanes(j) for j in range(count)]
     zero = jnp.zeros((SUB, LANES), jnp.float32)
     below, above = deep, deep + 1
@@ -604,7 +560,7 @@
         for i in range(deep + 2):
             for j in range(count):
                 own = i < deep and j < tiles
-                n = cnt[e, i, :, J[j]] if own else xcnt[e, i, :, J[j]]
+                n = cnt[e, j, pl.ds(i, SUB, stride=deep), :] if own else xcnt[e, i, :, J[j]]
                 r = old[i, :, J[j]]
                 s = (gauge_weight * n) * r
                 source[e, i, :, J[j]] = s
@@ -616,7 +572,7 @@
 
 def tangents(prim, cnt, *more_inputs):
     fields, _, _, cols = prim.shape
-    events, deep = cnt.shape[:2]
+    events, deep = cnt.shape[0], prim.shape[1] - 1
     steps = more_inputs[2].shape[1]
     wide = cols + LANES
     regs = deep + 2
@@ -783,17 +739,18 @@
 def local(depth, wet, bed, rough, direction, gauge_cells):
     events, steps, rows, cols = depth.shape
     cells = gauge_cells.reshape(events, 1, -1)
-    pays = edge_rows(cells, depth, wet, bed, rough, direction)
-    rims = [exchange(x, "row", k) for k, x in enumerate(pays)]
-    counts = gauges(cells, rows, cols)
-    block = inner(depth, wet, bed, rough, direction, counts)
-    rims, block = lax.optimization_barrier((rims, block))
-    rim_top, rim_bottom, send_b, send_a = rims_and_columns(
-        rims, depth, wet, bed, rough, direction, counts
-    )
+    sides = 2 if lax.axis_size("row") > 2 else 1
+    counts, send_a, send_b, *more = edges_and_gauges(cells, depth, wet, bed, rough, direction)
+    rims = [exchange(x, "row", k) for k, x in enumerate(more[:sides])]
+    side_a = exchange(send_a, "col", 0)
     side_b = exchange(send_b, "col", 1)
-    side_a = exchange(send_a, "col", 0)
-    curve, *coefficients = tangents(*block, rim_top, rim_bottom, side_b, side_a)
+    corners = [diagonal(x, k // 2, k % 2) for k, x in enumerate(more[sides:])]
+    block = inner(depth, wet, bed, rough, direction)
+    rims, side_a, side_b, corners, block = lax.optimization_barrier((rims, side_a, side_b, corners, block))
+    if sides == 1:
+        corners = corners + [jnp.zeros_like(x) for x in corners]
+    rim_top, rim_bottom = row_rims(rims, events, steps, rows)
+    curve, *coefficients = tangents(block[0], counts, *block[1:], rim_top, rim_bottom, side_a, side_b, *corners)
     hops = hops_over("event") + hops_over("row") + hops_over("col")
     sums = ()
     for e in range(events):

time: 44.6 us -> 42.9 us (0.962)
  waiting for transfers between devices: 10.7 us -> 6.09 us
  starting transfers between devices: 17 us -> 19.9 us
    ppermute x0 -> x2, starting transfers between devices: none -> 5.19 us  [diagonal(): return lax.ppermute(x, ('row', 'col'), perm)]
    ppermute x3, waiting for transfers between devices: 3.84 us -> 0.01 us  [exchange(): return lax.ppermute(x, axis, perm) if perm else None]
    ppermute x3, starting transfers between devices: 8.37 us -> 5.26 us  [exchange(): return lax.ppermute(x, axis, perm) if perm else None]
    ppermute x7, waiting for transfers between devices: 6.88 us -> 6.07 us  [from_hop(): lax.ppermute(x, axis, [(i, i ^ hop) for i in range(lax.axis_size(axis))])]
    ppermute x7, starting transfers between devices: 8.63 us -> 9.43 us  [from_hop(): lax.ppermute(x, axis, [(i, i ^ hop) for i in range(lax.axis_size(axis))])]
    pallas_call x4 -> x3, Pallas kernels: 7.05 us -> 7.03 us  [the longest x1 3.95 us: inner(): pl.pallas_call(inner_kernel, in_specs=[vmem] * 5, out_specs=[vmem] * 9, o...]
  transfers between devices with their start and end apart: 10 -> 12, of which waited for: 6 -> 4; matrix products, arithmetic and copies ran while one was open for 0% -> 0% of each run, Pallas kernels for 16% -> 16%
where the time goes in v5:
time: 42.9 us; the launch traced here: 42.7 us
  starting transfers between devices  19.9 us (46%)
  Pallas kernels  15.8 us (37%)
  waiting for transfers between devices  6.09 us (14%)
  between operations  0.85 us (2%)
    ppermute x7, starting transfers between devices, from_hop(): lax.ppermute(x, axis, [(i, i ^ hop) for i in range(lax.axis_size(axis))])  9.43 us
    ppermute x7, waiting for transfers between devices, from_hop(): lax.ppermute(x, axis, [(i, i ^ hop) for i in range(lax.axis_size(axis))])  6.07 us
    pallas_call x1, Pallas kernels, tangents(): pl.pallas_call(tangent_kernel, in_specs=[vmem] * (2 + len(more_inputs)),...  5.34 us
    ppermute x3, starting transfers between devices, exchange(): return lax.ppermute(x, axis, perm) if perm else None  5.26 us
    ppermute x2, starting transfers between devices, diagonal(): return lax.ppermute(x, ('row', 'col'), perm)  5.19 us
    pallas_call x1, Pallas kernels, inner(): pl.pallas_call(inner_kernel, in_specs=[vmem] * 5, out_specs=[vmem] * 9, o...  3.95 us
    pallas_call x2, Pallas kernels, gradient(): pl.pallas_call(functools.partial(adjoint_kernel, first, last), grid=(1,),...  2.75 us
    pallas_call x1, Pallas kernels, edges_and_gauges(): pl.pallas_call(functools.partial(edge_kernel, sides), in_specs=[anywhere]...  2.59 us
  transfers between devices with their start and end apart: 12, of which 4 were waited for; matrix products, arithmetic and copies ran while one was open for 0% of the time, Pallas kernels for 16%

profile of v5, /device:TPU:0, one launch (start us, length us, event | category | flops | bytes accessed | tf_op | source)
XLA Modules:
  0.0 42.7 jit_solution(8863804918079898834)
XLA Ops:
  0.6 0.0 copy-start.4
  0.6 0.0 copy-start.3
  0.7 0.0 copy-start.2
  0.7 0.0 copy-start.1
  0.7 0.0 copy-start
  0.7 2.6 %edges.1 = (f32[2,8,64,128]{3,2,1,0:T(8,128)}, f32[64,128]{1,0:T(8,128)}, f32[64,128]{1,0:T(8,128)}, f32[64,1024]{1,0:T(8,128)}, f32[8,128]{1,0:T(8,128)}, /*index=5*/f32[8,128]{1,0:T(8,128)}) custom-call(s32[2,1,1024]{2,1,0:T(1,128)} %bitcast.2, f32[2,3,64,1024]{3,2,1,0:T(8,128)} %depth.1, s32[2,64,1024]{2,1,0:T(8,128)} %wet.1, f32[64,1024]{1,0:T(8,128)} %bed.1, ...), custom_call_target="tpu_custom_call" | custom-call | tf_op jit(solution)/shard_map/edges/pallas_call | solution.py:145
  3.3 3.0 %collective-permute-start = (f32[64,1024]{1,0:T(8,128)}, f32[64,1024]{1,0:T(8,128)S(1)}, u32[]{:S(2)}, u32[]{:S(2)}) collective-permute-start(f32[64,1024]{1,0:T(8,128)} %get-tuple-element.52), channel_id=1, source_target_pairs={{0,4},{4,0},{1,5},{5,1},{2,6},{6,2},{3,7},{7,3},{8,12},{12,8},{9,1... | collective-permute-start | bytes 786440 | tf_op jit(solution)/shard_map/ppermute | solution.py:28
  6.3 1.6 %collective-permute-start.1 = (f32[64,128]{1,0:T(8,128)}, f32[64,128]{1,0:T(8,128)S(1)}, u32[]{:S(2)}, u32[]{:S(2)}) collective-permute-start(f32[64,128]{1,0:T(8,128)} %get-tuple-element.53), channel_id=1, source_target_pairs={{0,1},{1,0},{2,3},{3,2},{4,5},{5,4},{6,7},{7,6},{8,9},{9,8},{10,11... | collective-permute-start | bytes 98312 | tf_op jit(solution)/shard_map/ppermute | solution.py:28
  7.9 0.7 %collective-permute-start.2 = (f32[64,128]{1,0:T(8,128)}, f32[64,128]{1,0:T(8,128)S(1)}, u32[]{:S(2)}, u32[]{:S(2)}) collective-permute-start(f32[64,128]{1,0:T(8,128)} %get-tuple-element.54), channel_id=1, source_target_pairs={{1,2},{2,1},{5,6},{6,5},{9,10},{10,9},{13,14},{14,13},{17,18},{18,... | collective-permute-start | bytes 98312 | tf_op jit(solution)/shard_map/ppermute | solution.py:28
  8.6 4.4 %collective-permute-start.3 = (f32[8,128]{1,0:T(8,128)}, f32[8,128]{1,0:T(8,128)S(1)}, u32[]{:S(2)}, u32[]{:S(2)}) collective-permute-start(f32[8,128]{1,0:T(8,128)} %get-tuple-element.55), channel_id=1, source_target_pairs={{0,5},{1,4},{2,7},{3,6},{4,1},{5,0},{6,3},{7,2},{8,13},{9,12},{10,... | collective-permute-start | bytes 12296 | tf_op jit(solution)/shard_map/ppermute | solution.py:165
  13.0 0.0 copy-start.5
  13.0 0.8 %collective-permute-start.4 = (f32[8,128]{1,0:T(8,128)}, f32[8,128]{1,0:T(8,128)S(1)}, u32[]{:S(2)}, u32[]{:S(2)}) collective-permute-start(f32[8,128]{1,0:T(8,128)} %get-tuple-element.56), channel_id=1, source_target_pairs={{1,6},{2,5},{5,2},{6,1},{9,14},{10,13},{13,10},{14,9},{17,22},{18,... | collective-permute-start | bytes 12296 | tf_op jit(solution)/shard_map/ppermute | solution.py:165
  13.7 0.0 copy-done.4
  13.8 0.0 copy-done.3
  13.8 0.0 copy-done.2
  13.8 0.0 copy-done.1
  13.8 0.0 copy-done
  13.8 3.9 %inner.1 = (f32[11,9,8,1024]{3,2,1,0:T(8,128)S(1)}, f32[2,2,8,8,1024]{4,3,2,1,0:T(8,128)S(1)}, f32[2,2,8,8,1024]{4,3,2,1,0:T(8,128)S(1)}, f32[2,3,8,8,1024]{4,3,...) custom-call(f32[2,3,64,1024]{3,2,1,0:T(8,128)S(1)} %copy-done, ...), custom_call_target="tpu_custom_call" | custom-call | flops 100000000 | bytes 16000000 | tf_op jit(solution)/shard_map/inner/pallas_call | solution.py:375
  17.8 0.0 collective-permute-done.3.corner_aa
  17.8 0.0 collective-permute-done.4.corner_ab
  17.8 0.0 collective-permute-done.1.side_a
  17.8 0.0 collective-permute-done.2.side_b
  17.8 0.0 collective-permute-done.refs_0_
  17.8 0.5 %row_rims.1 = (f32[13,8,1024]{2,1,0:T(8,128)S(1)}, f32[13,8,1024]{2,1,0:T(8,128)S(1)}) custom-call(f32[64,1024]{1,0:T(8,128)S(1)} %collective-permute-done.refs_0_), custom_call_target="tpu_custom_call" | custom-call | tf_op jit(solution)/shard_map/row_rims/pallas_call | solution.py:212
  18.3 0.0 copy-done.5
  18.3 5.3 %tangents.1 = (f32[8,128]{1,0:T(8,128)S(1)}, f32[2,13,8,1152]{3,2,1,0:T(8,128)S(1)}, f32[2,2,10,8,1152]{4,3,2,1,0:T(8,128)S(1)}, f32[2,2,10,8,1152]{4,3,2,1,0:T(...) custom-call(f32[11,9,8,1024]{3,2,1,0:T(8,128)S(1)} %get-tuple-elemen, ...), custom_call_target="tpu_custom_call" | custom-call | tf_op jit(solution)/shard_map/tangents/pallas_call | solution.py:583
  23.7 0.1 collective-permute-start.5
  23.7 1.2 %gradient.2 = (f32[10,8,1152]{2,1,0:T(8,128)S(1)}, f32[10,8,1152]{2,1,0:T(8,128)S(1)}) custom-call(f32[11,9,8,1024]{3,2,1,0:T(8,128)S(1)} %get-tuple-element.66.prim.m_c, f32[2,13,8,1152]{3,2,1,0:T(8,128)S(1)} %get-tuple-element.83.source, f32[2,2,10,8,1152]{4,3,2,1,0:T(8,128)S(1)} %get-tuple-element.84.a_x, ...), custom_call_target="tpu_custom_call" | custom-call | flops 40000000 | bytes 12000000 | tf_op jit(solution)/shard_map/gradient/pallas_call | solution.py:687
  25.0 0.0 collective-permute-done.5
  25.0 1.6 %collective-permute-start.6 = (f32[8,128]{1,0:T(8,128)S(1)}, f32[8,128]{1,0:T(8,128)S(1)}, u32[]{:S(2)}, u32[]{:S(2)}) collective-permute-start(f32[8,128]{1,0:T(8,128)S(1)} %add.15), channel_id=1, source_target_pairs={{0,16},{8,24},{16,0},{24,8},{1,17},{9,25},{17,1},{25,9},{2,18},{10... | collective-permute-start | bytes 12296 | tf_op jit(solution)/shard_map/ppermute | solution.py:714
  26.6 1.5 %gradient.3 = f32[64,1024]{1,0:T(8,128)S(1)} custom-call(f32[11,9,8,1024]{3,2,1,0:T(8,128)S(1)} %get-tuple-element.66.prim.m_c, f32[2,13,8,1152]{3,2,1,0:T(8,128)S(1)} %get-tuple-element.83.source, f32[2,2,10,8,1152]{4,3,2,1,0:T(8,128)S(1)} %get-tuple-element.84.a_x, f32[2,2,10,8,1152]{4,3,2,1,0:T(8,128)S(1)} %get-tuple-element.85.b_x, ...), custom_call_target="tpu_custom_call" | custom-call | flops 40000000 | bytes 12000000 | tf_op jit(solution)/shard_map/gradient/pallas_call | solution.py:687
  28.1 0.6 %collective-permute-done.6 = f32[8,128]{1,0:T(8,128)S(1)} collective-permute-done((f32[8,128]{1,0:T(8,128)S(1)}, f32[8,128]{1,0:T(8,128)S(1)}, u32[]{:S(2)}, u32[]{:S(2)}) %collective-permute-start.6) | collective-permute-done | bytes 4128 | tf_op jit(solution)/shard_map/ppermute | solution.py:714
  28.7 0.0 collective-permute-start.7
  28.7 1.5 %collective-permute-start.8 = (f32[8,128]{1,0:T(8,128)S(1)}, f32[8,128]{1,0:T(8,128)S(1)}, u32[]{:S(2)}, u32[]{:S(2)}) collective-permute-start(f32[8,128]{1,0:T(8,128)S(1)} %add.16), channel_id=1, source_target_pairs={{0,4},{4,0},{1,5},{5,1},{2,6},{6,2},{3,7},{7,3},{8,12},{12,8},{9,1... | collective-permute-start | bytes 12296 | tf_op jit(solution)/shard_map/ppermute | solution.py:714
  30.2 2.1 %collective-permute-done.8 = f32[8,128]{1,0:T(8,128)S(1)} collective-permute-done((f32[8,128]{1,0:T(8,128)S(1)}, f32[8,128]{1,0:T(8,128)S(1)}, u32[]{:S(2)}, u32[]{:S(2)}) %collective-permute-start.8) | collective-permute-done | bytes 4128 | tf_op jit(solution)/shard_map/ppermute | solution.py:714
  32.3 0.0 collective-permute-done.7
  32.3 1.6 %collective-permute-start.9 = (f32[64,1024]{1,0:T(8,128)S(1)}, f32[64,1024]{1,0:T(8,128)S(1)}, u32[]{:S(2)}, u32[]{:S(2)}) collective-permute-start(f32[64,1024]{1,0:T(8,128)S(1)} %add.17.grad), channel_id=1, source_target_pairs={{0,16},{8,24},{16,0},{24,8},{1,17},{9,25},{17,1},{25,9},{2,18},{10... | collective-permute-start | bytes 786440 | tf_op jit(solution)/shard_map/ppermute | solution.py:714
  33.9 2.0 %collective-permute-start.10 = (f32[8,128]{1,0:T(8,128)S(1)}, f32[8,128]{1,0:T(8,128)S(1)}, u32[]{:S(2)}, u32[]{:S(2)}) collective-permute-start(f32[8,128]{1,0:T(8,128)S(1)} %add.18), channel_id=1, source_target_pairs={{0,1},{1,0},{2,3},{3,2},{4,5},{5,4},{6,7},{7,6},{8,9},{9,8},{10,11... | collective-permute-start | bytes 12296 | tf_op jit(solution)/shard_map/ppermute | solution.py:714
  35.9 1.6 %collective-permute-done.10 = f32[8,128]{1,0:T(8,128)S(1)} collective-permute-done((f32[8,128]{1,0:T(8,128)S(1)}, f32[8,128]{1,0:T(8,128)S(1)}, u32[]{:S(2)}, u32[]{:S(2)}) %collective-permute-start.10) | collective-permute-done | bytes 4128 | tf_op jit(solution)/shard_map/ppermute | solution.py:714
  37.5 2.7 %collective-permute-start.11 = (f32[8,128]{1,0:T(8,128)S(1)}, f32[8,128]{1,0:T(8,128)S(1)}, u32[]{:S(2)}, u32[]{:S(2)}) collective-permute-start(f32[8,128]{1,0:T(8,128)S(1)} %add.19.curve), channel_id=1, source_target_pairs={{0,2},{1,3},{2,0},{3,1},{4,6},{5,7},{6,4},{7,5},{8,10},{9,11},{10,... | collective-permute-start | bytes 12296 | tf_op jit(solution)/shard_map/ppermute | solution.py:714
  40.2 1.8 %collective-permute-done.11.curve_arrived = f32[8,128]{1,0:T(8,128)S(1)} collective-permute-done((f32[8,128]{1,0:T(8,128)S(1)}, f32[8,128]{1,0:T(8,128)S(1)}, u32[]{:S(2)}, u32[]{:S(2)}) %collective-permute-start.11) | collective-permute-done | bytes 4128 | tf_op jit(solution)/shard_map/ppermute | solution.py:714
  42.0 0.0 collective-permute-done.9.arrived
  42.0 0.7 %finish.1 = (f32[64,1024]{1,0:T(8,128)}, f32[1,1]{1,0:T(1,128)}) custom-call(f32[64,1024]{1,0:T(8,128)S(1)} %add.17.grad, f32[64,1024]{1,0:T(8,128)S(1)} %collective-permute-done.9.arrived, f32[8,128]{1,0:T(8,128)S(1)} %add.19.curve, f32[8,128]{1,0:T(8,128)S(1)} %collective-permute-done.11.curve_arrived), custom_call_target="tpu_custom_call" | custom-call | tf_op jit(solution)/shard_map/finish/pallas_call | solution.py:728
  (6 shorter events, 0.1 us)
Async XLA Ops:
  0.6 13.1 %copy-start.4 = (f32[64,1024]{1,0:T(8,128)S(1)}, f32[64,1024]{1,0:T(8,128)}, u32[]{:S(2)}) copy-start(f32[64,1024]{1,0:T(8,128)} %direction.1) | copy-start | bytes 786436
  0.6 13.1 %copy-start.3 = (f32[64,1024]{1,0:T(8,128)S(1)}, f32[64,1024]{1,0:T(8,128)}, u32[]{:S(2)}) copy-start(f32[64,1024]{1,0:T(8,128)} %rough.1) | copy-start | bytes 786436
  0.7 13.1 %copy-start.2 = (f32[64,1024]{1,0:T(8,128)S(1)}, f32[64,1024]{1,0:T(8,128)}, u32[]{:S(2)}) copy-start(f32[64,1024]{1,0:T(8,128)} %bed.1) | copy-start | bytes 786436
  0.7 13.1 %copy-start.1 = (s32[2,64,1024]{2,1,0:T(8,128)S(1)}, s32[2,64,1024]{2,1,0:T(8,128)}, u32[]{:S(2)}) copy-start(s32[2,64,1024]{2,1,0:T(8,128)} %wet.1) | copy-start | bytes 1572868
  0.7 13.1 %copy-start = (f32[2,3,64,1024]{3,2,1,0:T(8,128)S(1)}, f32[2,3,64,1024]{3,2,1,0:T(8,128)}, u32[]{:S(2)}) copy-start(f32[2,3,64,1024]{3,2,1,0:T(8,128)} %depth.1) | copy-start | bytes 4718596
  3.3 14.5 %collective-permute-start = (f32[64,1024]{1,0:T(8,128)}, f32[64,1024]{1,0:T(8,128)S(1)}, u32[]{:S(2)}, u32[]{:S(2)}) collective-permute-start(f32[64,1024]{1,0:T(8,128)} %get-tuple-element.52), channel_id=1, source_target_pairs={{0,4},{4,0},{1,5},{5,1},{2,6},{6,2},{3,7},{7,3},{8,12},{12,8},{9,1... | collective-permute-start | bytes 786440 | tf_op jit(solution)/shard_map/ppermute | solution.py:28
  6.3 11.5 %collective-permute-start.1 = (f32[64,128]{1,0:T(8,128)}, f32[64,128]{1,0:T(8,128)S(1)}, u32[]{:S(2)}, u32[]{:S(2)}) collective-permute-start(f32[64,128]{1,0:T(8,128)} %get-tuple-element.53), channel_id=1, source_target_pairs={{0,1},{1,0},{2,3},{3,2},{4,5},{5,4},{6,7},{7,6},{8,9},{9,8},{10,11... | collective-permute-start | bytes 98312 | tf_op jit(solution)/shard_map/ppermute | solution.py:28
  7.9 9.9 %collective-permute-start.2 = (f32[64,128]{1,0:T(8,128)}, f32[64,128]{1,0:T(8,128)S(1)}, u32[]{:S(2)}, u32[]{:S(2)}) collective-permute-start(f32[64,128]{1,0:T(8,128)} %get-tuple-element.54), channel_id=1, source_target_pairs={{1,2},{2,1},{5,6},{6,5},{9,10},{10,9},{13,14},{14,13},{17,18},{18,... | collective-permute-start | bytes 98312 | tf_op jit(solution)/shard_map/ppermute | solution.py:28
  8.6 9.2 %collective-permute-start.3 = (f32[8,128]{1,0:T(8,128)}, f32[8,128]{1,0:T(8,128)S(1)}, u32[]{:S(2)}, u32[]{:S(2)}) collective-permute-start(f32[8,128]{1,0:T(8,128)} %get-tuple-element.55), channel_id=1, source_target_pairs={{0,5},{1,4},{2,7},{3,6},{4,1},{5,0},{6,3},{7,2},{8,13},{9,12},{10,... | collective-permute-start | bytes 12296 | tf_op jit(solution)/shard_map/ppermute | solution.py:165
  13.0 5.4 %copy-start.5 = (f32[2,8,64,128]{3,2,1,0:T(8,128)S(1)}, f32[2,8,64,128]{3,2,1,0:T(8,128)}, u32[]{:S(2)}) copy-start(f32[2,8,64,128]{3,2,1,0:T(8,128)} %get-tuple-element.67.cnt) | copy-start | bytes 1572868
  13.0 4.8 %collective-permute-start.4 = (f32[8,128]{1,0:T(8,128)}, f32[8,128]{1,0:T(8,128)S(1)}, u32[]{:S(2)}, u32[]{:S(2)}) collective-permute-start(f32[8,128]{1,0:T(8,128)} %get-tuple-element.56), channel_id=1, source_target_pairs={{1,6},{2,5},{5,2},{6,1},{9,14},{10,13},{13,10},{14,9},{17,22},{18,... | collective-permute-start | bytes 12296 | tf_op jit(solution)/shard_map/ppermute | solution.py:165
  23.7 1.3 %collective-permute-start.5 = (f32[8,128]{1,0:T(8,128)S(1)}, f32[8,128]{1,0:T(8,128)S(1)}, u32[]{:S(2)}, u32[]{:S(2)}) collective-permute-start(f32[8,128]{1,0:T(8,128)S(1)} %get-tuple-element.92), channel_id=1, source_target_pairs={{0,8},{8,0},{16,24},{24,16},{1,9},{9,1},{17,25},{25,17},{2,10},{10... | collective-permute-start | bytes 12296 | tf_op jit(solution)/shard_map/ppermute | solution.py:714
  25.0 3.7 %collective-permute-start.6 = (f32[8,128]{1,0:T(8,128)S(1)}, f32[8,128]{1,0:T(8,128)S(1)}, u32[]{:S(2)}, u32[]{:S(2)}) collective-permute-start(f32[8,128]{1,0:T(8,128)S(1)} %add.15), channel_id=1, source_target_pairs={{0,16},{8,24},{16,0},{24,8},{1,17},{9,25},{17,1},{25,9},{2,18},{10... | collective-permute-start | bytes 12296 | tf_op jit(solution)/shard_map/ppermute | solution.py:714
  28.7 3.6 %collective-permute-start.7 = (f32[64,1024]{1,0:T(8,128)S(1)}, f32[64,1024]{1,0:T(8,128)S(1)}, u32[]{:S(2)}, u32[]{:S(2)}) collective-permute-start(f32[64,1024]{1,0:T(8,128)S(1)} %gradient.3), channel_id=1, source_target_pairs={{0,8},{8,0},{16,24},{24,16},{1,9},{9,1},{17,25},{25,17},{2,10},{10... | collective-permute-start | bytes 786440 | tf_op jit(solution)/shard_map/ppermute | solution.py:714
  28.7 3.6 %collective-permute-start.8 = (f32[8,128]{1,0:T(8,128)S(1)}, f32[8,128]{1,0:T(8,128)S(1)}, u32[]{:S(2)}, u32[]{:S(2)}) collective-permute-start(f32[8,128]{1,0:T(8,128)S(1)} %add.16), channel_id=1, source_target_pairs={{0,4},{4,0},{1,5},{5,1},{2,6},{6,2},{3,7},{7,3},{8,12},{12,8},{9,1... | collective-permute-start | bytes 12296 | tf_op jit(solution)/shard_map/ppermute | solution.py:714
  32.3 9.7 %collective-permute-start.9 = (f32[64,1024]{1,0:T(8,128)S(1)}, f32[64,1024]{1,0:T(8,128)S(1)}, u32[]{:S(2)}, u32[]{:S(2)}) collective-permute-start(f32[64,1024]{1,0:T(8,128)S(1)} %add.17.grad), channel_id=1, source_target_pairs={{0,16},{8,24},{16,0},{24,8},{1,17},{9,25},{17,1},{25,9},{2,18},{10... | collective-permute-start | bytes 786440 | tf_op jit(solution)/shard_map/ppermute | solution.py:714
  33.9 3.6 %collective-permute-start.10 = (f32[8,128]{1,0:T(8,128)S(1)}, f32[8,128]{1,0:T(8,128)S(1)}, u32[]{:S(2)}, u32[]{:S(2)}) collective-permute-start(f32[8,128]{1,0:T(8,128)S(1)} %add.18), channel_id=1, source_target_pairs={{0,1},{1,0},{2,3},{3,2},{4,5},{5,4},{6,7},{7,6},{8,9},{9,8},{10,11... | collective-permute-start | bytes 12296 | tf_op jit(solution)/shard_map/ppermute | solution.py:714
  37.5 4.5 %collective-permute-start.11 = (f32[8,128]{1,0:T(8,128)S(1)}, f32[8,128]{1,0:T(8,128)S(1)}, u32[]{:S(2)}, u32[]{:S(2)}) collective-permute-start(f32[8,128]{1,0:T(8,128)S(1)} %add.19.curve), channel_id=1, source_target_pairs={{0,2},{1,3},{2,0},{3,1},{4,6},{5,7},{6,4},{7,5},{8,10},{9,11},{10,... | collective-permute-start | bytes 12296 | tf_op jit(solution)/shard_map/ppermute | solution.py:714

commit v6 on v5

--- a/solution.py
+++ b/solution.py
@@ -34,7 +34,7 @@
 
 def plan(events, steps):
     out, slot = [], 0
-    for n in [REACH - t for _ in range(events) for t in range(steps)] + [REACH] * (events + 3) + [1] * events:
+    for n in [REACH - t for _ in range(events) for t in range(steps)] + [REACH] * (events + 3) + [REACH // 2] * events:
         out.append((n, slot))
         slot += n
     return out, -(-slot // SUB)
@@ -99,7 +99,10 @@
         d, w, b, r, v = rest[5 * k : 5 * k + 5]
         fields = [d[e, t] for e in range(events) for t in range(steps)]
         fields += [w[e].astype(jnp.float32) for e in range(events)] + [b[...], r[...], v[...]]
-        fields += [jnp.broadcast_to(cells[e].astype(jnp.float32), (SUB, cols)) for e in range(events)]
+        fields += [
+            jnp.concatenate([cnt[e, j, pl.ds(edges[k][1], SUB), :] for j in range(cols // LANES)], axis=1)
+            for e in range(events)
+        ]
         tiles = [jnp.zeros((SUB, cols), jnp.float32)] * count
         for x, (n, slot) in zip(fields, slots):
             if 1 < n < SUB:
@@ -165,14 +168,13 @@
     return lax.ppermute(x, ("row", "col"), perm)
 
 
-def rim_kernel(sides, events, steps, rows, *refs):
+def rim_kernel(sides, events, steps, *refs):
     rims_in = refs[:sides]
     rim_top, rim_bottom = refs[sides:]
     cols = rim_top.shape[-1]
     even_row = lax.axis_index("row") % 2 == 0
     sub = lax.broadcasted_iota(jnp.int32, (SUB, cols), 0)
     slots, _ = plan(events, steps)
-    base = events * (steps + 1) + 3
     nothing = jnp.zeros((SUB, cols), jnp.float32)
 
     def field(ref, n, slot):
@@ -184,33 +186,18 @@
             x = jnp.where((sub >= -low) & (sub < min(n, SUB - low)) & (sub >= max(0, -low)), y, x)
         return x
 
-    for f in range(base):
-        n, slot = slots[f]
+    for f, (n, slot) in enumerate(slots):
         x = field(rims_in[0], n, slot)
         y = field(rims_in[1], n, slot) if sides > 1 else nothing
         rim_bottom[f] = jnp.where(even_row, x, y)
         rim_top[f] = pltpu.roll(jnp.where(even_row, y, x), SUB - n, 0)
-    for e in range(events):
-        slot = slots[base + e][1]
-        for k in range(2):
-            lower = even_row if k == 0 else jnp.logical_not(even_row)
-            if k < sides:
-                g = rims_in[k][slot : slot + 1].astype(jnp.int32)
-                row = g // cols - jnp.where(lower, 0, rows - SUB)
-                hits = jnp.concatenate(tally_of(row, g % cols, SUB, cols), axis=1)
-            else:
-                hits = nothing
-            if k == 0:
-                first = hits
-        rim_bottom[base + e] = jnp.where(even_row, first, hits)
-        rim_top[base + e] = jnp.where(even_row, hits, first)
-
-
-def row_rims(rims, events, steps, rows):
+
+
+def row_rims(rims, events, steps):
     vmem = pl.BlockSpec(memory_space=pltpu.VMEM)
     rim = jax.ShapeDtypeStruct((events * (steps + 2) + 3, SUB, rims[0].shape[-1]), jnp.float32)
     return pl.pallas_call(
-        functools.partial(rim_kernel, len(rims), events, steps, rows),
+        functools.partial(rim_kernel, len(rims), events, steps),
         in_specs=[vmem] * len(rims),
         out_specs=[vmem] * 2,
         out_shape=[rim] * 2,
@@ -346,7 +333,7 @@
     def _(e):
         for t in range(steps):
 
-            @pl.loop(0, deep, unroll=4)
+            @pl.loop(0, deep, unroll=deep)
             def _(i):
                 k = 3 + events + e * steps + t
                 h = get(prim, k, i)
@@ -749,7 +736,7 @@
     rims, side_a, side_b, corners, block = lax.optimization_barrier((rims, side_a, side_b, corners, block))
     if sides == 1:
         corners = corners + [jnp.zeros_like(x) for x in corners]
-    rim_top, rim_bottom = row_rims(rims, events, steps, rows)
+    rim_top, rim_bottom = row_rims(rims, events, steps)
     curve, *coefficients = tangents(block[0], counts, *block[1:], rim_top, rim_bottom, side_a, side_b, *corners)
     hops = hops_over("event") + hops_over("row") + hops_over("col")
     sums = ()

time: 42.9 us -> 42.5 us (level)
  Pallas kernels: 15.8 us -> 15.3 us
where the time goes in v6:
time: 42.5 us; the launch traced here: 42.3 us
  starting transfers between devices  19.9 us (47%)
  Pallas kernels  15.3 us (36%)
  waiting for transfers between devices  6.15 us (14%)
  between operations  0.85 us (2%)
    ppermute x7, starting transfers between devices, from_hop(): lax.ppermute(x, axis, [(i, i ^ hop) for i in range(lax.axis_size(axis))])  9.47 us
    ppermute x7, waiting for transfers between devices, from_hop(): lax.ppermute(x, axis, [(i, i ^ hop) for i in range(lax.axis_size(axis))])  6.13 us
    pallas_call x1, Pallas kernels, tangents(): pl.pallas_call(tangent_kernel, in_specs=[vmem] * (2 + len(more_inputs)),...  5.34 us
    ppermute x3, starting transfers between devices, exchange(): return lax.ppermute(x, axis, perm) if perm else None  5.26 us
    ppermute x2, starting transfers between devices, diagonal(): return lax.ppermute(x, ('row', 'col'), perm)  5.19 us
    pallas_call x1, Pallas kernels, inner(): pl.pallas_call(inner_kernel, in_specs=[vmem] * 5, out_specs=[vmem] * 9, o...  3.82 us
    pallas_call x2, Pallas kernels, gradient(): pl.pallas_call(functools.partial(adjoint_kernel, first, last), grid=(1,),...  2.75 us
    pallas_call x1, Pallas kernels, edges_and_gauges(): pl.pallas_call(functools.partial(edge_kernel, sides), in_specs=[anywhere]...  2.59 us
  transfers between devices with their start and end apart: 12, of which 4 were waited for; matrix products, arithmetic and copies ran while one was open for 0% of the time, Pallas kernels for 16%

profile of v6, /device:TPU:0, one launch (start us, length us, event | category | flops | bytes accessed | tf_op | source)
XLA Modules:
  0.0 42.3 jit_solution(15527741852713446126)
XLA Ops:
  0.6 0.0 copy-start.4
  0.6 0.0 copy-start.3
  0.7 0.0 copy-start.2
  0.7 0.0 copy-start.1
  0.7 0.0 copy-start
  0.7 2.6 %edges.1 = (f32[2,8,64,128]{3,2,1,0:T(8,128)}, f32[64,128]{1,0:T(8,128)}, f32[64,128]{1,0:T(8,128)}, f32[72,1024]{1,0:T(8,128)}, f32[8,128]{1,0:T(8,128)}, /*index=5*/f32[8,128]{1,0:T(8,128)}) custom-call(s32[2,1,1024]{2,1,0:T(1,128)} %bitcast.2, f32[2,3,64,1024]{3,2,1,0:T(8,128)} %depth.1, s32[2,64,1024]{2,1,0:T(8,128)} %wet.1, f32[64,1024]{1,0:T(8,128)} %bed.1, ...), custom_call_target="tpu_custom_call" | custom-call | tf_op jit(solution)/shard_map/edges/pallas_call | solution.py:148
  3.3 3.0 %collective-permute-start = (f32[72,1024]{1,0:T(8,128)}, f32[72,1024]{1,0:T(8,128)S(1)}, u32[]{:S(2)}, u32[]{:S(2)}) collective-permute-start(f32[72,1024]{1,0:T(8,128)} %get-tuple-element.52), channel_id=1, source_target_pairs={{0,4},{4,0},{1,5},{5,1},{2,6},{6,2},{3,7},{7,3},{8,12},{12,8},{9,1... | collective-permute-start | bytes 884744 | tf_op jit(solution)/shard_map/ppermute | solution.py:28
  6.3 1.6 %collective-permute-start.1 = (f32[64,128]{1,0:T(8,128)}, f32[64,128]{1,0:T(8,128)S(1)}, u32[]{:S(2)}, u32[]{:S(2)}) collective-permute-start(f32[64,128]{1,0:T(8,128)} %get-tuple-element.53), channel_id=1, source_target_pairs={{0,1},{1,0},{2,3},{3,2},{4,5},{5,4},{6,7},{7,6},{8,9},{9,8},{10,11... | collective-permute-start | bytes 98312 | tf_op jit(solution)/shard_map/ppermute | solution.py:28
  7.9 0.7 %collective-permute-start.2 = (f32[64,128]{1,0:T(8,128)}, f32[64,128]{1,0:T(8,128)S(1)}, u32[]{:S(2)}, u32[]{:S(2)}) collective-permute-start(f32[64,128]{1,0:T(8,128)} %get-tuple-element.54), channel_id=1, source_target_pairs={{1,2},{2,1},{5,6},{6,5},{9,10},{10,9},{13,14},{14,13},{17,18},{18,... | collective-permute-start | bytes 98312 | tf_op jit(solution)/shard_map/ppermute | solution.py:28
  8.6 4.4 %collective-permute-start.3 = (f32[8,128]{1,0:T(8,128)}, f32[8,128]{1,0:T(8,128)S(1)}, u32[]{:S(2)}, u32[]{:S(2)}) collective-permute-start(f32[8,128]{1,0:T(8,128)} %get-tuple-element.55), channel_id=1, source_target_pairs={{0,5},{1,4},{2,7},{3,6},{4,1},{5,0},{6,3},{7,2},{8,13},{9,12},{10,... | collective-permute-start | bytes 12296 | tf_op jit(solution)/shard_map/ppermute | solution.py:168
  13.0 0.0 copy-start.5
  13.0 0.8 %collective-permute-start.4 = (f32[8,128]{1,0:T(8,128)}, f32[8,128]{1,0:T(8,128)S(1)}, u32[]{:S(2)}, u32[]{:S(2)}) collective-permute-start(f32[8,128]{1,0:T(8,128)} %get-tuple-element.56), channel_id=1, source_target_pairs={{1,6},{2,5},{5,2},{6,1},{9,14},{10,13},{13,10},{14,9},{17,22},{18,... | collective-permute-start | bytes 12296 | tf_op jit(solution)/shard_map/ppermute | solution.py:168
  13.7 0.0 copy-done.4
  13.8 0.0 copy-done.3
  13.8 0.0 copy-done.2
  13.8 0.0 copy-done.1
  13.8 0.0 copy-done
  13.8 3.8 %inner.1 = (f32[11,9,8,1024]{3,2,1,0:T(8,128)S(1)}, f32[2,2,8,8,1024]{4,3,2,1,0:T(8,128)S(1)}, f32[2,2,8,8,1024]{4,3,2,1,0:T(8,128)S(1)}, f32[2,3,8,8,1024]{4,3,...) custom-call(f32[2,3,64,1024]{3,2,1,0:T(8,128)S(1)} %copy-done, ...), custom_call_target="tpu_custom_call" | custom-call | flops 100000000 | bytes 16000000 | tf_op jit(solution)/shard_map/inner/pallas_call | solution.py:362
  17.6 0.0 collective-permute-done.3.corner_aa
  17.6 0.0 collective-permute-done.4.corner_ab
  17.6 0.0 collective-permute-done.1.side_a
  17.7 0.0 collective-permute-done.2.side_b
  17.7 0.0 collective-permute-done.refs_0_
  17.7 0.1 row_rims.1
  17.8 0.0 copy-done.5
  17.8 5.3 %tangents.1 = (f32[8,128]{1,0:T(8,128)S(1)}, f32[2,13,8,1152]{3,2,1,0:T(8,128)S(1)}, f32[2,2,10,8,1152]{4,3,2,1,0:T(8,128)S(1)}, f32[2,2,10,8,1152]{4,3,2,1,0:T(...) custom-call(f32[11,9,8,1024]{3,2,1,0:T(8,128)S(1)} %get-tuple-elemen, ...), custom_call_target="tpu_custom_call" | custom-call | tf_op jit(solution)/shard_map/tangents/pallas_call | solution.py:570
  23.1 0.1 collective-permute-start.5
  23.2 1.2 %gradient.2 = (f32[10,8,1152]{2,1,0:T(8,128)S(1)}, f32[10,8,1152]{2,1,0:T(8,128)S(1)}) custom-call(f32[11,9,8,1024]{3,2,1,0:T(8,128)S(1)} %get-tuple-element.66.prim.m_c, f32[2,13,8,1152]{3,2,1,0:T(8,128)S(1)} %get-tuple-element.83.source, f32[2,2,10,8,1152]{4,3,2,1,0:T(8,128)S(1)} %get-tuple-element.84.a_x, ...), custom_call_target="tpu_custom_call" | custom-call | flops 40000000 | bytes 12000000 | tf_op jit(solution)/shard_map/gradient/pallas_call | solution.py:674
  24.5 0.0 collective-permute-done.5
  24.5 1.6 %collective-permute-start.6 = (f32[8,128]{1,0:T(8,128)S(1)}, f32[8,128]{1,0:T(8,128)S(1)}, u32[]{:S(2)}, u32[]{:S(2)}) collective-permute-start(f32[8,128]{1,0:T(8,128)S(1)} %add.15), channel_id=1, source_target_pairs={{0,16},{8,24},{16,0},{24,8},{1,17},{9,25},{17,1},{25,9},{2,18},{10... | collective-permute-start | bytes 12296 | tf_op jit(solution)/shard_map/ppermute | solution.py:701
  26.0 1.5 %gradient.3 = f32[64,1024]{1,0:T(8,128)S(1)} custom-call(f32[11,9,8,1024]{3,2,1,0:T(8,128)S(1)} %get-tuple-element.66.prim.m_c, f32[2,13,8,1152]{3,2,1,0:T(8,128)S(1)} %get-tuple-element.83.source, f32[2,2,10,8,1152]{4,3,2,1,0:T(8,128)S(1)} %get-tuple-element.84.a_x, f32[2,2,10,8,1152]{4,3,2,1,0:T(8,128)S(1)} %get-tuple-element.85.b_x, ...), custom_call_target="tpu_custom_call" | custom-call | flops 40000000 | bytes 12000000 | tf_op jit(solution)/shard_map/gradient/pallas_call | solution.py:674
  27.6 0.6 %collective-permute-done.6 = f32[8,128]{1,0:T(8,128)S(1)} collective-permute-done((f32[8,128]{1,0:T(8,128)S(1)}, f32[8,128]{1,0:T(8,128)S(1)}, u32[]{:S(2)}, u32[]{:S(2)}) %collective-permute-start.6) | collective-permute-done | bytes 4128 | tf_op jit(solution)/shard_map/ppermute | solution.py:701
  28.1 0.0 collective-permute-start.7
  28.2 1.5 %collective-permute-start.8 = (f32[8,128]{1,0:T(8,128)S(1)}, f32[8,128]{1,0:T(8,128)S(1)}, u32[]{:S(2)}, u32[]{:S(2)}) collective-permute-start(f32[8,128]{1,0:T(8,128)S(1)} %add.16), channel_id=1, source_target_pairs={{0,4},{4,0},{1,5},{5,1},{2,6},{6,2},{3,7},{7,3},{8,12},{12,8},{9,1... | collective-permute-start | bytes 12296 | tf_op jit(solution)/shard_map/ppermute | solution.py:701
  29.7 2.1 %collective-permute-done.8 = f32[8,128]{1,0:T(8,128)S(1)} collective-permute-done((f32[8,128]{1,0:T(8,128)S(1)}, f32[8,128]{1,0:T(8,128)S(1)}, u32[]{:S(2)}, u32[]{:S(2)}) %collective-permute-start.8) | collective-permute-done | bytes 4128 | tf_op jit(solution)/shard_map/ppermute | solution.py:701
  31.8 0.0 collective-permute-done.7
  31.8 1.6 %collective-permute-start.9 = (f32[64,1024]{1,0:T(8,128)S(1)}, f32[64,1024]{1,0:T(8,128)S(1)}, u32[]{:S(2)}, u32[]{:S(2)}) collective-permute-start(f32[64,1024]{1,0:T(8,128)S(1)} %add.17.grad), channel_id=1, source_target_pairs={{0,16},{8,24},{16,0},{24,8},{1,17},{9,25},{17,1},{25,9},{2,18},{10... | collective-permute-start | bytes 786440 | tf_op jit(solution)/shard_map/ppermute | solution.py:701
  33.4 2.1 %collective-permute-start.10 = (f32[8,128]{1,0:T(8,128)S(1)}, f32[8,128]{1,0:T(8,128)S(1)}, u32[]{:S(2)}, u32[]{:S(2)}) collective-permute-start(f32[8,128]{1,0:T(8,128)S(1)} %add.18), channel_id=1, source_target_pairs={{0,1},{1,0},{2,3},{3,2},{4,5},{5,4},{6,7},{7,6},{8,9},{9,8},{10,11... | collective-permute-start | bytes 12296 | tf_op jit(solution)/shard_map/ppermute | solution.py:701
  35.5 1.6 %collective-permute-done.10 = f32[8,128]{1,0:T(8,128)S(1)} collective-permute-done((f32[8,128]{1,0:T(8,128)S(1)}, f32[8,128]{1,0:T(8,128)S(1)}, u32[]{:S(2)}, u32[]{:S(2)}) %collective-permute-start.10) | collective-permute-done | bytes 4128 | tf_op jit(solution)/shard_map/ppermute | solution.py:701
  37.1 2.6 %collective-permute-start.11 = (f32[8,128]{1,0:T(8,128)S(1)}, f32[8,128]{1,0:T(8,128)S(1)}, u32[]{:S(2)}, u32[]{:S(2)}) collective-permute-start(f32[8,128]{1,0:T(8,128)S(1)} %add.19.curve), channel_id=1, source_target_pairs={{0,2},{1,3},{2,0},{3,1},{4,6},{5,7},{6,4},{7,5},{8,10},{9,11},{10,... | collective-permute-start | bytes 12296 | tf_op jit(solution)/shard_map/ppermute | solution.py:701
  39.7 1.9 %collective-permute-done.11.curve_arrived = f32[8,128]{1,0:T(8,128)S(1)} collective-permute-done((f32[8,128]{1,0:T(8,128)S(1)}, f32[8,128]{1,0:T(8,128)S(1)}, u32[]{:S(2)}, u32[]{:S(2)}) %collective-permute-start.11) | collective-permute-done | bytes 4128 | tf_op jit(solution)/shard_map/ppermute | solution.py:701
  41.6 0.0 collective-permute-done.9.arrived
  41.6 0.7 %finish.1 = (f32[64,1024]{1,0:T(8,128)}, f32[1,1]{1,0:T(1,128)}) custom-call(f32[64,1024]{1,0:T(8,128)S(1)} %add.17.grad, f32[64,1024]{1,0:T(8,128)S(1)} %collective-permute-done.9.arrived, f32[8,128]{1,0:T(8,128)S(1)} %add.19.curve, f32[8,128]{1,0:T(8,128)S(1)} %collective-permute-done.11.curve_arrived), custom_call_target="tpu_custom_call" | custom-call | tf_op jit(solution)/shard_map/finish/pallas_call | solution.py:715
  (6 shorter events, 0.1 us)
Async XLA Ops:
  0.6 13.1 %copy-start.4 = (f32[64,1024]{1,0:T(8,128)S(1)}, f32[64,1024]{1,0:T(8,128)}, u32[]{:S(2)}) copy-start(f32[64,1024]{1,0:T(8,128)} %direction.1) | copy-start | bytes 786436
  0.6 13.1 %copy-start.3 = (f32[64,1024]{1,0:T(8,128)S(1)}, f32[64,1024]{1,0:T(8,128)}, u32[]{:S(2)}) copy-start(f32[64,1024]{1,0:T(8,128)} %rough.1) | copy-start | bytes 786436
  0.7 13.1 %copy-start.2 = (f32[64,1024]{1,0:T(8,128)S(1)}, f32[64,1024]{1,0:T(8,128)}, u32[]{:S(2)}) copy-start(f32[64,1024]{1,0:T(8,128)} %bed.1) | copy-start | bytes 786436
  0.7 13.1 %copy-start.1 = (s32[2,64,1024]{2,1,0:T(8,128)S(1)}, s32[2,64,1024]{2,1,0:T(8,128)}, u32[]{:S(2)}) copy-start(s32[2,64,1024]{2,1,0:T(8,128)} %wet.1) | copy-start | bytes 1572868
  0.7 13.1 %copy-start = (f32[2,3,64,1024]{3,2,1,0:T(8,128)S(1)}, f32[2,3,64,1024]{3,2,1,0:T(8,128)}, u32[]{:S(2)}) copy-start(f32[2,3,64,1024]{3,2,1,0:T(8,128)} %depth.1) | copy-start | bytes 4718596
  3.3 14.4 %collective-permute-start = (f32[72,1024]{1,0:T(8,128)}, f32[72,1024]{1,0:T(8,128)S(1)}, u32[]{:S(2)}, u32[]{:S(2)}) collective-permute-start(f32[72,1024]{1,0:T(8,128)} %get-tuple-element.52), channel_id=1, source_target_pairs={{0,4},{4,0},{1,5},{5,1},{2,6},{6,2},{3,7},{7,3},{8,12},{12,8},{9,1... | collective-permute-start | bytes 884744 | tf_op jit(solution)/shard_map/ppermute | solution.py:28
  6.3 11.3 %collective-permute-start.1 = (f32[64,128]{1,0:T(8,128)}, f32[64,128]{1,0:T(8,128)S(1)}, u32[]{:S(2)}, u32[]{:S(2)}) collective-permute-start(f32[64,128]{1,0:T(8,128)} %get-tuple-element.53), channel_id=1, source_target_pairs={{0,1},{1,0},{2,3},{3,2},{4,5},{5,4},{6,7},{7,6},{8,9},{9,8},{10,11... | collective-permute-start | bytes 98312 | tf_op jit(solution)/shard_map/ppermute | solution.py:28
  7.9 9.8 %collective-permute-start.2 = (f32[64,128]{1,0:T(8,128)}, f32[64,128]{1,0:T(8,128)S(1)}, u32[]{:S(2)}, u32[]{:S(2)}) collective-permute-start(f32[64,128]{1,0:T(8,128)} %get-tuple-element.54), channel_id=1, source_target_pairs={{1,2},{2,1},{5,6},{6,5},{9,10},{10,9},{13,14},{14,13},{17,18},{18,... | collective-permute-start | bytes 98312 | tf_op jit(solution)/shard_map/ppermute | solution.py:28
  8.6 9.1 %collective-permute-start.3 = (f32[8,128]{1,0:T(8,128)}, f32[8,128]{1,0:T(8,128)S(1)}, u32[]{:S(2)}, u32[]{:S(2)}) collective-permute-start(f32[8,128]{1,0:T(8,128)} %get-tuple-element.55), channel_id=1, source_target_pairs={{0,5},{1,4},{2,7},{3,6},{4,1},{5,0},{6,3},{7,2},{8,13},{9,12},{10,... | collective-permute-start | bytes 12296 | tf_op jit(solution)/shard_map/ppermute | solution.py:168
  13.0 4.8 %copy-start.5 = (f32[2,8,64,128]{3,2,1,0:T(8,128)S(1)}, f32[2,8,64,128]{3,2,1,0:T(8,128)}, u32[]{:S(2)}) copy-start(f32[2,8,64,128]{3,2,1,0:T(8,128)} %get-tuple-element.67.cnt) | copy-start | bytes 1572868
  13.0 4.7 %collective-permute-start.4 = (f32[8,128]{1,0:T(8,128)}, f32[8,128]{1,0:T(8,128)S(1)}, u32[]{:S(2)}, u32[]{:S(2)}) collective-permute-start(f32[8,128]{1,0:T(8,128)} %get-tuple-element.56), channel_id=1, source_target_pairs={{1,6},{2,5},{5,2},{6,1},{9,14},{10,13},{13,10},{14,9},{17,22},{18,... | collective-permute-start | bytes 12296 | tf_op jit(solution)/shard_map/ppermute | solution.py:168
  23.1 1.3 %collective-permute-start.5 = (f32[8,128]{1,0:T(8,128)S(1)}, f32[8,128]{1,0:T(8,128)S(1)}, u32[]{:S(2)}, u32[]{:S(2)}) collective-permute-start(f32[8,128]{1,0:T(8,128)S(1)} %get-tuple-element.92), channel_id=1, source_target_pairs={{0,8},{8,0},{16,24},{24,16},{1,9},{9,1},{17,25},{25,17},{2,10},{10... | collective-permute-start | bytes 12296 | tf_op jit(solution)/shard_map/ppermute | solution.py:701
  24.5 3.7 %collective-permute-start.6 = (f32[8,128]{1,0:T(8,128)S(1)}, f32[8,128]{1,0:T(8,128)S(1)}, u32[]{:S(2)}, u32[]{:S(2)}) collective-permute-start(f32[8,128]{1,0:T(8,128)S(1)} %add.15), channel_id=1, source_target_pairs={{0,16},{8,24},{16,0},{24,8},{1,17},{9,25},{17,1},{25,9},{2,18},{10... | collective-permute-start | bytes 12296 | tf_op jit(solution)/shard_map/ppermute | solution.py:701
  28.1 3.6 %collective-permute-start.7 = (f32[64,1024]{1,0:T(8,128)S(1)}, f32[64,1024]{1,0:T(8,128)S(1)}, u32[]{:S(2)}, u32[]{:S(2)}) collective-permute-start(f32[64,1024]{1,0:T(8,128)S(1)} %gradient.3), channel_id=1, source_target_pairs={{0,8},{8,0},{16,24},{24,16},{1,9},{9,1},{17,25},{25,17},{2,10},{10... | collective-permute-start | bytes 786440 | tf_op jit(solution)/shard_map/ppermute | solution.py:701
  28.2 3.6 %collective-permute-start.8 = (f32[8,128]{1,0:T(8,128)S(1)}, f32[8,128]{1,0:T(8,128)S(1)}, u32[]{:S(2)}, u32[]{:S(2)}) collective-permute-start(f32[8,128]{1,0:T(8,128)S(1)} %add.16), channel_id=1, source_target_pairs={{0,4},{4,0},{1,5},{5,1},{2,6},{6,2},{3,7},{7,3},{8,12},{12,8},{9,1... | collective-permute-start | bytes 12296 | tf_op jit(solution)/shard_map/ppermute | solution.py:701
  31.8 9.8 %collective-permute-start.9 = (f32[64,1024]{1,0:T(8,128)S(1)}, f32[64,1024]{1,0:T(8,128)S(1)}, u32[]{:S(2)}, u32[]{:S(2)}) collective-permute-start(f32[64,1024]{1,0:T(8,128)S(1)} %add.17.grad), channel_id=1, source_target_pairs={{0,16},{8,24},{16,0},{24,8},{1,17},{9,25},{17,1},{25,9},{2,18},{10... | collective-permute-start | bytes 786440 | tf_op jit(solution)/shard_map/ppermute | solution.py:701
  33.4 3.7 %collective-permute-start.10 = (f32[8,128]{1,0:T(8,128)S(1)}, f32[8,128]{1,0:T(8,128)S(1)}, u32[]{:S(2)}, u32[]{:S(2)}) collective-permute-start(f32[8,128]{1,0:T(8,128)S(1)} %add.18), channel_id=1, source_target_pairs={{0,1},{1,0},{2,3},{3,2},{4,5},{5,4},{6,7},{7,6},{8,9},{9,8},{10,11... | collective-permute-start | bytes 12296 | tf_op jit(solution)/shard_map/ppermute | solution.py:701
  37.1 4.5 %collective-permute-start.11 = (f32[8,128]{1,0:T(8,128)S(1)}, f32[8,128]{1,0:T(8,128)S(1)}, u32[]{:S(2)}, u32[]{:S(2)}) collective-permute-start(f32[8,128]{1,0:T(8,128)S(1)} %add.19.curve), channel_id=1, source_target_pairs={{0,2},{1,3},{2,0},{3,1},{4,6},{5,7},{6,4},{7,5},{8,10},{9,11},{10,... | collective-permute-start | bytes 12296 | tf_op jit(solution)/shard_map/ppermute | solution.py:701

commit v7 on v6

--- a/solution.py
+++ b/solution.py
@@ -279,12 +279,11 @@
     p = cond * (jnp.exp2((2.0 / 3.0 / LN2) * jnp.log(hs)) * (y * lax.rsqrt(y)))
     ps = p * s
     t = p * hs
-    A = (5.0 / 3.0) * ps
-    B = t * (0.5 + (0.5 * slope_floor) * (y * y))
-    return A - B, A + B, (ps * hs) * inv
-
-
-scale = time_step * 2.0 ** (-2.0 / 3.0)
+    B = t * (0.3 + (0.3 * slope_floor) * (y * y))
+    return ps - B, ps + B, (t * s) * inv
+
+
+scale = (5.0 / 3.0) * time_step * 2.0 ** (-2.0 / 3.0)
 
 
 def inner_kernel(
@@ -320,8 +319,8 @@
         put([y - x for x, y in zip(b, get(prim, 0, i + 1))], sb_y, i)
         ix = [1.0 / (x + y) for x, y in zip(m, right(m))]
         iy = [1.0 / (x + y) for x, y in zip(m, get(prim, 1, i + 1))]
-        put([-x for x in ix], inv_x, i)
-        put([-x for x in iy], inv_y, i)
+        put([-0.6 * x for x in ix], inv_x, i)
+        put([-0.6 * x for x in iy], inv_y, i)
         put([x + y for x, y in zip(q, right(q))], q_x, i)
         put([x + y for x, y in zip(q, get(prim, 2, i + 1))], q_y, i)
         for e in range(events):
@@ -446,7 +445,7 @@
         sb[i, :, J[j]] = y - x
         x, y = k_of(1)
         z = 1.0 / (x + y)
-        inv[i, :, J[j]] = -z
+        inv[i, :, J[j]] = -0.6 * z
         x, y = k_of(2)
         q[i, :, J[j]] = x + y
         for e in range(events):

time: 42.5 us -> 42.5 us (level)
  transfers between devices with their start and end apart: 12 -> 12, of which waited for: 4 -> 4; matrix products, arithmetic and copies ran while one was open for 0% -> 0% of each run, Pallas kernels for 16% -> 15%
where the time goes in v7:
time: 42.5 us; the launch traced here: 42.3 us
  starting transfers between devices  19.9 us (47%)
  Pallas kernels  15.3 us (36%)
  waiting for transfers between devices  6.19 us (15%)
  between operations  0.85 us (2%)
    ppermute x7, starting transfers between devices, from_hop(): lax.ppermute(x, axis, [(i, i ^ hop) for i in range(lax.axis_size(axis))])  9.47 us
    ppermute x7, waiting for transfers between devices, from_hop(): lax.ppermute(x, axis, [(i, i ^ hop) for i in range(lax.axis_size(axis))])  6.17 us
    pallas_call x1, Pallas kernels, tangents(): pl.pallas_call(tangent_kernel, in_specs=[vmem] * (2 + len(more_inputs)),...  5.35 us
    ppermute x3, starting transfers between devices, exchange(): return lax.ppermute(x, axis, perm) if perm else None  5.26 us
    ppermute x2, starting transfers between devices, diagonal(): return lax.ppermute(x, ('row', 'col'), perm)  5.19 us
    pallas_call x1, Pallas kernels, inner(): pl.pallas_call(inner_kernel, in_specs=[vmem] * 5, out_specs=[vmem] * 9, o...  3.78 us
    pallas_call x2, Pallas kernels, gradient(): pl.pallas_call(functools.partial(adjoint_kernel, first, last), grid=(1,),...  2.75 us
    pallas_call x1, Pallas kernels, edges_and_gauges(): pl.pallas_call(functools.partial(edge_kernel, sides), in_specs=[anywhere]...  2.59 us
  transfers between devices with their start and end apart: 12, of which 4 were waited for; matrix products, arithmetic and copies ran while one was open for 0% of the time, Pallas kernels for 15%

profile of v7, /device:TPU:0, one launch (start us, length us, event | category | flops | bytes accessed | tf_op | source)
XLA Modules:
  0.0 42.3 jit_solution(7437350299596532564)
XLA Ops:
  0.6 0.0 copy-start.4
  0.6 0.0 copy-start.3
  0.7 0.0 copy-start.2
  0.7 0.0 copy-start.1
  0.7 0.0 copy-start
  0.7 2.6 %edges.1 = (f32[2,8,64,128]{3,2,1,0:T(8,128)}, f32[64,128]{1,0:T(8,128)}, f32[64,128]{1,0:T(8,128)}, f32[72,1024]{1,0:T(8,128)}, f32[8,128]{1,0:T(8,128)}, /*index=5*/f32[8,128]{1,0:T(8,128)}) custom-call(s32[2,1,1024]{2,1,0:T(1,128)} %bitcast.2, f32[2,3,64,1024]{3,2,1,0:T(8,128)} %depth.1, s32[2,64,1024]{2,1,0:T(8,128)} %wet.1, f32[64,1024]{1,0:T(8,128)} %bed.1, ...), custom_call_target="tpu_custom_call" | custom-call | tf_op jit(solution)/shard_map/edges/pallas_call | solution.py:148
  3.3 3.0 %collective-permute-start = (f32[72,1024]{1,0:T(8,128)}, f32[72,1024]{1,0:T(8,128)S(1)}, u32[]{:S(2)}, u32[]{:S(2)}) collective-permute-start(f32[72,1024]{1,0:T(8,128)} %get-tuple-element.52), channel_id=1, source_target_pairs={{0,4},{4,0},{1,5},{5,1},{2,6},{6,2},{3,7},{7,3},{8,12},{12,8},{9,1... | collective-permute-start | bytes 884744 | tf_op jit(solution)/shard_map/ppermute | solution.py:28
  6.3 1.6 %collective-permute-start.1 = (f32[64,128]{1,0:T(8,128)}, f32[64,128]{1,0:T(8,128)S(1)}, u32[]{:S(2)}, u32[]{:S(2)}) collective-permute-start(f32[64,128]{1,0:T(8,128)} %get-tuple-element.53), channel_id=1, source_target_pairs={{0,1},{1,0},{2,3},{3,2},{4,5},{5,4},{6,7},{7,6},{8,9},{9,8},{10,11... | collective-permute-start | bytes 98312 | tf_op jit(solution)/shard_map/ppermute | solution.py:28
  7.9 0.7 %collective-permute-start.2 = (f32[64,128]{1,0:T(8,128)}, f32[64,128]{1,0:T(8,128)S(1)}, u32[]{:S(2)}, u32[]{:S(2)}) collective-permute-start(f32[64,128]{1,0:T(8,128)} %get-tuple-element.54), channel_id=1, source_target_pairs={{1,2},{2,1},{5,6},{6,5},{9,10},{10,9},{13,14},{14,13},{17,18},{18,... | collective-permute-start | bytes 98312 | tf_op jit(solution)/shard_map/ppermute | solution.py:28
  8.6 4.4 %collective-permute-start.3 = (f32[8,128]{1,0:T(8,128)}, f32[8,128]{1,0:T(8,128)S(1)}, u32[]{:S(2)}, u32[]{:S(2)}) collective-permute-start(f32[8,128]{1,0:T(8,128)} %get-tuple-element.55), channel_id=1, source_target_pairs={{0,5},{1,4},{2,7},{3,6},{4,1},{5,0},{6,3},{7,2},{8,13},{9,12},{10,... | collective-permute-start | bytes 12296 | tf_op jit(solution)/shard_map/ppermute | solution.py:168
  13.0 0.0 copy-start.5
  13.0 0.8 %collective-permute-start.4 = (f32[8,128]{1,0:T(8,128)}, f32[8,128]{1,0:T(8,128)S(1)}, u32[]{:S(2)}, u32[]{:S(2)}) collective-permute-start(f32[8,128]{1,0:T(8,128)} %get-tuple-element.56), channel_id=1, source_target_pairs={{1,6},{2,5},{5,2},{6,1},{9,14},{10,13},{13,10},{14,9},{17,22},{18,... | collective-permute-start | bytes 12296 | tf_op jit(solution)/shard_map/ppermute | solution.py:168
  13.7 0.0 copy-done.4
  13.8 0.0 copy-done.3
  13.8 0.0 copy-done.2
  13.8 0.0 copy-done.1
  13.8 0.0 copy-done
  13.8 3.8 %inner.1 = (f32[11,9,8,1024]{3,2,1,0:T(8,128)S(1)}, f32[2,2,8,8,1024]{4,3,2,1,0:T(8,128)S(1)}, f32[2,2,8,8,1024]{4,3,2,1,0:T(8,128)S(1)}, f32[2,3,8,8,1024]{4,3,...) custom-call(f32[2,3,64,1024]{3,2,1,0:T(8,128)S(1)} %copy-done, ...), custom_call_target="tpu_custom_call" | custom-call | flops 100000000 | bytes 16000000 | tf_op jit(solution)/shard_map/inner/pallas_call | solution.py:361
  17.6 0.0 collective-permute-done.3.corner_aa
  17.6 0.0 collective-permute-done.4.corner_ab
  17.6 0.0 collective-permute-done.1.side_a
  17.6 0.0 collective-permute-done.2.side_b
  17.6 0.0 collective-permute-done.refs_0_
  17.6 0.1 row_rims.1
  17.7 0.0 copy-done.5
  17.8 5.3 %tangents.1 = (f32[8,128]{1,0:T(8,128)S(1)}, f32[2,13,8,1152]{3,2,1,0:T(8,128)S(1)}, f32[2,2,10,8,1152]{4,3,2,1,0:T(8,128)S(1)}, f32[2,2,10,8,1152]{4,3,2,1,0:T(...) custom-call(f32[11,9,8,1024]{3,2,1,0:T(8,128)S(1)} %get-tuple-elemen, ...), custom_call_target="tpu_custom_call" | custom-call | tf_op jit(solution)/shard_map/tangents/pallas_call | solution.py:569
  23.1 0.1 collective-permute-start.5
  23.2 1.2 %gradient.2 = (f32[10,8,1152]{2,1,0:T(8,128)S(1)}, f32[10,8,1152]{2,1,0:T(8,128)S(1)}) custom-call(f32[11,9,8,1024]{3,2,1,0:T(8,128)S(1)} %get-tuple-element.66.prim.m_c, f32[2,13,8,1152]{3,2,1,0:T(8,128)S(1)} %get-tuple-element.83.source, f32[2,2,10,8,1152]{4,3,2,1,0:T(8,128)S(1)} %get-tuple-element.84.a_x, ...), custom_call_target="tpu_custom_call" | custom-call | flops 40000000 | bytes 12000000 | tf_op jit(solution)/shard_map/gradient/pallas_call | solution.py:673
  24.4 0.0 collective-permute-done.5
  24.4 1.6 %collective-permute-start.6 = (f32[8,128]{1,0:T(8,128)S(1)}, f32[8,128]{1,0:T(8,128)S(1)}, u32[]{:S(2)}, u32[]{:S(2)}) collective-permute-start(f32[8,128]{1,0:T(8,128)S(1)} %add.15), channel_id=1, source_target_pairs={{0,16},{8,24},{16,0},{24,8},{1,17},{9,25},{17,1},{25,9},{2,18},{10... | collective-permute-start | bytes 12296 | tf_op jit(solution)/shard_map/ppermute | solution.py:700
  26.0 1.5 %gradient.3 = f32[64,1024]{1,0:T(8,128)S(1)} custom-call(f32[11,9,8,1024]{3,2,1,0:T(8,128)S(1)} %get-tuple-element.66.prim.m_c, f32[2,13,8,1152]{3,2,1,0:T(8,128)S(1)} %get-tuple-element.83.source, f32[2,2,10,8,1152]{4,3,2,1,0:T(8,128)S(1)} %get-tuple-element.84.a_x, f32[2,2,10,8,1152]{4,3,2,1,0:T(8,128)S(1)} %get-tuple-element.85.b_x, ...), custom_call_target="tpu_custom_call" | custom-call | flops 40000000 | bytes 12000000 | tf_op jit(solution)/shard_map/gradient/pallas_call | solution.py:673
  27.5 0.6 %collective-permute-done.6 = f32[8,128]{1,0:T(8,128)S(1)} collective-permute-done((f32[8,128]{1,0:T(8,128)S(1)}, f32[8,128]{1,0:T(8,128)S(1)}, u32[]{:S(2)}, u32[]{:S(2)}) %collective-permute-start.6) | collective-permute-done | bytes 4128 | tf_op jit(solution)/shard_map/ppermute | solution.py:700
  28.1 0.0 collective-permute-start.7
  28.1 1.5 %collective-permute-start.8 = (f32[8,128]{1,0:T(8,128)S(1)}, f32[8,128]{1,0:T(8,128)S(1)}, u32[]{:S(2)}, u32[]{:S(2)}) collective-permute-start(f32[8,128]{1,0:T(8,128)S(1)} %add.16), channel_id=1, source_target_pairs={{0,4},{4,0},{1,5},{5,1},{2,6},{6,2},{3,7},{7,3},{8,12},{12,8},{9,1... | collective-permute-start | bytes 12296 | tf_op jit(solution)/shard_map/ppermute | solution.py:700
  29.6 2.1 %collective-permute-done.8 = f32[8,128]{1,0:T(8,128)S(1)} collective-permute-done((f32[8,128]{1,0:T(8,128)S(1)}, f32[8,128]{1,0:T(8,128)S(1)}, u32[]{:S(2)}, u32[]{:S(2)}) %collective-permute-start.8) | collective-permute-done | bytes 4128 | tf_op jit(solution)/shard_map/ppermute | solution.py:700
  31.7 0.0 collective-permute-done.7
  31.8 1.6 %collective-permute-start.9 = (f32[64,1024]{1,0:T(8,128)S(1)}, f32[64,1024]{1,0:T(8,128)S(1)}, u32[]{:S(2)}, u32[]{:S(2)}) collective-permute-start(f32[64,1024]{1,0:T(8,128)S(1)} %add.17.grad), channel_id=1, source_target_pairs={{0,16},{8,24},{16,0},{24,8},{1,17},{9,25},{17,1},{25,9},{2,18},{10... | collective-permute-start | bytes 786440 | tf_op jit(solution)/shard_map/ppermute | solution.py:700
  33.3 2.2 %collective-permute-start.10 = (f32[8,128]{1,0:T(8,128)S(1)}, f32[8,128]{1,0:T(8,128)S(1)}, u32[]{:S(2)}, u32[]{:S(2)}) collective-permute-start(f32[8,128]{1,0:T(8,128)S(1)} %add.18), channel_id=1, source_target_pairs={{0,1},{1,0},{2,3},{3,2},{4,5},{5,4},{6,7},{7,6},{8,9},{9,8},{10,11... | collective-permute-start | bytes 12296 | tf_op jit(solution)/shard_map/ppermute | solution.py:700
  35.5 1.6 %collective-permute-done.10 = f32[8,128]{1,0:T(8,128)S(1)} collective-permute-done((f32[8,128]{1,0:T(8,128)S(1)}, f32[8,128]{1,0:T(8,128)S(1)}, u32[]{:S(2)}, u32[]{:S(2)}) %collective-permute-start.10) | collective-permute-done | bytes 4128 | tf_op jit(solution)/shard_map/ppermute | solution.py:700
  37.1 2.6 %collective-permute-start.11 = (f32[8,128]{1,0:T(8,128)S(1)}, f32[8,128]{1,0:T(8,128)S(1)}, u32[]{:S(2)}, u32[]{:S(2)}) collective-permute-start(f32[8,128]{1,0:T(8,128)S(1)} %add.19.curve), channel_id=1, source_target_pairs={{0,2},{1,3},{2,0},{3,1},{4,6},{5,7},{6,4},{7,5},{8,10},{9,11},{10,... | collective-permute-start | bytes 12296 | tf_op jit(solution)/shard_map/ppermute | solution.py:700
  39.7 1.9 %collective-permute-done.11.curve_arrived = f32[8,128]{1,0:T(8,128)S(1)} collective-permute-done((f32[8,128]{1,0:T(8,128)S(1)}, f32[8,128]{1,0:T(8,128)S(1)}, u32[]{:S(2)}, u32[]{:S(2)}) %collective-permute-start.11) | collective-permute-done | bytes 4128 | tf_op jit(solution)/shard_map/ppermute | solution.py:700
  41.6 0.0 collective-permute-done.9.arrived
  41.6 0.7 %finish.1 = (f32[64,1024]{1,0:T(8,128)}, f32[1,1]{1,0:T(1,128)}) custom-call(f32[64,1024]{1,0:T(8,128)S(1)} %add.17.grad, f32[64,1024]{1,0:T(8,128)S(1)} %collective-permute-done.9.arrived, f32[8,128]{1,0:T(8,128)S(1)} %add.19.curve, f32[8,128]{1,0:T(8,128)S(1)} %collective-permute-done.11.curve_arrived), custom_call_target="tpu_custom_call" | custom-call | tf_op jit(solution)/shard_map/finish/pallas_call | solution.py:714
  (6 shorter events, 0.1 us)
Async XLA Ops:
  0.6 13.1 %copy-start.4 = (f32[64,1024]{1,0:T(8,128)S(1)}, f32[64,1024]{1,0:T(8,128)}, u32[]{:S(2)}) copy-start(f32[64,1024]{1,0:T(8,128)} %direction.1) | copy-start | bytes 786436
  0.6 13.1 %copy-start.3 = (f32[64,1024]{1,0:T(8,128)S(1)}, f32[64,1024]{1,0:T(8,128)}, u32[]{:S(2)}) copy-start(f32[64,1024]{1,0:T(8,128)} %rough.1) | copy-start | bytes 786436
  0.7 13.1 %copy-start.2 = (f32[64,1024]{1,0:T(8,128)S(1)}, f32[64,1024]{1,0:T(8,128)}, u32[]{:S(2)}) copy-start(f32[64,1024]{1,0:T(8,128)} %bed.1) | copy-start | bytes 786436
  0.7 13.1 %copy-start.1 = (s32[2,64,1024]{2,1,0:T(8,128)S(1)}, s32[2,64,1024]{2,1,0:T(8,128)}, u32[]{:S(2)}) copy-start(s32[2,64,1024]{2,1,0:T(8,128)} %wet.1) | copy-start | bytes 1572868
  0.7 13.1 %copy-start = (f32[2,3,64,1024]{3,2,1,0:T(8,128)S(1)}, f32[2,3,64,1024]{3,2,1,0:T(8,128)}, u32[]{:S(2)}) copy-start(f32[2,3,64,1024]{3,2,1,0:T(8,128)} %depth.1) | copy-start | bytes 4718596
  3.3 14.3 %collective-permute-start = (f32[72,1024]{1,0:T(8,128)}, f32[72,1024]{1,0:T(8,128)S(1)}, u32[]{:S(2)}, u32[]{:S(2)}) collective-permute-start(f32[72,1024]{1,0:T(8,128)} %get-tuple-element.52), channel_id=1, source_target_pairs={{0,4},{4,0},{1,5},{5,1},{2,6},{6,2},{3,7},{7,3},{8,12},{12,8},{9,1... | collective-permute-start | bytes 884744 | tf_op jit(solution)/shard_map/ppermute | solution.py:28
  6.3 11.3 %collective-permute-start.1 = (f32[64,128]{1,0:T(8,128)}, f32[64,128]{1,0:T(8,128)S(1)}, u32[]{:S(2)}, u32[]{:S(2)}) collective-permute-start(f32[64,128]{1,0:T(8,128)} %get-tuple-element.53), channel_id=1, source_target_pairs={{0,1},{1,0},{2,3},{3,2},{4,5},{5,4},{6,7},{7,6},{8,9},{9,8},{10,11... | collective-permute-start | bytes 98312 | tf_op jit(solution)/shard_map/ppermute | solution.py:28
  7.9 9.7 %collective-permute-start.2 = (f32[64,128]{1,0:T(8,128)}, f32[64,128]{1,0:T(8,128)S(1)}, u32[]{:S(2)}, u32[]{:S(2)}) collective-permute-start(f32[64,128]{1,0:T(8,128)} %get-tuple-element.54), channel_id=1, source_target_pairs={{1,2},{2,1},{5,6},{6,5},{9,10},{10,9},{13,14},{14,13},{17,18},{18,... | collective-permute-start | bytes 98312 | tf_op jit(solution)/shard_map/ppermute | solution.py:28
  8.6 9.0 %collective-permute-start.3 = (f32[8,128]{1,0:T(8,128)}, f32[8,128]{1,0:T(8,128)S(1)}, u32[]{:S(2)}, u32[]{:S(2)}) collective-permute-start(f32[8,128]{1,0:T(8,128)} %get-tuple-element.55), channel_id=1, source_target_pairs={{0,5},{1,4},{2,7},{3,6},{4,1},{5,0},{6,3},{7,2},{8,13},{9,12},{10,... | collective-permute-start | bytes 12296 | tf_op jit(solution)/shard_map/ppermute | solution.py:168
  13.0 4.8 %copy-start.5 = (f32[2,8,64,128]{3,2,1,0:T(8,128)S(1)}, f32[2,8,64,128]{3,2,1,0:T(8,128)}, u32[]{:S(2)}) copy-start(f32[2,8,64,128]{3,2,1,0:T(8,128)} %get-tuple-element.67.cnt) | copy-start | bytes 1572868
  13.0 4.6 %collective-permute-start.4 = (f32[8,128]{1,0:T(8,128)}, f32[8,128]{1,0:T(8,128)S(1)}, u32[]{:S(2)}, u32[]{:S(2)}) collective-permute-start(f32[8,128]{1,0:T(8,128)} %get-tuple-element.56), channel_id=1, source_target_pairs={{1,6},{2,5},{5,2},{6,1},{9,14},{10,13},{13,10},{14,9},{17,22},{18,... | collective-permute-start | bytes 12296 | tf_op jit(solution)/shard_map/ppermute | solution.py:168
  23.1 1.3 %collective-permute-start.5 = (f32[8,128]{1,0:T(8,128)S(1)}, f32[8,128]{1,0:T(8,128)S(1)}, u32[]{:S(2)}, u32[]{:S(2)}) collective-permute-start(f32[8,128]{1,0:T(8,128)S(1)} %get-tuple-element.92), channel_id=1, source_target_pairs={{0,8},{8,0},{16,24},{24,16},{1,9},{9,1},{17,25},{25,17},{2,10},{10... | collective-permute-start | bytes 12296 | tf_op jit(solution)/shard_map/ppermute | solution.py:700
  24.4 3.7 %collective-permute-start.6 = (f32[8,128]{1,0:T(8,128)S(1)}, f32[8,128]{1,0:T(8,128)S(1)}, u32[]{:S(2)}, u32[]{:S(2)}) collective-permute-start(f32[8,128]{1,0:T(8,128)S(1)} %add.15), channel_id=1, source_target_pairs={{0,16},{8,24},{16,0},{24,8},{1,17},{9,25},{17,1},{25,9},{2,18},{10... | collective-permute-start | bytes 12296 | tf_op jit(solution)/shard_map/ppermute | solution.py:700
  28.1 3.6 %collective-permute-start.7 = (f32[64,1024]{1,0:T(8,128)S(1)}, f32[64,1024]{1,0:T(8,128)S(1)}, u32[]{:S(2)}, u32[]{:S(2)}) collective-permute-start(f32[64,1024]{1,0:T(8,128)S(1)} %gradient.3), channel_id=1, source_target_pairs={{0,8},{8,0},{16,24},{24,16},{1,9},{9,1},{17,25},{25,17},{2,10},{10... | collective-permute-start | bytes 786440 | tf_op jit(solution)/shard_map/ppermute | solution.py:700
  28.1 3.6 %collective-permute-start.8 = (f32[8,128]{1,0:T(8,128)S(1)}, f32[8,128]{1,0:T(8,128)S(1)}, u32[]{:S(2)}, u32[]{:S(2)}) collective-permute-start(f32[8,128]{1,0:T(8,128)S(1)} %add.16), channel_id=1, source_target_pairs={{0,4},{4,0},{1,5},{5,1},{2,6},{6,2},{3,7},{7,3},{8,12},{12,8},{9,1... | collective-permute-start | bytes 12296 | tf_op jit(solution)/shard_map/ppermute | solution.py:700
  31.8 9.8 %collective-permute-start.9 = (f32[64,1024]{1,0:T(8,128)S(1)}, f32[64,1024]{1,0:T(8,128)S(1)}, u32[]{:S(2)}, u32[]{:S(2)}) collective-permute-start(f32[64,1024]{1,0:T(8,128)S(1)} %add.17.grad), channel_id=1, source_target_pairs={{0,16},{8,24},{16,0},{24,8},{1,17},{9,25},{17,1},{25,9},{2,18},{10... | collective-permute-start | bytes 786440 | tf_op jit(solution)/shard_map/ppermute | solution.py:700
  33.3 3.7 %collective-permute-start.10 = (f32[8,128]{1,0:T(8,128)S(1)}, f32[8,128]{1,0:T(8,128)S(1)}, u32[]{:S(2)}, u32[]{:S(2)}) collective-permute-start(f32[8,128]{1,0:T(8,128)S(1)} %add.18), channel_id=1, source_target_pairs={{0,1},{1,0},{2,3},{3,2},{4,5},{5,4},{6,7},{7,6},{8,9},{9,8},{10,11... | collective-permute-start | bytes 12296 | tf_op jit(solution)/shard_map/ppermute | solution.py:700
  37.1 4.5 %collective-permute-start.11 = (f32[8,128]{1,0:T(8,128)S(1)}, f32[8,128]{1,0:T(8,128)S(1)}, u32[]{:S(2)}, u32[]{:S(2)}) collective-permute-start(f32[8,128]{1,0:T(8,128)S(1)} %add.19.curve), channel_id=1, source_target_pairs={{0,2},{1,3},{2,0},{3,1},{4,6},{5,7},{6,4},{7,5},{8,10},{9,11},{10,... | collective-permute-start | bytes 12296 | tf_op jit(solution)/shard_map/ppermute | solution.py:700

commit v8 on v7

--- a/solution.py
+++ b/solution.py
@@ -299,7 +299,7 @@
         for j in range(count):
             nat[k, j] = x[:, at_lanes(j)].astype(jnp.float32)
 
-    @pl.loop(0, deep, unroll=4)
+    @pl.loop(0, deep, unroll=deep)
     def _(i):
         spread = lambda k: [nat[k, j, pl.ds(i, SUB, stride=deep), :] for j in range(count)]
         m = [jnp.exp(x) for x in spread(1)]
@@ -312,7 +312,7 @@
     for k in range(3 + events * (steps + 1)):
         put([up(x) for x in get(prim, k, 0)], prim, k, deep)
 
-    @pl.loop(0, deep, unroll=4)
+    @pl.loop(0, deep, unroll=deep)
     def _(i):
         b, m, q = (get(prim, k, i) for k in range(3))
         put([y - x for x, y in zip(b, right(b))], sb_x, i)

time: 42.5 us -> 42.5 us (level)
  no operation moved by 1% of the time
where the time goes in v8:
time: 42.5 us; the launch traced here: 42.3 us
  starting transfers between devices  19.9 us (47%)
  Pallas kernels  15 us (35%)
  waiting for transfers between devices  6.52 us (15%)
  between operations  0.85 us (2%)
    ppermute x7, starting transfers between devices, from_hop(): lax.ppermute(x, axis, [(i, i ^ hop) for i in range(lax.axis_size(axis))])  9.47 us
    ppermute x7, waiting for transfers between devices, from_hop(): lax.ppermute(x, axis, [(i, i ^ hop) for i in range(lax.axis_size(axis))])  6.51 us
    pallas_call x1, Pallas kernels, tangents(): pl.pallas_call(tangent_kernel, in_specs=[vmem] * (2 + len(more_inputs)),...  5.35 us
    ppermute x3, starting transfers between devices, exchange(): return lax.ppermute(x, axis, perm) if perm else None  5.26 us
    ppermute x2, starting transfers between devices, diagonal(): return lax.ppermute(x, ('row', 'col'), perm)  5.19 us
    pallas_call x1, Pallas kernels, inner(): pl.pallas_call(inner_kernel, in_specs=[vmem] * 5, out_specs=[vmem] * 9, o...  3.44 us
    pallas_call x2, Pallas kernels, gradient(): pl.pallas_call(functools.partial(adjoint_kernel, first, last), grid=(1,),...  2.75 us
    pallas_call x1, Pallas kernels, edges_and_gauges(): pl.pallas_call(functools.partial(edge_kernel, sides), in_specs=[anywhere]...  2.59 us
  transfers between devices with their start and end apart: 12, of which 4 were waited for; matrix products, arithmetic and copies ran while one was open for 0% of the time, Pallas kernels for 15%

profile of v8, /device:TPU:0, one launch (start us, length us, event | category | flops | bytes accessed | tf_op | source)
XLA Modules:
  0.0 42.3 jit_solution(11997344711333161338)
XLA Ops:
  0.6 0.0 copy-start.4
  0.6 0.0 copy-start.3
  0.7 0.0 copy-start.2
  0.7 0.0 copy-start.1
  0.7 0.0 copy-start
  0.7 2.6 %edges.1 = (f32[2,8,64,128]{3,2,1,0:T(8,128)}, f32[64,128]{1,0:T(8,128)}, f32[64,128]{1,0:T(8,128)}, f32[72,1024]{1,0:T(8,128)}, f32[8,128]{1,0:T(8,128)}, /*index=5*/f32[8,128]{1,0:T(8,128)}) custom-call(s32[2,1,1024]{2,1,0:T(1,128)} %bitcast.2, f32[2,3,64,1024]{3,2,1,0:T(8,128)} %depth.1, s32[2,64,1024]{2,1,0:T(8,128)} %wet.1, f32[64,1024]{1,0:T(8,128)} %bed.1, ...), custom_call_target="tpu_custom_call" | custom-call | tf_op jit(solution)/shard_map/edges/pallas_call | solution.py:148
  3.3 3.0 %collective-permute-start = (f32[72,1024]{1,0:T(8,128)}, f32[72,1024]{1,0:T(8,128)S(1)}, u32[]{:S(2)}, u32[]{:S(2)}) collective-permute-start(f32[72,1024]{1,0:T(8,128)} %get-tuple-element.52), channel_id=1, source_target_pairs={{0,4},{4,0},{1,5},{5,1},{2,6},{6,2},{3,7},{7,3},{8,12},{12,8},{9,1... | collective-permute-start | bytes 884744 | tf_op jit(solution)/shard_map/ppermute | solution.py:28
  6.3 1.6 %collective-permute-start.1 = (f32[64,128]{1,0:T(8,128)}, f32[64,128]{1,0:T(8,128)S(1)}, u32[]{:S(2)}, u32[]{:S(2)}) collective-permute-start(f32[64,128]{1,0:T(8,128)} %get-tuple-element.53), channel_id=1, source_target_pairs={{0,1},{1,0},{2,3},{3,2},{4,5},{5,4},{6,7},{7,6},{8,9},{9,8},{10,11... | collective-permute-start | bytes 98312 | tf_op jit(solution)/shard_map/ppermute | solution.py:28
  7.9 0.7 %collective-permute-start.2 = (f32[64,128]{1,0:T(8,128)}, f32[64,128]{1,0:T(8,128)S(1)}, u32[]{:S(2)}, u32[]{:S(2)}) collective-permute-start(f32[64,128]{1,0:T(8,128)} %get-tuple-element.54), channel_id=1, source_target_pairs={{1,2},{2,1},{5,6},{6,5},{9,10},{10,9},{13,14},{14,13},{17,18},{18,... | collective-permute-start | bytes 98312 | tf_op jit(solution)/shard_map/ppermute | solution.py:28
  8.6 4.4 %collective-permute-start.3 = (f32[8,128]{1,0:T(8,128)}, f32[8,128]{1,0:T(8,128)S(1)}, u32[]{:S(2)}, u32[]{:S(2)}) collective-permute-start(f32[8,128]{1,0:T(8,128)} %get-tuple-element.55), channel_id=1, source_target_pairs={{0,5},{1,4},{2,7},{3,6},{4,1},{5,0},{6,3},{7,2},{8,13},{9,12},{10,... | collective-permute-start | bytes 12296 | tf_op jit(solution)/shard_map/ppermute | solution.py:168
  13.0 0.0 copy-start.5
  13.0 0.8 %collective-permute-start.4 = (f32[8,128]{1,0:T(8,128)}, f32[8,128]{1,0:T(8,128)S(1)}, u32[]{:S(2)}, u32[]{:S(2)}) collective-permute-start(f32[8,128]{1,0:T(8,128)} %get-tuple-element.56), channel_id=1, source_target_pairs={{1,6},{2,5},{5,2},{6,1},{9,14},{10,13},{13,10},{14,9},{17,22},{18,... | collective-permute-start | bytes 12296 | tf_op jit(solution)/shard_map/ppermute | solution.py:168
  13.7 0.0 copy-done.4
  13.8 0.0 copy-done.3
  13.8 0.0 copy-done.2
  13.8 0.0 copy-done.1
  13.8 0.0 copy-done
  13.8 3.4 %inner.1 = (f32[11,9,8,1024]{3,2,1,0:T(8,128)S(1)}, f32[2,2,8,8,1024]{4,3,2,1,0:T(8,128)S(1)}, f32[2,2,8,8,1024]{4,3,2,1,0:T(8,128)S(1)}, f32[2,3,8,8,1024]{4,3,...) custom-call(f32[2,3,64,1024]{3,2,1,0:T(8,128)S(1)} %copy-done, ...), custom_call_target="tpu_custom_call" | custom-call | flops 100000000 | bytes 16000000 | tf_op jit(solution)/shard_map/inner/pallas_call | solution.py:361
  17.2 0.0 collective-permute-done.3.corner_aa
  17.3 0.0 collective-permute-done.4.corner_ab
  17.3 0.0 collective-permute-done.1.side_a
  17.3 0.0 collective-permute-done.2.side_b
  17.3 0.0 collective-permute-done.refs_0_
  17.3 0.1 row_rims.1
  17.4 0.0 copy-done.5
  17.4 5.3 %tangents.1 = (f32[8,128]{1,0:T(8,128)S(1)}, f32[2,13,8,1152]{3,2,1,0:T(8,128)S(1)}, f32[2,2,10,8,1152]{4,3,2,1,0:T(8,128)S(1)}, f32[2,2,10,8,1152]{4,3,2,1,0:T(...) custom-call(f32[11,9,8,1024]{3,2,1,0:T(8,128)S(1)} %get-tuple-elemen, ...), custom_call_target="tpu_custom_call" | custom-call | tf_op jit(solution)/shard_map/tangents/pallas_call | solution.py:569
  22.8 0.1 collective-permute-start.5
  22.8 1.2 %gradient.2 = (f32[10,8,1152]{2,1,0:T(8,128)S(1)}, f32[10,8,1152]{2,1,0:T(8,128)S(1)}) custom-call(f32[11,9,8,1024]{3,2,1,0:T(8,128)S(1)} %get-tuple-element.66.prim.m_c, f32[2,13,8,1152]{3,2,1,0:T(8,128)S(1)} %get-tuple-element.83.source, f32[2,2,10,8,1152]{4,3,2,1,0:T(8,128)S(1)} %get-tuple-element.84.a_x, ...), custom_call_target="tpu_custom_call" | custom-call | flops 40000000 | bytes 12000000 | tf_op jit(solution)/shard_map/gradient/pallas_call | solution.py:673
  24.1 0.0 collective-permute-done.5
  24.1 1.6 %collective-permute-start.6 = (f32[8,128]{1,0:T(8,128)S(1)}, f32[8,128]{1,0:T(8,128)S(1)}, u32[]{:S(2)}, u32[]{:S(2)}) collective-permute-start(f32[8,128]{1,0:T(8,128)S(1)} %add.15), channel_id=1, source_target_pairs={{0,16},{8,24},{16,0},{24,8},{1,17},{9,25},{17,1},{25,9},{2,18},{10... | collective-permute-start | bytes 12296 | tf_op jit(solution)/shard_map/ppermute | solution.py:700
  25.7 1.5 %gradient.3 = f32[64,1024]{1,0:T(8,128)S(1)} custom-call(f32[11,9,8,1024]{3,2,1,0:T(8,128)S(1)} %get-tuple-element.66.prim.m_c, f32[2,13,8,1152]{3,2,1,0:T(8,128)S(1)} %get-tuple-element.83.source, f32[2,2,10,8,1152]{4,3,2,1,0:T(8,128)S(1)} %get-tuple-element.84.a_x, f32[2,2,10,8,1152]{4,3,2,1,0:T(8,128)S(1)} %get-tuple-element.85.b_x, ...), custom_call_target="tpu_custom_call" | custom-call | flops 40000000 | bytes 12000000 | tf_op jit(solution)/shard_map/gradient/pallas_call | solution.py:673
  27.2 0.6 %collective-permute-done.6 = f32[8,128]{1,0:T(8,128)S(1)} collective-permute-done((f32[8,128]{1,0:T(8,128)S(1)}, f32[8,128]{1,0:T(8,128)S(1)}, u32[]{:S(2)}, u32[]{:S(2)}) %collective-permute-start.6) | collective-permute-done | bytes 4128 | tf_op jit(solution)/shard_map/ppermute | solution.py:700
  27.8 0.0 collective-permute-start.7
  27.8 1.5 %collective-permute-start.8 = (f32[8,128]{1,0:T(8,128)S(1)}, f32[8,128]{1,0:T(8,128)S(1)}, u32[]{:S(2)}, u32[]{:S(2)}) collective-permute-start(f32[8,128]{1,0:T(8,128)S(1)} %add.16), channel_id=1, source_target_pairs={{0,4},{4,0},{1,5},{5,1},{2,6},{6,2},{3,7},{7,3},{8,12},{12,8},{9,1... | collective-permute-start | bytes 12296 | tf_op jit(solution)/shard_map/ppermute | solution.py:700
  29.3 2.1 %collective-permute-done.8 = f32[8,128]{1,0:T(8,128)S(1)} collective-permute-done((f32[8,128]{1,0:T(8,128)S(1)}, f32[8,128]{1,0:T(8,128)S(1)}, u32[]{:S(2)}, u32[]{:S(2)}) %collective-permute-start.8) | collective-permute-done | bytes 4128 | tf_op jit(solution)/shard_map/ppermute | solution.py:700
  31.4 0.0 collective-permute-done.7
  31.4 1.6 %collective-permute-start.9 = (f32[64,1024]{1,0:T(8,128)S(1)}, f32[64,1024]{1,0:T(8,128)S(1)}, u32[]{:S(2)}, u32[]{:S(2)}) collective-permute-start(f32[64,1024]{1,0:T(8,128)S(1)} %add.17.grad), channel_id=1, source_target_pairs={{0,16},{8,24},{16,0},{24,8},{1,17},{9,25},{17,1},{25,9},{2,18},{10... | collective-permute-start | bytes 786440 | tf_op jit(solution)/shard_map/ppermute | solution.py:700
  33.0 2.5 %collective-permute-start.10 = (f32[8,128]{1,0:T(8,128)S(1)}, f32[8,128]{1,0:T(8,128)S(1)}, u32[]{:S(2)}, u32[]{:S(2)}) collective-permute-start(f32[8,128]{1,0:T(8,128)S(1)} %add.18), channel_id=1, source_target_pairs={{0,1},{1,0},{2,3},{3,2},{4,5},{5,4},{6,7},{7,6},{8,9},{9,8},{10,11... | collective-permute-start | bytes 12296 | tf_op jit(solution)/shard_map/ppermute | solution.py:700
  35.5 1.6 %collective-permute-done.10 = f32[8,128]{1,0:T(8,128)S(1)} collective-permute-done((f32[8,128]{1,0:T(8,128)S(1)}, f32[8,128]{1,0:T(8,128)S(1)}, u32[]{:S(2)}, u32[]{:S(2)}) %collective-permute-start.10) | collective-permute-done | bytes 4128 | tf_op jit(solution)/shard_map/ppermute | solution.py:700
  37.1 2.3 %collective-permute-start.11 = (f32[8,128]{1,0:T(8,128)S(1)}, f32[8,128]{1,0:T(8,128)S(1)}, u32[]{:S(2)}, u32[]{:S(2)}) collective-permute-start(f32[8,128]{1,0:T(8,128)S(1)} %add.19.curve), channel_id=1, source_target_pairs={{0,2},{1,3},{2,0},{3,1},{4,6},{5,7},{6,4},{7,5},{8,10},{9,11},{10,... | collective-permute-start | bytes 12296 | tf_op jit(solution)/shard_map/ppermute | solution.py:700
  39.4 2.2 %collective-permute-done.11.curve_arrived = f32[8,128]{1,0:T(8,128)S(1)} collective-permute-done((f32[8,128]{1,0:T(8,128)S(1)}, f32[8,128]{1,0:T(8,128)S(1)}, u32[]{:S(2)}, u32[]{:S(2)}) %collective-permute-start.11) | collective-permute-done | bytes 4128 | tf_op jit(solution)/shard_map/ppermute | solution.py:700
  41.6 0.0 collective-permute-done.9.arrived
  41.6 0.7 %finish.1 = (f32[64,1024]{1,0:T(8,128)}, f32[1,1]{1,0:T(1,128)}) custom-call(f32[64,1024]{1,0:T(8,128)S(1)} %add.17.grad, f32[64,1024]{1,0:T(8,128)S(1)} %collective-permute-done.9.arrived, f32[8,128]{1,0:T(8,128)S(1)} %add.19.curve, f32[8,128]{1,0:T(8,128)S(1)} %collective-permute-done.11.curve_arrived), custom_call_target="tpu_custom_call" | custom-call | tf_op jit(solution)/shard_map/finish/pallas_call | solution.py:714
  (6 shorter events, 0.1 us)
Async XLA Ops:
  0.6 13.1 %copy-start.4 = (f32[64,1024]{1,0:T(8,128)S(1)}, f32[64,1024]{1,0:T(8,128)}, u32[]{:S(2)}) copy-start(f32[64,1024]{1,0:T(8,128)} %direction.1) | copy-start | bytes 786436
  0.6 13.1 %copy-start.3 = (f32[64,1024]{1,0:T(8,128)S(1)}, f32[64,1024]{1,0:T(8,128)}, u32[]{:S(2)}) copy-start(f32[64,1024]{1,0:T(8,128)} %rough.1) | copy-start | bytes 786436
  0.7 13.1 %copy-start.2 = (f32[64,1024]{1,0:T(8,128)S(1)}, f32[64,1024]{1,0:T(8,128)}, u32[]{:S(2)}) copy-start(f32[64,1024]{1,0:T(8,128)} %bed.1) | copy-start | bytes 786436
  0.7 13.1 %copy-start.1 = (s32[2,64,1024]{2,1,0:T(8,128)S(1)}, s32[2,64,1024]{2,1,0:T(8,128)}, u32[]{:S(2)}) copy-start(s32[2,64,1024]{2,1,0:T(8,128)} %wet.1) | copy-start | bytes 1572868
  0.7 13.1 %copy-start = (f32[2,3,64,1024]{3,2,1,0:T(8,128)S(1)}, f32[2,3,64,1024]{3,2,1,0:T(8,128)}, u32[]{:S(2)}) copy-start(f32[2,3,64,1024]{3,2,1,0:T(8,128)} %depth.1) | copy-start | bytes 4718596
  3.3 14.0 %collective-permute-start = (f32[72,1024]{1,0:T(8,128)}, f32[72,1024]{1,0:T(8,128)S(1)}, u32[]{:S(2)}, u32[]{:S(2)}) collective-permute-start(f32[72,1024]{1,0:T(8,128)} %get-tuple-element.52), channel_id=1, source_target_pairs={{0,4},{4,0},{1,5},{5,1},{2,6},{6,2},{3,7},{7,3},{8,12},{12,8},{9,1... | collective-permute-start | bytes 884744 | tf_op jit(solution)/shard_map/ppermute | solution.py:28
  6.3 11.0 %collective-permute-start.1 = (f32[64,128]{1,0:T(8,128)}, f32[64,128]{1,0:T(8,128)S(1)}, u32[]{:S(2)}, u32[]{:S(2)}) collective-permute-start(f32[64,128]{1,0:T(8,128)} %get-tuple-element.53), channel_id=1, source_target_pairs={{0,1},{1,0},{2,3},{3,2},{4,5},{5,4},{6,7},{7,6},{8,9},{9,8},{10,11... | collective-permute-start | bytes 98312 | tf_op jit(solution)/shard_map/ppermute | solution.py:28
  7.9 9.4 %collective-permute-start.2 = (f32[64,128]{1,0:T(8,128)}, f32[64,128]{1,0:T(8,128)S(1)}, u32[]{:S(2)}, u32[]{:S(2)}) collective-permute-start(f32[64,128]{1,0:T(8,128)} %get-tuple-element.54), channel_id=1, source_target_pairs={{1,2},{2,1},{5,6},{6,5},{9,10},{10,9},{13,14},{14,13},{17,18},{18,... | collective-permute-start | bytes 98312 | tf_op jit(solution)/shard_map/ppermute | solution.py:28
  8.6 8.7 %collective-permute-start.3 = (f32[8,128]{1,0:T(8,128)}, f32[8,128]{1,0:T(8,128)S(1)}, u32[]{:S(2)}, u32[]{:S(2)}) collective-permute-start(f32[8,128]{1,0:T(8,128)} %get-tuple-element.55), channel_id=1, source_target_pairs={{0,5},{1,4},{2,7},{3,6},{4,1},{5,0},{6,3},{7,2},{8,13},{9,12},{10,... | collective-permute-start | bytes 12296 | tf_op jit(solution)/shard_map/ppermute | solution.py:168
  13.0 4.4 %copy-start.5 = (f32[2,8,64,128]{3,2,1,0:T(8,128)S(1)}, f32[2,8,64,128]{3,2,1,0:T(8,128)}, u32[]{:S(2)}) copy-start(f32[2,8,64,128]{3,2,1,0:T(8,128)} %get-tuple-element.67.cnt) | copy-start | bytes 1572868
  13.0 4.3 %collective-permute-start.4 = (f32[8,128]{1,0:T(8,128)}, f32[8,128]{1,0:T(8,128)S(1)}, u32[]{:S(2)}, u32[]{:S(2)}) collective-permute-start(f32[8,128]{1,0:T(8,128)} %get-tuple-element.56), channel_id=1, source_target_pairs={{1,6},{2,5},{5,2},{6,1},{9,14},{10,13},{13,10},{14,9},{17,22},{18,... | collective-permute-start | bytes 12296 | tf_op jit(solution)/shard_map/ppermute | solution.py:168
  22.8 1.3 %collective-permute-start.5 = (f32[8,128]{1,0:T(8,128)S(1)}, f32[8,128]{1,0:T(8,128)S(1)}, u32[]{:S(2)}, u32[]{:S(2)}) collective-permute-start(f32[8,128]{1,0:T(8,128)S(1)} %get-tuple-element.92), channel_id=1, source_target_pairs={{0,8},{8,0},{16,24},{24,16},{1,9},{9,1},{17,25},{25,17},{2,10},{10... | collective-permute-start | bytes 12296 | tf_op jit(solution)/shard_map/ppermute | solution.py:700
  24.1 3.7 %collective-permute-start.6 = (f32[8,128]{1,0:T(8,128)S(1)}, f32[8,128]{1,0:T(8,128)S(1)}, u32[]{:S(2)}, u32[]{:S(2)}) collective-permute-start(f32[8,128]{1,0:T(8,128)S(1)} %add.15), channel_id=1, source_target_pairs={{0,16},{8,24},{16,0},{24,8},{1,17},{9,25},{17,1},{25,9},{2,18},{10... | collective-permute-start | bytes 12296 | tf_op jit(solution)/shard_map/ppermute | solution.py:700
  27.8 3.6 %collective-permute-start.7 = (f32[64,1024]{1,0:T(8,128)S(1)}, f32[64,1024]{1,0:T(8,128)S(1)}, u32[]{:S(2)}, u32[]{:S(2)}) collective-permute-start(f32[64,1024]{1,0:T(8,128)S(1)} %gradient.3), channel_id=1, source_target_pairs={{0,8},{8,0},{16,24},{24,16},{1,9},{9,1},{17,25},{25,17},{2,10},{10... | collective-permute-start | bytes 786440 | tf_op jit(solution)/shard_map/ppermute | solution.py:700
  27.8 3.6 %collective-permute-start.8 = (f32[8,128]{1,0:T(8,128)S(1)}, f32[8,128]{1,0:T(8,128)S(1)}, u32[]{:S(2)}, u32[]{:S(2)}) collective-permute-start(f32[8,128]{1,0:T(8,128)S(1)} %add.16), channel_id=1, source_target_pairs={{0,4},{4,0},{1,5},{5,1},{2,6},{6,2},{3,7},{7,3},{8,12},{12,8},{9,1... | collective-permute-start | bytes 12296 | tf_op jit(solution)/shard_map/ppermute | solution.py:700
  31.4 10.2 %collective-permute-start.9 = (f32[64,1024]{1,0:T(8,128)S(1)}, f32[64,1024]{1,0:T(8,128)S(1)}, u32[]{:S(2)}, u32[]{:S(2)}) collective-permute-start(f32[64,1024]{1,0:T(8,128)S(1)} %add.17.grad), channel_id=1, source_target_pairs={{0,16},{8,24},{16,0},{24,8},{1,17},{9,25},{17,1},{25,9},{2,18},{10... | collective-permute-start | bytes 786440 | tf_op jit(solution)/shard_map/ppermute | solution.py:700
  33.0 4.1 %collective-permute-start.10 = (f32[8,128]{1,0:T(8,128)S(1)}, f32[8,128]{1,0:T(8,128)S(1)}, u32[]{:S(2)}, u32[]{:S(2)}) collective-permute-start(f32[8,128]{1,0:T(8,128)S(1)} %add.18), channel_id=1, source_target_pairs={{0,1},{1,0},{2,3},{3,2},{4,5},{5,4},{6,7},{7,6},{8,9},{9,8},{10,11... | collective-permute-start | bytes 12296 | tf_op jit(solution)/shard_map/ppermute | solution.py:700
  37.1 4.5 %collective-permute-start.11 = (f32[8,128]{1,0:T(8,128)S(1)}, f32[8,128]{1,0:T(8,128)S(1)}, u32[]{:S(2)}, u32[]{:S(2)}) collective-permute-start(f32[8,128]{1,0:T(8,128)S(1)} %add.19.curve), channel_id=1, source_target_pairs={{0,2},{1,3},{2,0},{3,1},{4,6},{5,7},{6,4},{7,5},{8,10},{9,11},{10,... | collective-permute-start | bytes 12296 | tf_op jit(solution)/shard_map/ppermute | solution.py:700
